TPU v7x, 128 devices: a whole 4x4x4 slice. The times are simulated.
128 devices in a mesh: row: 16 (over z_hi, x, core), col: 8 (over z_lo, y).
Axes of the slice: x: 4, y: 4, z: 4 (z_hi: 2, z_lo: 2; z = z_hi * 2 + z_lo), core: 2. Of those that a mesh axis runs over, the one named last changes fastest.
Arguments:
- chol: float32 [12288, 640], P(('row', 'col')), may hold values from -6 to 6
- eps_occ: float32 [48], replicated, may hold values from -2 to -0.5
- eps_vir: float32 [256], replicated, may hold values from 0.3 to 3
Outputs:
- work: float32 [12288, 640], P(('row', 'col'))
- energies: float32 [2], replicated
All inputs are finite; a program needn't handle non-finite values.
Results may differ from a plain program's by a relative error of at most 0.00013.
Values sent between devices are 32-bit elements; how exact they have to be, the bound alone decides.
No kernel may reach another device: no remote copies, remote signals or barrier semaphores. Data moves between devices by JAX's collectives and lax.ppermute only.
A program may use at most 128 MiB of HBM per device.

v0:
```python
import functools

import jax
import jax.numpy as jnp
from jax import lax
from jax.experimental import pallas as pl
from jax.experimental.pallas import tpu as pltpu
from jax.sharding import Mesh
from jax.sharding import PartitionSpec as P

ITERS = 2
AXES = ("zh", "x", "c", "zl", "y")
NO = 48
NAUX = 640
TILES = NAUX // 128
GROUP = 4
CHUNK = 256
LOOP_PRODUCT = (True, False)
VMEM = pl.BlockSpec(memory_space=pltpu.VMEM)
NT = (((1,), (1,)), ((), ()))


def x_step(v, shift, flip):
    pairs = []
    for zh in range(2):
        for x in range(4):
            for zl in range(2):
                to_zh, to_zl = (1 - zh, 1 - zl) if flip else (zh, zl)
                pairs.append(((zh * 4 + x) * 2 + zl, (to_zh * 4 + (x + shift) % 4) * 2 + to_zl))
    return lax.ppermute(v, ("zh", "x", "zl"), pairs)


def y_step(v, shift, flip):
    pairs = []
    for zl in range(2):
        for y in range(4):
            pairs.append((zl * 4 + y, (1 - zl if flip else zl) * 4 + (y + shift) % 4))
    return lax.ppermute(v, ("zl", "y"), pairs)


def core_swap(v):
    return lax.ppermute(v, "c", [(0, 1), (1, 0)])


def place(zh, x, c, zl, y):
    return (((zh * 4 + x % 4) * 2 + c) * 2 + zl) * 4 + y % 4


def side_step(v, shift, flip):
    pairs = []
    for zh in range(2):
        for x in range(4):
            for zl in range(2):
                for y in range(4):
                    there = 1 - zl if flip else zl
                    pairs.append((place(zh, x, 0, zl, y), place(zh, x, 0, there, y + shift)))
                    far = 1 - zh if flip else zh
                    pairs.append((place(zh, x, 1, zl, y), place(far, x + shift, 1, there, y)))
    return lax.ppermute(v, AXES, pairs)


def gather(own, core):
    pair = jnp.concatenate((own, core_swap(own)), 1)
    partner = side_step(pair, 0, True)
    left = side_step(pair, 1, False)
    right = side_step(pair, -1, False)
    near = lax.optimization_barrier([pair, partner, left, right])
    pair, partner, left, right = near
    far_left = side_step(left, 0, True)
    far_right = side_step(right, 0, True)
    far = side_step(pair, 2, False)
    far_partner = side_step(partner, 2, False)
    first = prepare(core, near, [core_swap(v) for v in near])
    far, first = lax.optimization_barrier(([far, far_partner, far_left, far_right], first))
    return [first, prepare(core, far, [core_swap(v) for v in far])]


def split(v):
    hi = v.astype(jnp.bfloat16)
    lo = (v - hi.astype(jnp.float32)).astype(jnp.bfloat16)
    return hi, lo


def occupied(i, count):
    return pl.ds(i, count, stride=NO)


def prepare_kernel(*refs):
    core, got, swapped = refs[0], refs[1:5], refs[5:9]
    col_hi, col_lo, row_hi, row_lo, rows, cols = refs[9:]
    span = GROUP * NO
    count = GROUP * len(got)
    half = GROUP // 2

    def fill(row_refs, col_refs, first):
        def tile_of(k, _):
            source = pl.ds(pl.multiple_of(k * span, 8), span)
            lanes = pl.ds(pl.multiple_of(k * 128, 128), 128)
            for i in range(NO):
                for g, ref in enumerate(col_refs):
                    at = i * count + g * GROUP
                    cols[at : at + GROUP, lanes] = ref.at[source, :][occupied(i, GROUP), :]
                for g, ref in enumerate(row_refs):
                    at = i * count // 2 + g * half
                    rows[at : at + half, lanes] = ref.at[source, :][occupied(first + i, half), :]
            return 0

        lax.fori_loop(0, TILES, tile_of, 0)

    @pl.when(core[0, 0] == 0)
    def _():
        fill(got, swapped, 0)

    @pl.when(core[0, 0] != 0)
    def _():
        fill(swapped, got, half * NO)

    def halve(source, hi, lo):
        step = 128

        def body(i, _):
            at = pl.ds(pl.multiple_of(i * step, step), step)
            hi[at, :], lo[at, :] = split(source[at, :])
            return 0

        lax.fori_loop(0, source.shape[0] // step, body, 0)

    halve(rows, row_hi, row_lo)
    halve(cols, col_hi, col_lo)


def flat(v):
    return v.reshape(-1, v.shape[2])


def prepare(core, got, swapped):
    width = NO * GROUP * len(got)
    height = width // 2
    col = jax.ShapeDtypeStruct((width, NAUX), jnp.bfloat16)
    row = jax.ShapeDtypeStruct((height, NAUX), jnp.bfloat16)
    return pl.pallas_call(
        prepare_kernel,
        out_shape=(col, col, row, row, jax.ShapeDtypeStruct(row.shape, jnp.float32)),
        in_specs=[pl.BlockSpec(memory_space=pltpu.SMEM)] + [VMEM] * (2 * len(got)),
        out_specs=(VMEM,) * 5,
        scratch_shapes=[pltpu.VMEM((width, NAUX), jnp.float32)],
        compiler_params=pltpu.CompilerParams(vmem_limit_bytes=8 << 20),
        name="prepare",
    )(core, *map(flat, got), *map(flat, swapped))


def swap_chunks(v):
    lane = lax.broadcasted_iota(jnp.int32, v[0].shape, 1)
    low = lane < 64
    even = (lane // 32) % 2 == 0

    def halves(a, b):
        r = pltpu.roll(jnp.where(low, b, a), 64, 1)
        return jnp.where(low, a, r), jnp.where(low, r, b)

    def quarters(a, b):
        m = jnp.where(even, b, a)
        return (
            jnp.where(even, a, pltpu.roll(m, 32, 1)),
            jnp.where(even, pltpu.roll(m, 96, 1), b),
        )

    a0, a2 = halves(v[0], v[2])
    a1, a3 = halves(v[1], v[3])
    w0, w1 = quarters(a0, a1)
    w2, w3 = quarters(a2, a3)
    return w0, w1, w2, w3


def tile_kernel(count, scale, *refs):
    fhi, flo, chi, clo = refs[:2], refs[2:4], refs[4:6], refs[6:8]
    rhi, rlo, c_rows, row_pair = (refs[8 + k * count : 8 + (k + 1) * count] for k in range(4))
    col_pair = refs[8 + 4 * count]
    outs = refs[9 + 4 * count : 9 + 6 * count]
    energy, rows, direct, *slots = refs[9 + 6 * count :]
    na = 8
    block = NO * na
    width = direct.shape[1]
    nb = width // NO
    per = 128 // nb
    blocks = NO // per
    tall = per * na

    def span(start, size):
        if isinstance(start, int):
            return slice(start, start + size)
        return pl.ds(pl.multiple_of(start, size), size)

    def chunk(pair, n):
        piece = nb // len(pair)
        first = n * (CHUNK // nb)
        return jnp.concatenate(
            [r[span((first + i) * piece, piece), :] for i in range(CHUNK // nb) for r in pair], 0
        )

    def product(n, _):
        hi, lo = chunk(fhi, n), chunk(flo, n)
        for g in range(count):
            acc = lax.dot_general(rhi[g][...], hi, NT, preferred_element_type=jnp.float32)
            acc += lax.dot_general(rhi[g][...], lo, NT, preferred_element_type=jnp.float32)
            acc += lax.dot_general(rlo[g][...], hi, NT, preferred_element_type=jnp.float32)
            direct[g * block : (g + 1) * block, span(n * CHUNK, CHUNK)] = acc
        return 0

    chunks = width // CHUNK
    if LOOP_PRODUCT[count - 1]:
        lax.fori_loop(0, chunks, product, 0)
    else:
        for n in range(chunks):
            product(n, 0)

    def amplitudes(n, slot):
        hi, lo = slots[2 * slot], slots[2 * slot + 1]
        for jj in range(CHUNK // 128):
            j = n * (CHUNK // 128) + jj
            lanes = span(j * 128, 128)
            at = slice(jj * 128, (jj + 1) * 128)
            for g in range(count):
                top = g * block
                for i in range(blocks):
                    here = slice(top + i * tall, top + (i + 1) * tall)
                    other = direct[span(top + j * tall, tall), i * 128 : (i + 1) * 128]
                    parts = [other[k * na : (k + 1) * na] for k in range(per)]
                    value = direct[here, lanes]
                    value = value + value - jnp.concatenate(swap_chunks(parts), 0)
                    e_sum = row_pair[g][i * tall : (i + 1) * tall, :] + col_pair[0:1, lanes]
                    hi[here, at], lo[here, at] = split(value / e_sum)

    def contract(n, slot):
        hi, lo = slots[2 * slot], slots[2 * slot + 1]
        right = chunk(chi, n)
        acc = jnp.dot(hi[...], right, preferred_element_type=jnp.float32)
        acc += jnp.dot(hi[...], chunk(clo, n), preferred_element_type=jnp.float32)
        acc += jnp.dot(lo[...], right, preferred_element_type=jnp.float32)
        rows[...] += acc

    def two_chunks(m, _):
        amplitudes(2 * m + 1, 1)
        contract(2 * m, 0)
        amplitudes(2 * m + 2, 0)
        contract(2 * m + 1, 1)
        return 0

    last = chunks - 1
    rows[...] = jnp.zeros_like(rows)
    amplitudes(0, 0)
    for m in range(last // 2):
        two_chunks(m, 0)
    amplitudes(last, 1)
    contract(last - 1, 0)
    contract(last, 1)

    def finish(k, total):
        target = pl.ds(pl.multiple_of(k * GROUP * NO, 8), GROUP * NO)
        lanes = pl.ds(pl.multiple_of(k * 128, 128), 128)
        for i in range(count * NO):
            w = rows[i * na : (i + 1) * na, lanes] * scale
            g, o = i // NO, i % NO
            for h in range(2):
                out = outs[g * 2 + h].at[target, :]
                out[occupied(o, GROUP), :] = w[h * GROUP : (h + 1) * GROUP]
            total += w * c_rows[g][o * na : (o + 1) * na, lanes]
        return total

    total = lax.fori_loop(0, TILES, finish, jnp.zeros((na, 128), jnp.float32))
    energy[...] = jnp.full(energy.shape, jnp.sum(total), jnp.float32)


def tile(groups, factor, chol, row_pair, col_pair, total):
    count = len(groups)
    height = 8 * NO * count
    width = 2 * factor[0][0].shape[0]
    part = jax.ShapeDtypeStruct((TILES * NO * GROUP, 128), jnp.float32)
    out = pl.pallas_call(
        functools.partial(tile_kernel, count, -1.0 / total),
        out_shape=(part,) * (2 * count) + (jax.ShapeDtypeStruct((8, 128), jnp.float32),),
        in_specs=[VMEM] * (9 + 4 * count),
        out_specs=(VMEM,) * (2 * count + 1),
        scratch_shapes=[
            pltpu.VMEM((height, NAUX), jnp.float32),
            pltpu.VMEM((height, width), jnp.float32),
        ]
        + [pltpu.VMEM((height, CHUNK), jnp.bfloat16)] * 4,
        compiler_params=pltpu.CompilerParams(vmem_limit_bytes=(8 if count == 1 else 14) << 20),
        name="amplitude_tile",
    )(
        *[f[0] for f in factor], *[f[1] for f in factor],
        *[c[0] for c in chol], *[c[1] for c in chol],
        *[factor[g][2] for g in groups], *[factor[g][3] for g in groups],
        *[chol[g][4] for g in groups], *[row_pair[g] for g in groups], col_pair,
    )
    return [v.reshape(TILES, -1, 128) for v in out[: 2 * count]], out[2 * count]


def shards(chol, eps_occ, eps_vir):
    zh, x, c, zl, y = (lax.axis_index(a) for a in AXES)
    total = eps_vir.shape[0] * eps_occ.shape[0]

    def virtuals(places):
        ids = jnp.stack([place(*p) for p in places])
        return eps_vir.reshape(-1, 2)[ids].reshape(-1)

    order = ((0, 0), (1, 0), (0, 3), (0, 1), (0, 2), (1, 2), (1, 3), (1, 1))
    col_vir = virtuals(
        [(zh ^ f, x + d, cc, zl ^ f, y) for f, d in order for cc in (1, 0)]
    )
    row_vir = virtuals([(zh, x, c, zl ^ f, y + d) for f, d in order]).reshape(2, -1)
    col_pair = jnp.broadcast_to((col_vir[None, :] - eps_occ[:, None]).reshape(1, -1), (8, col_vir.shape[0] * NO))
    row_pair = (row_vir[:, None, :] - eps_occ[None, :, None]).reshape(2, -1, 1)
    row_pair = jnp.broadcast_to(row_pair, row_pair.shape[:2] + (128,))

    half = chol.shape[0]
    chol = jnp.transpose(chol.reshape(half, TILES, 128), (1, 0, 2))
    core = c.astype(jnp.int32).reshape(1, 1)
    chol_parts = None
    factor = chol
    energies = []
    for step in range(ITERS):
        factor_parts = gather(factor, core)
        if step == 0:
            chol_parts = factor_parts
        if step < ITERS - 1:
            (p_far, p_far_sides), e_far = tile((1,), factor_parts, chol_parts, row_pair, col_pair, total)
            (p_mine, p_sides), e_near = tile((0,), factor_parts, chol_parts, row_pair, col_pair, total)
            energies.append(e_far + e_near)
        else:
            (p_mine, p_sides, p_far, p_far_sides), e_all = tile(
                (0, 1), factor_parts, chol_parts, row_pair, col_pair, total
            )
            energies.append(e_all)
        p_mine = p_mine + y_step(p_far, 2, False)
        p_sides = p_sides + y_step(p_far_sides, 0, True)
        to_left, to_right, to_partner = p_sides[:, :half], p_sides[:, half:], p_mine[:, half:]
        if step == ITERS - 1:
            lane = lax.broadcasted_iota(jnp.int32, (8, 128), 1)
            e = jnp.where(lane == 0, energies[0], energies[1])
            e = e + core_swap(e)
            e = e + x_step(e, 0, True)
            e = e + y_step(e, 2, True)
            tail = jnp.broadcast_to(e[None], (TILES, 8, 128))
            to_left, to_right, to_partner = (
                jnp.concatenate((v, tail), 1) for v in (to_left, to_right, to_partner)
            )
        a = y_step(to_left, -1, False)
        b = y_step(to_right, 1, False)
        p = y_step(to_partner, 0, True)
        work = p_mine[:, :half] + a[:, :half] + b[:, :half] + p[:, :half]
        factor = chol + work

    e = e + a[0, half:] + b[0, half:] + p[0, half:]
    e = e + x_step(e, 1, False) + x_step(e, -1, False) + x_step(e, 2, False)
    work = jnp.transpose(work, (1, 0, 2)).reshape(half, -1)
    return (work, e[0, :2] / jnp.float32(total))


def solution(mesh):
    torus = Mesh(mesh.devices.reshape(2, 4, 2, 2, 4), AXES)
    placed = (P(AXES, None), P(), P())
    return jax.shard_map(
        shards, mesh=torus, in_specs=placed, out_specs=(P(AXES, None), P()), check_vma=False
    )
```

profile of v0, /device:TPU:0, one launch (start us, length us, event | category | flops | bytes accessed | tf_op | source)
XLA Modules:
  0.0 168.5 jit_solution(2085215377734337075)
XLA Ops:
  0.6 1.1 copy.64
  2.0 1.5 collective-permute-done
  3.5 2.1 %collective-permute-start.1 = (f32[5,192,128]{2,1,0:T(8,128)S(1)}, f32[5,192,128]{2,1,0:T(8,128)}, u32[]{:S(2)}, u32[]{:S(2)}) collective-permute-start(f32[5,192,128]{2,1,0:T(8,128)S(1)} %pad_maximum_fusion.3), channel_id=1, source_target_pairs={{0,4},{8,76},{1,5},{9,77},{2,6},{10,78},{3,7},{11,79},{4,0},{12,72... | collective-permute-start | bytes 1474568 | tf_op jit(solution)/shard_map/ppermute | solution.py:59
  5.6 1.6 collective-permute-start.2
  7.2 1.7 collective-permute-start.3
  8.9 3.7 %collective-permute-done.1 = f32[5,192,128]{2,1,0:T(8,128)} collective-permute-done((f32[5,192,128]{2,1,0:T(8,128)S(1)}, f32[5,192,128]{2,1,0:T(8,128)}, u32[]{:S(2)}, u32[]{:S(2)}) %collective-permute-start.1) | collective-permute-done | bytes 491552 | tf_op jit(solution)/shard_map/ppermute | solution.py:59
  12.6 3.2 %collective-permute-done.2 = f32[5,192,128]{2,1,0:T(8,128)} collective-permute-done((f32[5,192,128]{2,1,0:T(8,128)S(1)}, f32[5,192,128]{2,1,0:T(8,128)}, u32[]{:S(2)}, u32[]{:S(2)}) %collective-permute-start.2) | collective-permute-done | bytes 491552 | tf_op jit(solution)/shard_map/ppermute | solution.py:59
  18.1 3.3 %collective-permute-start.4 = (f32[5,192,128]{2,1,0:T(8,128)S(1)}, f32[5,192,128]{2,1,0:T(8,128)}, u32[]{:S(2)}, u32[]{:S(2)}) collective-permute-start(f32[5,192,128]{2,1,0:T(8,128)S(1)} %pad_maximum_fusion.3), channel_id=1, source_target_pairs={{0,2},{8,40},{1,3},{9,41},{2,0},{10,42},{3,1},{11,43},{4,6},{12,44... | collective-permute-start | bytes 1474568 | tf_op jit(solution)/shard_map/ppermute | solution.py:59
  21.7 0.8 copy-done
  22.5 0.8 copy-done.2
  23.3 0.8 copy-done.4
  24.0 2.0 %collective-permute-start.7 = (f32[5,192,128]{2,1,0:T(8,128)}, f32[5,192,128]{2,1,0:T(8,128)}, u32[]{:S(2)}, u32[]{:S(2)}) collective-permute-start(f32[5,192,128]{2,1,0:T(8,128)} %collective-permute-done.3), channel_id=1, source_target_pairs={{0,4},{8,76},{1,5},{9,77},{2,6},{10,78},{3,7},{11,79},{4,0},{12,72... | collective-permute-start | bytes 1474568 | tf_op jit(solution)/shard_map/ppermute | solution.py:59
  27.5 0.8 copy-done.10
  28.3 1.0 copy-done.1
  29.3 1.0 copy-done.3
  30.3 1.0 copy-done.5
  31.4 1.0 copy-done.11
  32.4 3.3 %prepare.4 = (bf16[768,640]{1,0:T(8,128)(2,1)S(1)}, bf16[768,640]{1,0:T(8,128)(2,1)S(1)}, bf16[384,640]{1,0:T(8,128)(2,1)S(1)}, bf16[384,640]{1,0:T(8,128)(2,1)S(1)}, f32[384,640]{1,0:T(8,128)S(1)}) custom-call(s32[1,1]{1,0:T(1,128)} %bitcast.2.refs_0_, f32[960,128]{1,0:T(8,128)S(1)} %bitcast.93, f32[960,128]{1,0:T(8,128)} %bitcast.4.refs_2_, ...), custom_call_target="tpu_custom_call" | custom-call | tf_op jit(solution)/shard_map/prepare/pallas_call | solution.py:141
  35.7 0.8 copy-done.6
  36.4 0.8 copy-done.8
  37.7 0.8 collective-permute-start.12
  40.2 0.8 collective-permute-done.13
  41.7 0.7 collective-permute-done.15
  42.4 3.8 %prepare.5 = (bf16[768,640]{1,0:T(8,128)(2,1)S(1)}, bf16[768,640]{1,0:T(8,128)(2,1)S(1)}, bf16[384,640]{1,0:T(8,128)(2,1)S(1)}, bf16[384,640]{1,0:T(8,128)(2,1)S(1)}, f32[384,640]{1,0:T(8,128)S(1)}) custom-call(s32[1,1]{1,0:T(1,128)} %bitcast.2.refs_0_, f32[960,128]{1,0:T(8,128)} %bitcast.11.refs_1_, f32[960,128]{1,0:T(8,128)} %bitcast.12.refs_2_, ...), custom_call_target="tpu_custom_call" | custom-call | tf_op jit(solution)/shard_map/prepare/pallas_call | solution.py:141
  46.4 7.9 %amplitude_tile.4 = (f32[960,128]{1,0:T(8,128)S(1)}, f32[960,128]{1,0:T(8,128)S(1)}, f32[8,128]{1,0:T(8,128)S(1)}) custom-call(bf16[768,640]{1,0:T(8,128)(2,1)S(1)} %get-tuple-element.65.refs_0_.refs_4_, bf16[768,640]{1,0:T(8,128)(2,1)S(1)} %get-tuple-element.70.refs_1_.refs_5_, bf16[768,640]{1,0:T(8,128)(2,1)S(1)} %get-tuple-element.71.refs_2_.refs_6_, ...), custom_call_target="tpu_custom_call" | custom-call | tf_op jit(solution)/shard_map/amplitude_tile/pallas_call | solution.py:279
  54.5 3.3 %collective-permute-start.16 = (f32[5,192,128]{2,1,0:T(8,128)S(1)}, f32[5,192,128]{2,1,0:T(8,128)S(1)}, u32[]{:S(2)}, u32[]{:S(2)}) collective-permute-start(f32[5,192,128]{2,1,0:T(8,128)S(1)} %bitcast.121), channel_id=1, source_target_pairs={{0,2},{1,3},{2,0},{3,1},{4,6},{5,7},{6,4},{7,5},{8,10},{9,11},{10,... | collective-permute-start | bytes 1474568 | tf_op jit(solution)/shard_map/ppermute | solution.py:38
  58.0 7.8 %amplitude_tile.3 = (f32[960,128]{1,0:T(8,128)S(1)}, f32[960,128]{1,0:T(8,128)S(1)}, f32[8,128]{1,0:T(8,128)S(1)}) custom-call(bf16[768,640]{1,0:T(8,128)(2,1)S(1)} %get-tuple-element.65.refs_0_.refs_4_, bf16[768,640]{1,0:T(8,128)(2,1)S(1)} %get-tuple-element.70.refs_1_.refs_5_, bf16[768,640]{1,0:T(8,128)(2,1)S(1)} %get-tuple-element.71.refs_2_.refs_6_, ...), custom_call_target="tpu_custom_call" | custom-call | tf_op jit(solution)/shard_map/amplitude_tile/pallas_call | solution.py:279
  65.8 2.0 %collective-permute-done.17 = f32[5,192,128]{2,1,0:T(8,128)S(1)} collective-permute-done((f32[5,192,128]{2,1,0:T(8,128)S(1)}, f32[5,192,128]{2,1,0:T(8,128)S(1)}, u32[]{:S(2)}, u32[]{:S(2)}) %collective-permute-start.17) | collective-permute-done | bytes 491552 | tf_op jit(solution)/shard_map/ppermute | solution.py:38
  67.9 3.1 %collective-permute-start.18 = (f32[5,96,128]{2,1,0:T(8,128)S(1)}, f32[5,96,128]{2,1,0:T(8,128)S(1)}, u32[]{:S(2)}, u32[]{:S(2)}) collective-permute-start(f32[5,96,128]{2,1,0:T(8,128)S(1)} %get-tuple-element.120), channel_id=1, source_target_pairs={{0,3},{1,0},{2,1},{3,2},{4,7},{5,4},{6,5},{7,6},{8,11},{9,8},{10,9... | collective-permute-start | bytes 737288 | tf_op jit(solution)/shard_map/ppermute | solution.py:38
  71.5 4.5 %collective-permute-done.18 = f32[5,96,128]{2,1,0:T(8,128)S(1)} collective-permute-done((f32[5,96,128]{2,1,0:T(8,128)S(1)}, f32[5,96,128]{2,1,0:T(8,128)S(1)}, u32[]{:S(2)}, u32[]{:S(2)}) %collective-permute-start.18) | collective-permute-done | bytes 245792 | tf_op jit(solution)/shard_map/ppermute | solution.py:38
  75.9 3.4 %collective-permute-done.19 = f32[5,96,128]{2,1,0:T(8,128)S(1)} collective-permute-done((f32[5,96,128]{2,1,0:T(8,128)S(1)}, f32[5,96,128]{2,1,0:T(8,128)S(1)}, u32[]{:S(2)}, u32[]{:S(2)}) %collective-permute-start.19) | collective-permute-done | bytes 245792 | tf_op jit(solution)/shard_map/ppermute | solution.py:38
  79.5 1.5 collective-permute-done.21
  81.7 3.2 %collective-permute-start.24 = (f32[5,192,128]{2,1,0:T(8,128)S(1)}, f32[5,192,128]{2,1,0:T(8,128)S(1)}, u32[]{:S(2)}, u32[]{:S(2)}) collective-permute-start(f32[5,192,128]{2,1,0:T(8,128)S(1)} %pad_maximum_fusion.4), channel_id=1, source_target_pairs={{0,3},{8,56},{1,0},{9,57},{2,1},{10,58},{3,2},{11,59},{4,7},{12,60... | collective-permute-start | bytes 1474568 | tf_op jit(solution)/shard_map/ppermute | solution.py:59
  84.9 5.1 %collective-permute-done.22 = f32[5,192,128]{2,1,0:T(8,128)S(1)} collective-permute-done((f32[5,192,128]{2,1,0:T(8,128)S(1)}, f32[5,192,128]{2,1,0:T(8,128)S(1)}, u32[]{:S(2)}, u32[]{:S(2)}) %collective-permute-start.22) | collective-permute-done | bytes 491552 | tf_op jit(solution)/shard_map/ppermute | solution.py:59
  90.0 1.7 %collective-permute-done.23 = f32[5,192,128]{2,1,0:T(8,128)S(1)} collective-permute-done((f32[5,192,128]{2,1,0:T(8,128)S(1)}, f32[5,192,128]{2,1,0:T(8,128)S(1)}, u32[]{:S(2)}, u32[]{:S(2)}) %collective-permute-start.23) | collective-permute-done | bytes 491552 | tf_op jit(solution)/shard_map/ppermute | solution.py:59
  92.7 2.2 %collective-permute-start.25 = (f32[5,192,128]{2,1,0:T(8,128)S(1)}, f32[5,192,128]{2,1,0:T(8,128)S(1)}, u32[]{:S(2)}, u32[]{:S(2)}) collective-permute-start(f32[5,192,128]{2,1,0:T(8,128)S(1)} %pad_maximum_fusion.4), channel_id=1, source_target_pairs={{0,2},{8,40},{1,3},{9,41},{2,0},{10,42},{3,1},{11,43},{4,6},{12,44... | collective-permute-start | bytes 1474568 | tf_op jit(solution)/shard_map/ppermute | solution.py:59
  94.9 1.4 collective-permute-start.26
  96.3 1.5 collective-permute-start.27
  98.3 2.9 %prepare.6 = (bf16[768,640]{1,0:T(8,128)(2,1)S(1)}, bf16[768,640]{1,0:T(8,128)(2,1)S(1)}, bf16[384,640]{1,0:T(8,128)(2,1)S(1)}, bf16[384,640]{1,0:T(8,128)(2,1)S(1)}, f32[384,640]{1,0:T(8,128)}) custom-call(s32[1,1]{1,0:T(1,128)} %bitcast.2.refs_0_, f32[960,128]{1,0:T(8,128)S(1)} %bitcast.94, f32[960,128]{1,0:T(8,128)S(1)} %bitcast.101, ...), custom_call_target="tpu_custom_call" | custom-call | tf_op jit(solution)/shard_map/prepare/pallas_call | solution.py:141
  101.2 1.9 %collective-permute-done.25 = f32[5,192,128]{2,1,0:T(8,128)S(1)} collective-permute-done((f32[5,192,128]{2,1,0:T(8,128)S(1)}, f32[5,192,128]{2,1,0:T(8,128)S(1)}, u32[]{:S(2)}, u32[]{:S(2)}) %collective-permute-start.25) | collective-permute-done | bytes 491552 | tf_op jit(solution)/shard_map/ppermute | solution.py:59
  103.1 5.3 %collective-permute-done.26 = f32[5,192,128]{2,1,0:T(8,128)S(1)} collective-permute-done((f32[5,192,128]{2,1,0:T(8,128)S(1)}, f32[5,192,128]{2,1,0:T(8,128)S(1)}, u32[]{:S(2)}, u32[]{:S(2)}) %collective-permute-start.26) | collective-permute-done | bytes 491552 | tf_op jit(solution)/shard_map/ppermute | solution.py:59
  108.3 2.0 %collective-permute-done.28 = f32[5,192,128]{2,1,0:T(8,128)S(1)} collective-permute-done((f32[5,192,128]{2,1,0:T(8,128)S(1)}, f32[5,192,128]{2,1,0:T(8,128)S(1)}, u32[]{:S(2)}, u32[]{:S(2)}) %collective-permute-start.28) | collective-permute-done | bytes 491552 | tf_op jit(solution)/shard_map/ppermute | solution.py:59
  111.4 0.8 collective-permute-done.33
  112.2 0.7 collective-permute-done.34
  112.9 0.7 collective-permute-done.35
  113.6 0.7 collective-permute-done.36
  114.3 3.1 %prepare.7 = (bf16[768,640]{1,0:T(8,128)(2,1)S(1)}, bf16[768,640]{1,0:T(8,128)(2,1)S(1)}, bf16[384,640]{1,0:T(8,128)(2,1)S(1)}, bf16[384,640]{1,0:T(8,128)(2,1)S(1)}, f32[384,640]{1,0:T(8,128)}) custom-call(s32[1,1]{1,0:T(1,128)} %bitcast.2.refs_0_, f32[960,128]{1,0:T(8,128)S(1)} %bitcast.98, f32[960,128]{1,0:T(8,128)S(1)} %bitcast.99, ...), custom_call_target="tpu_custom_call" | custom-call | tf_op jit(solution)/shard_map/prepare/pallas_call | solution.py:141
  117.4 12.8 %amplitude_tile.5 = (f32[960,128]{1,0:T(8,128)S(1)}, f32[960,128]{1,0:T(8,128)S(1)}, f32[960,128]{1,0:T(8,128)S(1)}, f32[960,128]{1,0:T(8,128)S(1)}, f32[8,128]{1,0:T(8,128)S(1)}) custom-call(bf16[768,640]{1,0:T(8,128)(2,1)S(1)} %get-tuple-element.91.refs_0_, bf16[768,640]{1,0:T(8,128)(2,1)S(1)} %get-tuple-element.96.refs_1_, ...), custom_call_target="tpu_custom_call" | custom-call | tf_op jit(solution)/shard_map/amplitude_tile/pallas_call | solution.py:279
  130.2 2.2 %collective-permute-start.37 = (f32[5,192,128]{2,1,0:T(8,128)S(1)}, f32[5,192,128]{2,1,0:T(8,128)S(1)}, u32[]{:S(2)}, u32[]{:S(2)}) collective-permute-start(f32[5,192,128]{2,1,0:T(8,128)S(1)} %bitcast.120), channel_id=1, source_target_pairs={{0,2},{1,3},{2,0},{3,1},{4,6},{5,7},{6,4},{7,5},{8,10},{9,11},{10,... | collective-permute-start | bytes 1474568 | tf_op jit(solution)/shard_map/ppermute | solution.py:38
  132.5 1.5 collective-permute-start.38
  134.1 1.2 collective-permute-done.39
  135.2 1.9 %collective-permute-start.40 = (f32[8,128]{1,0:T(8,128)S(1)}, f32[8,128]{1,0:T(8,128)S(1)}, u32[]{:S(2)}, u32[]{:S(2)}) collective-permute-start(f32[8,128]{1,0:T(8,128)S(1)} %add.468), channel_id=1, source_target_pairs={{0,68},{4,64},{16,84},{20,80},{32,100},{36,96},{48,116},{52,112},{... | collective-permute-start | bytes 12296 | tf_op jit(solution)/shard_map/ppermute | solution.py:30
  137.2 2.9 %collective-permute-done.40 = f32[8,128]{1,0:T(8,128)S(1)} collective-permute-done((f32[8,128]{1,0:T(8,128)S(1)}, f32[8,128]{1,0:T(8,128)S(1)}, u32[]{:S(2)}, u32[]{:S(2)}) %collective-permute-start.40) | collective-permute-done | bytes 4128 | tf_op jit(solution)/shard_map/ppermute | solution.py:30
  140.2 5.9 %collective-permute-done.41 = f32[8,128]{1,0:T(8,128)S(1)} collective-permute-done((f32[8,128]{1,0:T(8,128)S(1)}, f32[8,128]{1,0:T(8,128)S(1)}, u32[]{:S(2)}, u32[]{:S(2)}) %collective-permute-start.41) | collective-permute-done | bytes 4128 | tf_op jit(solution)/shard_map/ppermute | solution.py:38
  146.1 0.8 copy-done.14
  147.1 0.9 slice-done
  148.0 3.3 %collective-permute-start.42 = (f32[5,104,128]{2,1,0:T(8,128)S(1)}, f32[5,104,128]{2,1,0:T(8,128)S(1)}, u32[]{:S(2)}, u32[]{:S(2)}) collective-permute-start(f32[5,104,128]{2,1,0:T(8,128)S(1)} %get-tuple-element.122), channel_id=1, source_target_pairs={{0,3},{1,0},{2,1},{3,2},{4,7},{5,4},{6,5},{7,6},{8,11},{9,8},{10,9... | collective-permute-start | bytes 798728 | tf_op jit(solution)/shard_map/ppermute | solution.py:38
  151.8 4.3 %collective-permute-done.42 = f32[5,104,128]{2,1,0:T(8,128)S(1)} collective-permute-done((f32[5,104,128]{2,1,0:T(8,128)S(1)}, f32[5,104,128]{2,1,0:T(8,128)S(1)}, u32[]{:S(2)}, u32[]{:S(2)}) %collective-permute-start.42) | collective-permute-done | bytes 266272 | tf_op jit(solution)/shard_map/ppermute | solution.py:38
  156.1 3.4 %collective-permute-done.43 = f32[5,104,128]{2,1,0:T(8,128)S(1)} collective-permute-done((f32[5,104,128]{2,1,0:T(8,128)S(1)}, f32[5,104,128]{2,1,0:T(8,128)S(1)}, u32[]{:S(2)}, u32[]{:S(2)}) %collective-permute-start.43) | collective-permute-done | bytes 266272 | tf_op jit(solution)/shard_map/ppermute | solution.py:38
  159.6 1.6 collective-permute-start.45
  161.1 1.7 %collective-permute-start.46 = (f32[8,128]{1,0:T(8,128)S(1)}, f32[8,128]{1,0:T(8,128)S(1)}, u32[]{:S(2)}, u32[]{:S(2)}) collective-permute-start(f32[8,128]{1,0:T(8,128)S(1)} %fusion.4), channel_id=1, source_target_pairs={{0,48},{4,52},{16,0},{20,4},{32,16},{36,20},{48,32},{52,36},{64,11... | collective-permute-start | bytes 12296 | tf_op jit(solution)/shard_map/ppermute | solution.py:30
  162.9 1.5 collective-permute-start.47
  164.6 0.9 copy.67
  165.5 2.5 %collective-permute-done.47 = f32[8,128]{1,0:T(8,128)S(1)} collective-permute-done((f32[8,128]{1,0:T(8,128)S(1)}, f32[8,128]{1,0:T(8,128)S(1)}, u32[]{:S(2)}, u32[]{:S(2)}) %collective-permute-start.47) | collective-permute-done | bytes 4128 | tf_op jit(solution)/shard_map/ppermute | solution.py:30
  (124 shorter events, 13.2 us)
Async XLA Ops:
  1.9 1.6 copy-start.12
  1.9 1.6 collective-permute-start
  3.5 9.0 %collective-permute-start.1 = (f32[5,192,128]{2,1,0:T(8,128)S(1)}, f32[5,192,128]{2,1,0:T(8,128)}, u32[]{:S(2)}, u32[]{:S(2)}) collective-permute-start(f32[5,192,128]{2,1,0:T(8,128)S(1)} %pad_maximum_fusion.3), channel_id=1, source_target_pairs={{0,4},{8,76},{1,5},{9,77},{2,6},{10,78},{3,7},{11,79},{4,0},{12,72... | collective-permute-start | bytes 1474568 | tf_op jit(solution)/shard_map/ppermute | solution.py:59
  5.6 10.1 %collective-permute-start.2 = (f32[5,192,128]{2,1,0:T(8,128)S(1)}, f32[5,192,128]{2,1,0:T(8,128)}, u32[]{:S(2)}, u32[]{:S(2)}) collective-permute-start(f32[5,192,128]{2,1,0:T(8,128)S(1)} %pad_maximum_fusion.3), channel_id=1, source_target_pairs={{0,1},{8,24},{1,2},{9,25},{2,3},{10,26},{3,0},{11,27},{4,5},{12,28... | collective-permute-start | bytes 1474568 | tf_op jit(solution)/shard_map/ppermute | solution.py:59
  7.2 8.9 %collective-permute-start.3 = (f32[5,192,128]{2,1,0:T(8,128)S(1)}, f32[5,192,128]{2,1,0:T(8,128)}, u32[]{:S(2)}, u32[]{:S(2)}) collective-permute-start(f32[5,192,128]{2,1,0:T(8,128)S(1)} %pad_maximum_fusion.3), channel_id=1, source_target_pairs={{0,3},{8,56},{1,0},{9,57},{2,1},{10,58},{3,2},{11,59},{4,7},{12,60... | collective-permute-start | bytes 1474568 | tf_op jit(solution)/shard_map/ppermute | solution.py:59
  16.1 5.5 %collective-permute-start.11 = (f32[5,192,128]{2,1,0:T(8,128)}, f32[5,192,128]{2,1,0:T(8,128)S(1)}, u32[]{:S(2)}, u32[]{:S(2)}) collective-permute-start(f32[5,192,128]{2,1,0:T(8,128)} %collective-permute-done.3), channel_id=1, source_target_pairs={{0,8},{8,0},{1,9},{9,1},{2,10},{10,2},{3,11},{11,3},{4,12},{12,4},... | collective-permute-start | bytes 1474568 | tf_op jit(solution)/shard_map/ppermute | solution.py:42
  16.6 5.8 %collective-permute-start.8 = (f32[5,192,128]{2,1,0:T(8,128)S(1)}, f32[5,192,128]{2,1,0:T(8,128)S(1)}, u32[]{:S(2)}, u32[]{:S(2)}) collective-permute-start(f32[5,192,128]{2,1,0:T(8,128)S(1)} %pad_maximum_fusion.3), channel_id=1, source_target_pairs={{0,8},{8,0},{1,9},{9,1},{2,10},{10,2},{3,11},{11,3},{4,12},{12,4},... | collective-permute-start | bytes 1474568 | tf_op jit(solution)/shard_map/ppermute | solution.py:42
  16.7 6.6 %collective-permute-start.9 = (f32[5,192,128]{2,1,0:T(8,128)}, f32[5,192,128]{2,1,0:T(8,128)S(1)}, u32[]{:S(2)}, u32[]{:S(2)}) collective-permute-start(f32[5,192,128]{2,1,0:T(8,128)} %collective-permute-done.1), channel_id=1, source_target_pairs={{0,8},{8,0},{1,9},{9,1},{2,10},{10,2},{3,11},{11,3},{4,12},{12,4},... | collective-permute-start | bytes 1474568 | tf_op jit(solution)/shard_map/ppermute | solution.py:42
  18.1 19.2 %collective-permute-start.4 = (f32[5,192,128]{2,1,0:T(8,128)S(1)}, f32[5,192,128]{2,1,0:T(8,128)}, u32[]{:S(2)}, u32[]{:S(2)}) collective-permute-start(f32[5,192,128]{2,1,0:T(8,128)S(1)} %pad_maximum_fusion.3), channel_id=1, source_target_pairs={{0,2},{8,40},{1,3},{9,41},{2,0},{10,42},{3,1},{11,43},{4,6},{12,44... | collective-permute-start | bytes 1474568 | tf_op jit(solution)/shard_map/ppermute | solution.py:59
  21.3 15.9 %collective-permute-start.5 = (f32[5,192,128]{2,1,0:T(8,128)}, f32[5,192,128]{2,1,0:T(8,128)}, u32[]{:S(2)}, u32[]{:S(2)}) collective-permute-start(f32[5,192,128]{2,1,0:T(8,128)} %collective-permute-done.1), channel_id=1, source_target_pairs={{0,2},{8,40},{1,3},{9,41},{2,0},{10,42},{3,1},{11,43},{4,6},{12,44... | collective-permute-start | bytes 1474568 | tf_op jit(solution)/shard_map/ppermute | solution.py:59
  21.7 0.8 copy-start
  22.4 5.0 %collective-permute-start.10 = (f32[5,192,128]{2,1,0:T(8,128)}, f32[5,192,128]{2,1,0:T(8,128)S(1)}, u32[]{:S(2)}, u32[]{:S(2)}) collective-permute-start(f32[5,192,128]{2,1,0:T(8,128)} %collective-permute-done.2), channel_id=1, source_target_pairs={{0,8},{8,0},{1,9},{9,1},{2,10},{10,2},{3,11},{11,3},{4,12},{12,4},... | collective-permute-start | bytes 1474568 | tf_op jit(solution)/shard_map/ppermute | solution.py:42
  22.4 0.8 copy-start.2
  23.2 14.0 %collective-permute-start.6 = (f32[5,192,128]{2,1,0:T(8,128)}, f32[5,192,128]{2,1,0:T(8,128)}, u32[]{:S(2)}, u32[]{:S(2)}) collective-permute-start(f32[5,192,128]{2,1,0:T(8,128)} %collective-permute-done.2), channel_id=1, source_target_pairs={{0,4},{8,76},{1,5},{9,77},{2,6},{10,78},{3,7},{11,79},{4,0},{12,72... | collective-permute-start | bytes 1474568 | tf_op jit(solution)/shard_map/ppermute | solution.py:59
  23.2 0.8 copy-start.4
  24.0 13.6 %collective-permute-start.7 = (f32[5,192,128]{2,1,0:T(8,128)}, f32[5,192,128]{2,1,0:T(8,128)}, u32[]{:S(2)}, u32[]{:S(2)}) collective-permute-start(f32[5,192,128]{2,1,0:T(8,128)} %collective-permute-done.3), channel_id=1, source_target_pairs={{0,4},{8,76},{1,5},{9,77},{2,6},{10,78},{3,7},{11,79},{4,0},{12,72... | collective-permute-start | bytes 1474568 | tf_op jit(solution)/shard_map/ppermute | solution.py:59
  27.5 0.8 copy-start.10
  28.3 1.0 copy-start.1
  29.3 1.0 copy-start.3
  30.3 1.0 copy-start.5
  31.4 1.0 copy-start.11
  35.6 0.8 copy-start.6
  37.7 2.5 %collective-permute-start.12 = (f32[5,192,128]{2,1,0:T(8,128)}, f32[5,192,128]{2,1,0:T(8,128)S(1)}, u32[]{:S(2)}, u32[]{:S(2)}) collective-permute-start(f32[5,192,128]{2,1,0:T(8,128)} %collective-permute-done.4), channel_id=1, source_target_pairs={{0,8},{8,0},{1,9},{9,1},{2,10},{10,2},{3,11},{11,3},{4,12},{12,4},... | collective-permute-start | bytes 1474568 | tf_op jit(solution)/shard_map/ppermute | solution.py:42
  38.5 2.5 %collective-permute-start.13 = (f32[5,192,128]{2,1,0:T(8,128)}, f32[5,192,128]{2,1,0:T(8,128)}, u32[]{:S(2)}, u32[]{:S(2)}) collective-permute-start(f32[5,192,128]{2,1,0:T(8,128)} %collective-permute-done.5), channel_id=1, source_target_pairs={{0,8},{8,0},{1,9},{9,1},{2,10},{10,2},{3,11},{11,3},{4,12},{12,4},... | collective-permute-start | bytes 1474568 | tf_op jit(solution)/shard_map/ppermute | solution.py:42
  38.6 3.1 %collective-permute-start.14 = (f32[5,192,128]{2,1,0:T(8,128)}, f32[5,192,128]{2,1,0:T(8,128)}, u32[]{:S(2)}, u32[]{:S(2)}) collective-permute-start(f32[5,192,128]{2,1,0:T(8,128)} %collective-permute-done.6), channel_id=1, source_target_pairs={{0,8},{8,0},{1,9},{9,1},{2,10},{10,2},{3,11},{11,3},{4,12},{12,4},... | collective-permute-start | bytes 1474568 | tf_op jit(solution)/shard_map/ppermute | solution.py:42
  39.0 3.4 %collective-permute-start.15 = (f32[5,192,128]{2,1,0:T(8,128)}, f32[5,192,128]{2,1,0:T(8,128)}, u32[]{:S(2)}, u32[]{:S(2)}) collective-permute-start(f32[5,192,128]{2,1,0:T(8,128)} %collective-permute-done.7), channel_id=1, source_target_pairs={{0,8},{8,0},{1,9},{9,1},{2,10},{10,2},{3,11},{11,3},{4,12},{12,4},... | collective-permute-start | bytes 1474568 | tf_op jit(solution)/shard_map/ppermute | solution.py:42
  46.4 11.6 %copy-start.7 = (bf16[384,640]{1,0:T(8,128)(2,1)S(1)}, bf16[384,640]{1,0:T(8,128)(2,1)}, u32[]{:S(2)}) copy-start(bf16[384,640]{1,0:T(8,128)(2,1)} %copy-done.6) | copy-start | bytes 1474564
  46.4 11.6 %copy-start.9 = (bf16[384,640]{1,0:T(8,128)(2,1)S(1)}, bf16[384,640]{1,0:T(8,128)(2,1)}, u32[]{:S(2)}) copy-start(bf16[384,640]{1,0:T(8,128)(2,1)} %copy-done.8) | copy-start | bytes 1474564
  54.3 13.6 %collective-permute-start.17 = (f32[5,192,128]{2,1,0:T(8,128)S(1)}, f32[5,192,128]{2,1,0:T(8,128)S(1)}, u32[]{:S(2)}, u32[]{:S(2)}) collective-permute-start(f32[5,192,128]{2,1,0:T(8,128)S(1)} %bitcast.122), channel_id=1, source_target_pairs={{0,4},{1,5},{2,6},{3,7},{4,0},{5,1},{6,2},{7,3},{8,12},{9,13},{10,... | collective-permute-start | bytes 1474568 | tf_op jit(solution)/shard_map/ppermute | solution.py:38
  54.5 16.5 %collective-permute-start.16 = (f32[5,192,128]{2,1,0:T(8,128)S(1)}, f32[5,192,128]{2,1,0:T(8,128)S(1)}, u32[]{:S(2)}, u32[]{:S(2)}) collective-permute-start(f32[5,192,128]{2,1,0:T(8,128)S(1)} %bitcast.121), channel_id=1, source_target_pairs={{0,2},{1,3},{2,0},{3,1},{4,6},{5,7},{6,4},{7,5},{8,10},{9,11},{10,... | collective-permute-start | bytes 1474568 | tf_op jit(solution)/shard_map/ppermute | solution.py:38
  67.9 8.0 %collective-permute-start.18 = (f32[5,96,128]{2,1,0:T(8,128)S(1)}, f32[5,96,128]{2,1,0:T(8,128)S(1)}, u32[]{:S(2)}, u32[]{:S(2)}) collective-permute-start(f32[5,96,128]{2,1,0:T(8,128)S(1)} %get-tuple-element.120), channel_id=1, source_target_pairs={{0,3},{1,0},{2,1},{3,2},{4,7},{5,4},{6,5},{7,6},{8,11},{9,8},{10,9... | collective-permute-start | bytes 737288 | tf_op jit(solution)/shard_map/ppermute | solution.py:38
  71.0 8.3 %collective-permute-start.19 = (f32[5,96,128]{2,1,0:T(8,128)S(1)}, f32[5,96,128]{2,1,0:T(8,128)S(1)}, u32[]{:S(2)}, u32[]{:S(2)}) collective-permute-start(f32[5,96,128]{2,1,0:T(8,128)S(1)} %get-tuple-element.121), channel_id=1, source_target_pairs={{0,1},{1,2},{2,3},{3,0},{4,5},{5,6},{6,7},{7,4},{8,9},{9,10},{10,1... | collective-permute-start | bytes 737288 | tf_op jit(solution)/shard_map/ppermute | solution.py:38
  71.1 8.3 %copy-start.13 = (f32[96,5,128]{2,0,1:T(8,128)S(1)}, f32[96,5,128]{2,0,1:T(8,128)}, u32[]{:S(2)}) copy-start(f32[96,5,128]{2,0,1:T(8,128)} %copy-done.12) | copy-start | bytes 737284
  71.1 8.2 %collective-permute-start.20 = (f32[5,96,128]{2,1,0:T(8,128)S(1)}, f32[5,96,128]{2,1,0:T(8,128)S(1)}, u32[]{:S(2)}, u32[]{:S(2)}) collective-permute-start(f32[5,96,128]{2,1,0:T(8,128)S(1)} %slice.83), channel_id=1, source_target_pairs={{0,4},{1,5},{2,6},{3,7},{4,0},{5,1},{6,2},{7,3},{8,12},{9,13},{10,... | collective-permute-start | bytes 737288 | tf_op jit(solution)/shard_map/ppermute | solution.py:38
  79.4 1.6 collective-permute-start.21
  81.0 8.9 %collective-permute-start.22 = (f32[5,192,128]{2,1,0:T(8,128)S(1)}, f32[5,192,128]{2,1,0:T(8,128)S(1)}, u32[]{:S(2)}, u32[]{:S(2)}) collective-permute-start(f32[5,192,128]{2,1,0:T(8,128)S(1)} %pad_maximum_fusion.4), channel_id=1, source_target_pairs={{0,4},{8,76},{1,5},{9,77},{2,6},{10,78},{3,7},{11,79},{4,0},{12,72... | collective-permute-start | bytes 1474568 | tf_op jit(solution)/shard_map/ppermute | solution.py:59
  81.7 10.0 %collective-permute-start.23 = (f32[5,192,128]{2,1,0:T(8,128)S(1)}, f32[5,192,128]{2,1,0:T(8,128)S(1)}, u32[]{:S(2)}, u32[]{:S(2)}) collective-permute-start(f32[5,192,128]{2,1,0:T(8,128)S(1)} %pad_maximum_fusion.4), channel_id=1, source_target_pairs={{0,1},{8,24},{1,2},{9,25},{2,3},{10,26},{3,0},{11,27},{4,5},{12,28... | collective-permute-start | bytes 1474568 | tf_op jit(solution)/shard_map/ppermute | solution.py:59
  81.7 10.0 %collective-permute-start.24 = (f32[5,192,128]{2,1,0:T(8,128)S(1)}, f32[5,192,128]{2,1,0:T(8,128)S(1)}, u32[]{:S(2)}, u32[]{:S(2)}) collective-permute-start(f32[5,192,128]{2,1,0:T(8,128)S(1)} %pad_maximum_fusion.4), channel_id=1, source_target_pairs={{0,3},{8,56},{1,0},{9,57},{2,1},{10,58},{3,2},{11,59},{4,7},{12,60... | collective-permute-start | bytes 1474568 | tf_op jit(solution)/shard_map/ppermute | solution.py:59
  91.7 3.2 %collective-permute-start.29 = (f32[5,192,128]{2,1,0:T(8,128)S(1)}, f32[5,192,128]{2,1,0:T(8,128)S(1)}, u32[]{:S(2)}, u32[]{:S(2)}) collective-permute-start(f32[5,192,128]{2,1,0:T(8,128)S(1)} %pad_maximum_fusion.4), channel_id=1, source_target_pairs={{0,8},{8,0},{1,9},{9,1},{2,10},{10,2},{3,11},{11,3},{4,12},{12,4},... | collective-permute-start | bytes 1474568 | tf_op jit(solution)/shard_map/ppermute | solution.py:42
  91.8 4.4 %collective-permute-start.30 = (f32[5,192,128]{2,1,0:T(8,128)S(1)}, f32[5,192,128]{2,1,0:T(8,128)S(1)}, u32[]{:S(2)}, u32[]{:S(2)}) collective-permute-start(f32[5,192,128]{2,1,0:T(8,128)S(1)} %collective-permute-done.22), channel_id=1, source_target_pairs={{0,8},{8,0},{1,9},{9,1},{2,10},{10,2},{3,11},{11,3},{4,12},{12,4},... | collective-permute-start | bytes 1474568 | tf_op jit(solution)/shard_map/ppermute | solution.py:42
  92.2 5.6 %collective-permute-start.31 = (f32[5,192,128]{2,1,0:T(8,128)S(1)}, f32[5,192,128]{2,1,0:T(8,128)S(1)}, u32[]{:S(2)}, u32[]{:S(2)}) collective-permute-start(f32[5,192,128]{2,1,0:T(8,128)S(1)} %collective-permute-done.23), channel_id=1, source_target_pairs={{0,8},{8,0},{1,9},{9,1},{2,10},{10,2},{3,11},{11,3},{4,12},{12,4},... | collective-permute-start | bytes 1474568 | tf_op jit(solution)/shard_map/ppermute | solution.py:42
  92.3 6.0 %collective-permute-start.32 = (f32[5,192,128]{2,1,0:T(8,128)S(1)}, f32[5,192,128]{2,1,0:T(8,128)S(1)}, u32[]{:S(2)}, u32[]{:S(2)}) collective-permute-start(f32[5,192,128]{2,1,0:T(8,128)S(1)} %collective-permute-done.24), channel_id=1, source_target_pairs={{0,8},{8,0},{1,9},{9,1},{2,10},{10,2},{3,11},{11,3},{4,12},{12,4},... | collective-permute-start | bytes 1474568 | tf_op jit(solution)/shard_map/ppermute | solution.py:42
  92.7 10.3 %collective-permute-start.25 = (f32[5,192,128]{2,1,0:T(8,128)S(1)}, f32[5,192,128]{2,1,0:T(8,128)S(1)}, u32[]{:S(2)}, u32[]{:S(2)}) collective-permute-start(f32[5,192,128]{2,1,0:T(8,128)S(1)} %pad_maximum_fusion.4), channel_id=1, source_target_pairs={{0,2},{8,40},{1,3},{9,41},{2,0},{10,42},{3,1},{11,43},{4,6},{12,44... | collective-permute-start | bytes 1474568 | tf_op jit(solution)/shard_map/ppermute | solution.py:59
  94.9 13.4 %collective-permute-start.26 = (f32[5,192,128]{2,1,0:T(8,128)S(1)}, f32[5,192,128]{2,1,0:T(8,128)S(1)}, u32[]{:S(2)}, u32[]{:S(2)}) collective-permute-start(f32[5,192,128]{2,1,0:T(8,128)S(1)} %collective-permute-done.22), channel_id=1, source_target_pairs={{0,2},{8,40},{1,3},{9,41},{2,0},{10,42},{3,1},{11,43},{4,6},{12,44... | collective-permute-start | bytes 1474568 | tf_op jit(solution)/shard_map/ppermute | solution.py:59
  96.3 12.1 %collective-permute-start.27 = (f32[5,192,128]{2,1,0:T(8,128)S(1)}, f32[5,192,128]{2,1,0:T(8,128)S(1)}, u32[]{:S(2)}, u32[]{:S(2)}) collective-permute-start(f32[5,192,128]{2,1,0:T(8,128)S(1)} %collective-permute-done.23), channel_id=1, source_target_pairs={{0,4},{8,76},{1,5},{9,77},{2,6},{10,78},{3,7},{11,79},{4,0},{12,72... | collective-permute-start | bytes 1474568 | tf_op jit(solution)/shard_map/ppermute | solution.py:59
  97.8 12.6 %collective-permute-start.28 = (f32[5,192,128]{2,1,0:T(8,128)S(1)}, f32[5,192,128]{2,1,0:T(8,128)S(1)}, u32[]{:S(2)}, u32[]{:S(2)}) collective-permute-start(f32[5,192,128]{2,1,0:T(8,128)S(1)} %collective-permute-done.24), channel_id=1, source_target_pairs={{0,4},{8,76},{1,5},{9,77},{2,6},{10,78},{3,7},{11,79},{4,0},{12,72... | collective-permute-start | bytes 1474568 | tf_op jit(solution)/shard_map/ppermute | solution.py:59
  110.4 1.9 %collective-permute-start.33 = (f32[5,192,128]{2,1,0:T(8,128)S(1)}, f32[5,192,128]{2,1,0:T(8,128)S(1)}, u32[]{:S(2)}, u32[]{:S(2)}) collective-permute-start(f32[5,192,128]{2,1,0:T(8,128)S(1)} %collective-permute-done.25), channel_id=1, source_target_pairs={{0,8},{8,0},{1,9},{9,1},{2,10},{10,2},{3,11},{11,3},{4,12},{12,4},... | collective-permute-start | bytes 1474568 | tf_op jit(solution)/shard_map/ppermute | solution.py:42
  110.4 2.6 %collective-permute-start.34 = (f32[5,192,128]{2,1,0:T(8,128)S(1)}, f32[5,192,128]{2,1,0:T(8,128)S(1)}, u32[]{:S(2)}, u32[]{:S(2)}) collective-permute-start(f32[5,192,128]{2,1,0:T(8,128)S(1)} %collective-permute-done.26), channel_id=1, source_target_pairs={{0,8},{8,0},{1,9},{9,1},{2,10},{10,2},{3,11},{11,3},{4,12},{12,4},... | collective-permute-start | bytes 1474568 | tf_op jit(solution)/shard_map/ppermute | solution.py:42
  110.9 2.8 %collective-permute-start.35 = (f32[5,192,128]{2,1,0:T(8,128)S(1)}, f32[5,192,128]{2,1,0:T(8,128)S(1)}, u32[]{:S(2)}, u32[]{:S(2)}) collective-permute-start(f32[5,192,128]{2,1,0:T(8,128)S(1)} %collective-permute-done.27), channel_id=1, source_target_pairs={{0,8},{8,0},{1,9},{9,1},{2,10},{10,2},{3,11},{11,3},{4,12},{12,4},... | collective-permute-start | bytes 1474568 | tf_op jit(solution)/shard_map/ppermute | solution.py:42
  110.9 3.5 %collective-permute-start.36 = (f32[5,192,128]{2,1,0:T(8,128)S(1)}, f32[5,192,128]{2,1,0:T(8,128)S(1)}, u32[]{:S(2)}, u32[]{:S(2)}) collective-permute-start(f32[5,192,128]{2,1,0:T(8,128)S(1)} %collective-permute-done.28), channel_id=1, source_target_pairs={{0,8},{8,0},{1,9},{9,1},{2,10},{10,2},{3,11},{11,3},{4,12},{12,4},... | collective-permute-start | bytes 1474568 | tf_op jit(solution)/shard_map/ppermute | solution.py:42
  130.2 15.9 %collective-permute-start.37 = (f32[5,192,128]{2,1,0:T(8,128)S(1)}, f32[5,192,128]{2,1,0:T(8,128)S(1)}, u32[]{:S(2)}, u32[]{:S(2)}) collective-permute-start(f32[5,192,128]{2,1,0:T(8,128)S(1)} %bitcast.120), channel_id=1, source_target_pairs={{0,2},{1,3},{2,0},{3,1},{4,6},{5,7},{6,4},{7,5},{8,10},{9,11},{10,... | collective-permute-start | bytes 1474568 | tf_op jit(solution)/shard_map/ppermute | solution.py:38
  132.5 14.5 %collective-permute-start.38 = (f32[5,192,128]{2,1,0:T(8,128)S(1)}, f32[5,192,128]{2,1,0:T(8,128)S(1)}, u32[]{:S(2)}, u32[]{:S(2)}) collective-permute-start(f32[5,192,128]{2,1,0:T(8,128)S(1)} %bitcast.119), channel_id=1, source_target_pairs={{0,4},{1,5},{2,6},{3,7},{4,0},{5,1},{6,2},{7,3},{8,12},{9,13},{10,... | collective-permute-start | bytes 1474568 | tf_op jit(solution)/shard_map/ppermute | solution.py:38
  134.0 1.2 collective-permute-start.39
  135.2 4.8 %collective-permute-start.40 = (f32[8,128]{1,0:T(8,128)S(1)}, f32[8,128]{1,0:T(8,128)S(1)}, u32[]{:S(2)}, u32[]{:S(2)}) collective-permute-start(f32[8,128]{1,0:T(8,128)S(1)} %add.468), channel_id=1, source_target_pairs={{0,68},{4,64},{16,84},{20,80},{32,100},{36,96},{48,116},{52,112},{... | collective-permute-start | bytes 12296 | tf_op jit(solution)/shard_map/ppermute | solution.py:30
  140.0 6.0 %collective-permute-start.41 = (f32[8,128]{1,0:T(8,128)S(1)}, f32[8,128]{1,0:T(8,128)S(1)}, u32[]{:S(2)}, u32[]{:S(2)}) collective-permute-start(f32[8,128]{1,0:T(8,128)S(1)} %add.469), channel_id=1, source_target_pairs={{0,6},{1,7},{2,4},{3,5},{4,2},{5,3},{6,0},{7,1},{8,14},{9,15},{10,... | collective-permute-start | bytes 12296 | tf_op jit(solution)/shard_map/ppermute | solution.py:38
  146.1 0.8 copy-start.14
  147.0 0.9 slice-start
  147.9 16.4 %copy-start.15 = (f32[5,192,128]{2,1,0:T(8,128)S(1)}, f32[5,192,128]{2,1,0:T(8,128)}, u32[]{:S(2)}) copy-start(f32[5,192,128]{2,1,0:T(8,128)} %copy-done.14) | copy-start | bytes 1474564
  148.0 8.1 %collective-permute-start.42 = (f32[5,104,128]{2,1,0:T(8,128)S(1)}, f32[5,104,128]{2,1,0:T(8,128)S(1)}, u32[]{:S(2)}, u32[]{:S(2)}) collective-permute-start(f32[5,104,128]{2,1,0:T(8,128)S(1)} %get-tuple-element.122), channel_id=1, source_target_pairs={{0,3},{1,0},{2,1},{3,2},{4,7},{5,4},{6,5},{7,6},{8,11},{9,8},{10,9... | collective-permute-start | bytes 798728 | tf_op jit(solution)/shard_map/ppermute | solution.py:38
  151.3 8.2 %collective-permute-start.43 = (f32[5,104,128]{2,1,0:T(8,128)S(1)}, f32[5,104,128]{2,1,0:T(8,128)S(1)}, u32[]{:S(2)}, u32[]{:S(2)}) collective-permute-start(f32[5,104,128]{2,1,0:T(8,128)S(1)} %get-tuple-element.123), channel_id=1, source_target_pairs={{0,1},{1,2},{2,3},{3,0},{4,5},{5,6},{6,7},{7,4},{8,9},{9,10},{10,1... | collective-permute-start | bytes 798728 | tf_op jit(solution)/shard_map/ppermute | solution.py:38
  151.3 8.2 %collective-permute-start.44 = (f32[5,104,128]{2,1,0:T(8,128)S(1)}, f32[5,104,128]{2,1,0:T(8,128)S(1)}, u32[]{:S(2)}, u32[]{:S(2)}) collective-permute-start(f32[5,104,128]{2,1,0:T(8,128)S(1)} %get-tuple-element.124), channel_id=1, source_target_pairs={{0,4},{1,5},{2,6},{3,7},{4,0},{5,1},{6,2},{7,3},{8,12},{9,13},{10,... | collective-permute-start | bytes 798728 | tf_op jit(solution)/shard_map/ppermute | solution.py:38
  159.6 5.9 %collective-permute-start.45 = (f32[8,128]{1,0:T(8,128)S(1)}, f32[8,128]{1,0:T(8,128)S(1)}, u32[]{:S(2)}, u32[]{:S(2)}) collective-permute-start(f32[8,128]{1,0:T(8,128)S(1)} %fusion.4), channel_id=1, source_target_pairs={{0,16},{4,20},{16,32},{20,36},{32,48},{36,52},{48,0},{52,4},{64,80... | collective-permute-start | bytes 12296 | tf_op jit(solution)/shard_map/ppermute | solution.py:30
  161.1 4.4 %collective-permute-start.46 = (f32[8,128]{1,0:T(8,128)S(1)}, f32[8,128]{1,0:T(8,128)S(1)}, u32[]{:S(2)}, u32[]{:S(2)}) collective-permute-start(f32[8,128]{1,0:T(8,128)S(1)} %fusion.4), channel_id=1, source_target_pairs={{0,48},{4,52},{16,0},{20,4},{32,16},{36,20},{48,32},{52,36},{64,11... | collective-permute-start | bytes 12296 | tf_op jit(solution)/shard_map/ppermute | solution.py:30
  162.9 5.1 %collective-permute-start.47 = (f32[8,128]{1,0:T(8,128)S(1)}, f32[8,128]{1,0:T(8,128)S(1)}, u32[]{:S(2)}, u32[]{:S(2)}) collective-permute-start(f32[8,128]{1,0:T(8,128)S(1)} %fusion.4), channel_id=1, source_target_pairs={{0,32},{4,36},{16,48},{20,52},{32,0},{36,4},{48,16},{52,20},{64,96... | collective-permute-start | bytes 12296 | tf_op jit(solution)/shard_map/ppermute | solution.py:30
  (3 other events, 2.1 us)
where the time goes:
time: 169 us
  waiting for transfers between devices  62.1 us (37%)
  starting transfers between devices  46.5 us (28%)
  Pallas kernels  41.5 us (25%)
  local copies, waits for them, and re-layouts  16.3 us (10%)
    pallas_call x3, Pallas kernels, tile(): pl.pallas_call(functools.partial(tile_kernel, count, -1.0 / total), out_s...  28.4 us
    ppermute x14, waiting for transfers between devices, side_step(): return lax.ppermute(v, AXES, pairs)  23.7 us
    ppermute x11, waiting for transfers between devices, y_step(): return lax.ppermute(v, ('zl', 'y'), pairs)  23.5 us
    ppermute x14, starting transfers between devices, side_step(): return lax.ppermute(v, AXES, pairs)  20.3 us
    ppermute x11, starting transfers between devices, y_step(): return lax.ppermute(v, ('zl', 'y'), pairs)  14.7 us
    pallas_call x4, Pallas kernels, prepare(): pl.pallas_call(prepare_kernel, out_shape=(col, col, row, row, jax.ShapeDt...  13.1 us
    unnamed x38, local copies, waits for them, and re-layouts  12.8 us
    ppermute x19, waiting for transfers between devices, core_swap(): return lax.ppermute(v, 'c', [(0, 1), (1, 0)])  9.43 us
  transfers between devices with their start and end apart: 48, of which 28 were waited for; matrix products, arithmetic and copies ran while one was open for 2% of the time, Pallas kernels for 8%

commit v1 on v0

--- a/solution.py
+++ b/solution.py
@@ -20,16 +20,6 @@
 NT = (((1,), (1,)), ((), ()))
 
 
-def x_step(v, shift, flip):
-    pairs = []
-    for zh in range(2):
-        for x in range(4):
-            for zl in range(2):
-                to_zh, to_zl = (1 - zh, 1 - zl) if flip else (zh, zl)
-                pairs.append(((zh * 4 + x) * 2 + zl, (to_zh * 4 + (x + shift) % 4) * 2 + to_zl))
-    return lax.ppermute(v, ("zh", "x", "zl"), pairs)
-
-
 def y_step(v, shift, flip):
     pairs = []
     for zl in range(2):
@@ -44,6 +34,14 @@
 
 def place(zh, x, c, zl, y):
     return (((zh * 4 + x % 4) * 2 + c) * 2 + zl) * 4 + y % 4
+
+
+def hop(v, flip_zh, shift_x, flip_zl, shift_y):
+    pairs = [
+        (place(zh, x, c, zl, y), place(zh ^ flip_zh, x + shift_x, c, zl ^ flip_zl, y + shift_y))
+        for zh in range(2) for x in range(4) for c in range(2) for zl in range(2) for y in range(4)
+    ]
+    return lax.ppermute(v, AXES, pairs)
 
 
 def side_step(v, shift, flip):
@@ -64,14 +62,14 @@
     partner = side_step(pair, 0, True)
     left = side_step(pair, 1, False)
     right = side_step(pair, -1, False)
-    near = lax.optimization_barrier([pair, partner, left, right])
-    pair, partner, left, right = near
+    near = [pair, partner, left, right]
     far_left = side_step(left, 0, True)
     far_right = side_step(right, 0, True)
-    far = side_step(pair, 2, False)
+    far = side_step(lax.optimization_barrier((pair, left, right))[0], 2, False)
     far_partner = side_step(partner, 2, False)
     first = prepare(core, near, [core_swap(v) for v in near])
-    far, first = lax.optimization_barrier(([far, far_partner, far_left, far_right], first))
+    far = [far, far_partner, far_left, far_right]
+    far = [lax.optimization_barrier((v, first))[0] for v in far]
     return [first, prepare(core, far, [core_swap(v) for v in far])]
 
 
@@ -340,8 +338,8 @@
             lane = lax.broadcasted_iota(jnp.int32, (8, 128), 1)
             e = jnp.where(lane == 0, energies[0], energies[1])
             e = e + core_swap(e)
-            e = e + x_step(e, 0, True)
-            e = e + y_step(e, 2, True)
+            e = e + hop(e, 1, 0, 1, 0) + hop(e, 0, 0, 1, 2) + hop(e, 1, 0, 0, 2)
+            e = e + hop(e, 0, 1, 0, 0) + hop(e, 0, 3, 0, 0) + hop(e, 0, 2, 0, 0)
             tail = jnp.broadcast_to(e[None], (TILES, 8, 128))
             to_left, to_right, to_partner = (
                 jnp.concatenate((v, tail), 1) for v in (to_left, to_right, to_partner)
@@ -353,7 +351,6 @@
         factor = chol + work
 
     e = e + a[0, half:] + b[0, half:] + p[0, half:]
-    e = e + x_step(e, 1, False) + x_step(e, -1, False) + x_step(e, 2, False)
     work = jnp.transpose(work, (1, 0, 2)).reshape(half, -1)
     return (work, e[0, :2] / jnp.float32(total))
 

time: 169 us -> 167 us (0.988)
  waiting for transfers between devices: 62.1 us -> 51.6 us
  starting transfers between devices: 46.5 us -> 55 us
    ppermute x11 -> x10, waiting for transfers between devices: 23.5 us -> 14.6 us  [y_step(): return lax.ppermute(v, ('zl', 'y'), pairs)]
    ppermute x19, starting transfers between devices: 4.68 us -> 9.96 us  [core_swap(): return lax.ppermute(v, 'c', [(0, 1), (1, 0)])]
    ppermute x4 -> x6, starting transfers between devices: 6.75 us -> 11.9 us  [hop(): return lax.ppermute(v, AXES, pairs)]
    ppermute x14, waiting for transfers between devices: 23.7 us -> 19.4 us  [side_step(): return lax.ppermute(v, AXES, pairs)]
    ppermute x4 -> x6, waiting for transfers between devices: 5.39 us -> 9.47 us  [hop(): return lax.ppermute(v, AXES, pairs)]
    ppermute x11 -> x10, starting transfers between devices: 14.7 us -> 14.3 us  [y_step(): return lax.ppermute(v, ('zl', 'y'), pairs)]
  transfers between devices with their start and end apart: 48 -> 49, of which waited for: 28 -> 23; matrix products, arithmetic and copies ran while one was open for 2% -> 1% of each run, Pallas kernels for 8% -> 8%
where the time goes in v1:
time: 167 us
  starting transfers between devices  55 us (33%)
  waiting for transfers between devices  51.6 us (31%)
  Pallas kernels  41.6 us (25%)
  local copies, waits for them, and re-layouts  16.4 us (10%)
    pallas_call x3, Pallas kernels, tile(): pl.pallas_call(functools.partial(tile_kernel, count, -1.0 / total), out_s...  28.5 us
    ppermute x14, waiting for transfers between devices, side_step(): return lax.ppermute(v, AXES, pairs)  19.4 us
    ppermute x14, starting transfers between devices, side_step(): return lax.ppermute(v, AXES, pairs)  18.8 us
    ppermute x10, waiting for transfers between devices, y_step(): return lax.ppermute(v, ('zl', 'y'), pairs)  14.6 us
    ppermute x10, starting transfers between devices, y_step(): return lax.ppermute(v, ('zl', 'y'), pairs)  14.3 us
    pallas_call x4, Pallas kernels, prepare(): pl.pallas_call(prepare_kernel, out_shape=(col, col, row, row, jax.ShapeDt...  13.1 us
    unnamed x38, local copies, waits for them, and re-layouts  12.9 us
    ppermute x6, starting transfers between devices, hop(): return lax.ppermute(v, AXES, pairs)  11.9 us
  transfers between devices with their start and end apart: 49, of which 23 were waited for; matrix products, arithmetic and copies ran while one was open for 1% of the time, Pallas kernels for 8%

profile of v1, /device:TPU:0, one launch (start us, length us, event | category | flops | bytes accessed | tf_op | source)
XLA Modules:
  0.0 166.7 jit_solution(10507120586153153576)
XLA Ops:
  0.6 1.1 copy.64
  2.0 1.5 collective-permute-done
  3.5 3.2 %collective-permute-start.3 = (f32[5,192,128]{2,1,0:T(8,128)S(1)}, f32[5,192,128]{2,1,0:T(8,128)}, u32[]{:S(2)}, u32[]{:S(2)}) collective-permute-start(f32[5,192,128]{2,1,0:T(8,128)S(1)} %pad_maximum_fusion.3), channel_id=1, source_target_pairs={{0,3},{8,56},{1,0},{9,57},{2,1},{10,58},{3,2},{11,59},{4,7},{12,60... | collective-permute-start | bytes 1474568 | tf_op jit(solution)/shard_map/ppermute | solution.py:57
  6.7 1.9 %collective-permute-start.1 = (f32[5,192,128]{2,1,0:T(8,128)S(1)}, f32[5,192,128]{2,1,0:T(8,128)}, u32[]{:S(2)}, u32[]{:S(2)}) collective-permute-start(f32[5,192,128]{2,1,0:T(8,128)S(1)} %pad_maximum_fusion.3), channel_id=1, source_target_pairs={{0,4},{8,76},{1,5},{9,77},{2,6},{10,78},{3,7},{11,79},{4,0},{12,72... | collective-permute-start | bytes 1474568 | tf_op jit(solution)/shard_map/ppermute | solution.py:57
  8.6 1.4 collective-permute-start.4
  10.1 3.0 %collective-permute-done.3 = f32[5,192,128]{2,1,0:T(8,128)} collective-permute-done((f32[5,192,128]{2,1,0:T(8,128)S(1)}, f32[5,192,128]{2,1,0:T(8,128)}, u32[]{:S(2)}, u32[]{:S(2)}) %collective-permute-start.3) | collective-permute-done | bytes 491552 | tf_op jit(solution)/shard_map/ppermute | solution.py:57
  13.1 3.8 %collective-permute-done.2 = f32[5,192,128]{2,1,0:T(8,128)} collective-permute-done((f32[5,192,128]{2,1,0:T(8,128)S(1)}, f32[5,192,128]{2,1,0:T(8,128)}, u32[]{:S(2)}, u32[]{:S(2)}) %collective-permute-start.2) | collective-permute-done | bytes 491552 | tf_op jit(solution)/shard_map/ppermute | solution.py:57
  17.8 1.7 %collective-permute-start.8 = (f32[5,192,128]{2,1,0:T(8,128)S(1)}, f32[5,192,128]{2,1,0:T(8,128)}, u32[]{:S(2)}, u32[]{:S(2)}) collective-permute-start(f32[5,192,128]{2,1,0:T(8,128)S(1)} %pad_maximum_fusion.3), channel_id=1, source_target_pairs={{0,2},{8,40},{1,3},{9,41},{2,0},{10,42},{3,1},{11,43},{4,6},{12,44... | collective-permute-start | bytes 1474568 | tf_op jit(solution)/shard_map/ppermute | solution.py:57
  19.5 1.9 %collective-permute-start.11 = (f32[5,192,128]{2,1,0:T(8,128)}, f32[5,192,128]{2,1,0:T(8,128)}, u32[]{:S(2)}, u32[]{:S(2)}) collective-permute-start(f32[5,192,128]{2,1,0:T(8,128)} %collective-permute-done.3), channel_id=1, source_target_pairs={{0,4},{8,76},{1,5},{9,77},{2,6},{10,78},{3,7},{11,79},{4,0},{12,72... | collective-permute-start | bytes 1474568 | tf_op jit(solution)/shard_map/ppermute | solution.py:57
  21.5 0.8 copy-done
  22.4 0.8 copy-done.2
  23.1 3.3 %collective-permute-start.5 = (f32[5,192,128]{2,1,0:T(8,128)}, f32[5,192,128]{2,1,0:T(8,128)S(1)}, u32[]{:S(2)}, u32[]{:S(2)}) collective-permute-start(f32[5,192,128]{2,1,0:T(8,128)} %collective-permute-done.1), channel_id=1, source_target_pairs={{0,8},{8,0},{1,9},{9,1},{2,10},{10,2},{3,11},{11,3},{4,12},{12,4},... | collective-permute-start | bytes 1474568 | tf_op jit(solution)/shard_map/ppermute | solution.py:32
  26.5 0.8 copy-done.4
  28.7 0.8 copy-done.10
  29.5 1.0 copy-done.1
  30.5 1.0 copy-done.3
  31.5 1.0 copy-done.5
  32.6 1.0 copy-done.11
  33.6 3.3 %prepare.4 = (bf16[768,640]{1,0:T(8,128)(2,1)S(1)}, bf16[768,640]{1,0:T(8,128)(2,1)S(1)}, bf16[384,640]{1,0:T(8,128)(2,1)S(1)}, bf16[384,640]{1,0:T(8,128)(2,1)S(1)}, f32[384,640]{1,0:T(8,128)S(1)}) custom-call(s32[1,1]{1,0:T(1,128)} %bitcast.refs_0_, f32[960,128]{1,0:T(8,128)S(1)} %bitcast.93, f32[960,128]{1,0:T(8,128)} %bitcast.4.refs_2_, ...), custom_call_target="tpu_custom_call" | custom-call | tf_op jit(solution)/shard_map/prepare/pallas_call | solution.py:139
  37.6 0.8 copy-done.8
  41.4 1.4 collective-permute-done.13
  42.8 3.9 %prepare.5 = (bf16[768,640]{1,0:T(8,128)(2,1)S(1)}, bf16[768,640]{1,0:T(8,128)(2,1)S(1)}, bf16[384,640]{1,0:T(8,128)(2,1)S(1)}, bf16[384,640]{1,0:T(8,128)(2,1)S(1)}, f32[384,640]{1,0:T(8,128)S(1)}) custom-call(s32[1,1]{1,0:T(1,128)} %bitcast.refs_0_, f32[960,128]{1,0:T(8,128)} %bitcast.11.refs_1_, f32[960,128]{1,0:T(8,128)} %bitcast.12.refs_2_, ...), custom_call_target="tpu_custom_call" | custom-call | tf_op jit(solution)/shard_map/prepare/pallas_call | solution.py:139
  46.8 7.9 %amplitude_tile.4 = (f32[960,128]{1,0:T(8,128)S(1)}, f32[960,128]{1,0:T(8,128)S(1)}, f32[8,128]{1,0:T(8,128)S(1)}) custom-call(bf16[768,640]{1,0:T(8,128)(2,1)S(1)} %get-tuple-element.42.refs_0_.refs_4_, bf16[768,640]{1,0:T(8,128)(2,1)S(1)} %get-tuple-element.52.refs_1_.refs_5_, bf16[768,640]{1,0:T(8,128)(2,1)S(1)} %get-tuple-element.44.refs_2_.refs_6_, ...), custom_call_target="tpu_custom_call" | custom-call | tf_op jit(solution)/shard_map/amplitude_tile/pallas_call | solution.py:277
  55.2 3.3 %collective-permute-start.16 = (f32[5,192,128]{2,1,0:T(8,128)S(1)}, f32[5,192,128]{2,1,0:T(8,128)S(1)}, u32[]{:S(2)}, u32[]{:S(2)}) collective-permute-start(f32[5,192,128]{2,1,0:T(8,128)S(1)} %bitcast.121), channel_id=1, source_target_pairs={{0,2},{1,3},{2,0},{3,1},{4,6},{5,7},{6,4},{7,5},{8,10},{9,11},{10,... | collective-permute-start | bytes 1474568 | tf_op jit(solution)/shard_map/ppermute | solution.py:28
  58.6 7.8 %amplitude_tile.3 = (f32[960,128]{1,0:T(8,128)S(1)}, f32[960,128]{1,0:T(8,128)S(1)}, f32[8,128]{1,0:T(8,128)S(1)}) custom-call(bf16[768,640]{1,0:T(8,128)(2,1)S(1)} %get-tuple-element.42.refs_0_.refs_4_, bf16[768,640]{1,0:T(8,128)(2,1)S(1)} %get-tuple-element.52.refs_1_.refs_5_, bf16[768,640]{1,0:T(8,128)(2,1)S(1)} %get-tuple-element.44.refs_2_.refs_6_, ...), custom_call_target="tpu_custom_call" | custom-call | tf_op jit(solution)/shard_map/amplitude_tile/pallas_call | solution.py:277
  66.5 1.6 collective-permute-done.17
  68.1 1.4 collective-permute-start.18
  70.3 1.4 collective-permute-start.20
  71.8 3.7 %collective-permute-done.18 = f32[5,96,128]{2,1,0:T(8,128)S(1)} collective-permute-done((f32[5,96,128]{2,1,0:T(8,128)S(1)}, f32[5,96,128]{2,1,0:T(8,128)S(1)}, u32[]{:S(2)}, u32[]{:S(2)}) %collective-permute-start.18) | collective-permute-done | bytes 245792 | tf_op jit(solution)/shard_map/ppermute | solution.py:28
  75.5 2.2 %collective-permute-done.19 = f32[5,96,128]{2,1,0:T(8,128)S(1)} collective-permute-done((f32[5,96,128]{2,1,0:T(8,128)S(1)}, f32[5,96,128]{2,1,0:T(8,128)S(1)}, u32[]{:S(2)}, u32[]{:S(2)}) %collective-permute-start.19) | collective-permute-done | bytes 245792 | tf_op jit(solution)/shard_map/ppermute | solution.py:28
  77.8 1.5 collective-permute-done.21
  79.4 1.2 collective-permute-start.22
  81.1 2.7 %collective-permute-start.24 = (f32[5,192,128]{2,1,0:T(8,128)S(1)}, f32[5,192,128]{2,1,0:T(8,128)S(1)}, u32[]{:S(2)}, u32[]{:S(2)}) collective-permute-start(f32[5,192,128]{2,1,0:T(8,128)S(1)} %pad_maximum_fusion.4), channel_id=1, source_target_pairs={{0,3},{8,56},{1,0},{9,57},{2,1},{10,58},{3,2},{11,59},{4,7},{12,60... | collective-permute-start | bytes 1474568 | tf_op jit(solution)/shard_map/ppermute | solution.py:57
  83.8 1.1 collective-permute-start.25
  84.9 3.3 %collective-permute-done.22 = f32[5,192,128]{2,1,0:T(8,128)S(1)} collective-permute-done((f32[5,192,128]{2,1,0:T(8,128)S(1)}, f32[5,192,128]{2,1,0:T(8,128)S(1)}, u32[]{:S(2)}, u32[]{:S(2)}) %collective-permute-start.22) | collective-permute-done | bytes 491552 | tf_op jit(solution)/shard_map/ppermute | solution.py:57
  88.8 1.9 %collective-permute-done.23 = f32[5,192,128]{2,1,0:T(8,128)S(1)} collective-permute-done((f32[5,192,128]{2,1,0:T(8,128)S(1)}, f32[5,192,128]{2,1,0:T(8,128)S(1)}, u32[]{:S(2)}, u32[]{:S(2)}) %collective-permute-start.23) | collective-permute-done | bytes 491552 | tf_op jit(solution)/shard_map/ppermute | solution.py:57
  91.2 0.9 collective-permute-start.32
  92.0 1.2 collective-permute-start.31
  93.2 2.9 %collective-permute-start.30 = (f32[5,192,128]{2,1,0:T(8,128)S(1)}, f32[5,192,128]{2,1,0:T(8,128)S(1)}, u32[]{:S(2)}, u32[]{:S(2)}) collective-permute-start(f32[5,192,128]{2,1,0:T(8,128)S(1)} %collective-permute-done.22), channel_id=1, source_target_pairs={{0,2},{8,40},{1,3},{9,41},{2,0},{10,42},{3,1},{11,43},{4,6},{12,44... | collective-permute-start | bytes 1474568 | tf_op jit(solution)/shard_map/ppermute | solution.py:57
  96.7 2.9 %prepare.6 = (bf16[768,640]{1,0:T(8,128)(2,1)S(1)}, bf16[768,640]{1,0:T(8,128)(2,1)S(1)}, bf16[384,640]{1,0:T(8,128)(2,1)S(1)}, bf16[384,640]{1,0:T(8,128)(2,1)S(1)}, f32[384,640]{1,0:T(8,128)}) custom-call(s32[1,1]{1,0:T(1,128)} %bitcast.refs_0_, f32[960,128]{1,0:T(8,128)S(1)} %bitcast.94, f32[960,128]{1,0:T(8,128)S(1)} %bitcast.100, ...), custom_call_target="tpu_custom_call" | custom-call | tf_op jit(solution)/shard_map/prepare/pallas_call | solution.py:139
  100.0 0.9 collective-permute-start.36
  100.8 4.4 %collective-permute-done.31 = f32[5,192,128]{2,1,0:T(8,128)S(1)} collective-permute-done((f32[5,192,128]{2,1,0:T(8,128)S(1)}, f32[5,192,128]{2,1,0:T(8,128)S(1)}, u32[]{:S(2)}, u32[]{:S(2)}) %collective-permute-start.31) | collective-permute-done | bytes 491552 | tf_op jit(solution)/shard_map/ppermute | solution.py:57
  105.3 0.9 collective-permute-start.35
  106.1 2.7 %collective-permute-done.29 = f32[5,192,128]{2,1,0:T(8,128)S(1)} collective-permute-done((f32[5,192,128]{2,1,0:T(8,128)S(1)}, f32[5,192,128]{2,1,0:T(8,128)S(1)}, u32[]{:S(2)}, u32[]{:S(2)}) %collective-permute-start.29) | collective-permute-done | bytes 491552 | tf_op jit(solution)/shard_map/ppermute | solution.py:57
  108.9 1.7 %collective-permute-done.33 = f32[5,192,128]{2,1,0:T(8,128)S(1)} collective-permute-done((f32[5,192,128]{2,1,0:T(8,128)S(1)}, f32[5,192,128]{2,1,0:T(8,128)S(1)}, u32[]{:S(2)}, u32[]{:S(2)}) %collective-permute-start.33) | collective-permute-done | bytes 491552 | tf_op jit(solution)/shard_map/ppermute | solution.py:32
  110.7 3.1 %prepare.7 = (bf16[768,640]{1,0:T(8,128)(2,1)S(1)}, bf16[768,640]{1,0:T(8,128)(2,1)S(1)}, bf16[384,640]{1,0:T(8,128)(2,1)S(1)}, bf16[384,640]{1,0:T(8,128)(2,1)S(1)}, f32[384,640]{1,0:T(8,128)}) custom-call(s32[1,1]{1,0:T(1,128)} %bitcast.refs_0_, f32[960,128]{1,0:T(8,128)S(1)} %bitcast.105, f32[960,128]{1,0:T(8,128)S(1)} %bitcast.104, ...), custom_call_target="tpu_custom_call" | custom-call | tf_op jit(solution)/shard_map/prepare/pallas_call | solution.py:139
  113.8 12.8 %amplitude_tile.5 = (f32[960,128]{1,0:T(8,128)S(1)}, f32[960,128]{1,0:T(8,128)S(1)}, f32[960,128]{1,0:T(8,128)S(1)}, f32[960,128]{1,0:T(8,128)S(1)}, f32[8,128]{1,0:T(8,128)S(1)}) custom-call(bf16[768,640]{1,0:T(8,128)(2,1)S(1)} %get-tuple-element.61.refs_0_, bf16[768,640]{1,0:T(8,128)(2,1)S(1)} %get-tuple-element.71.refs_1_, ...), custom_call_target="tpu_custom_call" | custom-call | tf_op jit(solution)/shard_map/amplitude_tile/pallas_call | solution.py:277
  126.6 3.0 %collective-permute-start.37 = (f32[5,192,128]{2,1,0:T(8,128)S(1)}, f32[5,192,128]{2,1,0:T(8,128)S(1)}, u32[]{:S(2)}, u32[]{:S(2)}) collective-permute-start(f32[5,192,128]{2,1,0:T(8,128)S(1)} %bitcast.120), channel_id=1, source_target_pairs={{0,2},{1,3},{2,0},{3,1},{4,6},{5,7},{6,4},{7,5},{8,10},{9,11},{10,... | collective-permute-start | bytes 1474568 | tf_op jit(solution)/shard_map/ppermute | solution.py:28
  130.2 1.2 collective-permute-done.39
  131.4 2.0 %collective-permute-start.40 = (f32[8,128]{1,0:T(8,128)S(1)}, f32[8,128]{1,0:T(8,128)S(1)}, u32[]{:S(2)}, u32[]{:S(2)}) collective-permute-start(f32[8,128]{1,0:T(8,128)S(1)} %add.471), channel_id=1, source_target_pairs={{0,68},{1,69},{2,70},{3,71},{4,64},{5,65},{6,66},{7,67},{8,76},{9,... | collective-permute-start | bytes 12296 | tf_op jit(solution)/shard_map/ppermute | solution.py:44
  133.4 1.8 %collective-permute-start.41 = (f32[8,128]{1,0:T(8,128)S(1)}, f32[8,128]{1,0:T(8,128)S(1)}, u32[]{:S(2)}, u32[]{:S(2)}) collective-permute-start(f32[8,128]{1,0:T(8,128)S(1)} %add.471), channel_id=1, source_target_pairs={{0,6},{1,7},{2,4},{3,5},{4,2},{5,3},{6,0},{7,1},{8,14},{9,15},{10,... | collective-permute-start | bytes 12296 | tf_op jit(solution)/shard_map/ppermute | solution.py:44
  135.2 3.3 %collective-permute-start.42 = (f32[8,128]{1,0:T(8,128)S(1)}, f32[8,128]{1,0:T(8,128)S(1)}, u32[]{:S(2)}, u32[]{:S(2)}) collective-permute-start(f32[8,128]{1,0:T(8,128)S(1)} %add.471), channel_id=1, source_target_pairs={{0,66},{1,67},{2,64},{3,65},{4,70},{5,71},{6,68},{7,69},{8,74},{9,... | collective-permute-start | bytes 12296 | tf_op jit(solution)/shard_map/ppermute | solution.py:44
  138.5 3.5 %collective-permute-done.41 = f32[8,128]{1,0:T(8,128)S(1)} collective-permute-done((f32[8,128]{1,0:T(8,128)S(1)}, f32[8,128]{1,0:T(8,128)S(1)}, u32[]{:S(2)}, u32[]{:S(2)}) %collective-permute-start.41) | collective-permute-done | bytes 4128 | tf_op jit(solution)/shard_map/ppermute | solution.py:44
  142.0 2.3 %collective-permute-done.42 = f32[8,128]{1,0:T(8,128)S(1)} collective-permute-done((f32[8,128]{1,0:T(8,128)S(1)}, f32[8,128]{1,0:T(8,128)S(1)}, u32[]{:S(2)}, u32[]{:S(2)}) %collective-permute-start.42) | collective-permute-done | bytes 4128 | tf_op jit(solution)/shard_map/ppermute | solution.py:44
  144.3 1.2 collective-permute-start.43
  145.6 2.0 %collective-permute-start.44 = (f32[8,128]{1,0:T(8,128)S(1)}, f32[8,128]{1,0:T(8,128)S(1)}, u32[]{:S(2)}, u32[]{:S(2)}) collective-permute-start(f32[8,128]{1,0:T(8,128)S(1)} %add_add_fusion.1), channel_id=1, source_target_pairs={{0,48},{1,49},{2,50},{3,51},{4,52},{5,53},{6,54},{7,55},{8,56},{9,... | collective-permute-start | bytes 12296 | tf_op jit(solution)/shard_map/ppermute | solution.py:44
  147.6 1.5 collective-permute-start.45
  149.2 3.5 %collective-permute-done.45 = f32[8,128]{1,0:T(8,128)S(1)} collective-permute-done((f32[8,128]{1,0:T(8,128)S(1)}, f32[8,128]{1,0:T(8,128)S(1)}, u32[]{:S(2)}, u32[]{:S(2)}) %collective-permute-start.45) | collective-permute-done | bytes 4128 | tf_op jit(solution)/shard_map/ppermute | solution.py:44
  152.8 0.8 copy-done.14
  153.7 0.9 slice-done
  154.6 2.8 %collective-permute-start.46 = (f32[5,104,128]{2,1,0:T(8,128)S(1)}, f32[5,104,128]{2,1,0:T(8,128)S(1)}, u32[]{:S(2)}, u32[]{:S(2)}) collective-permute-start(f32[5,104,128]{2,1,0:T(8,128)S(1)} %get-tuple-element.94), channel_id=1, source_target_pairs={{0,3},{1,0},{2,1},{3,2},{4,7},{5,4},{6,5},{7,6},{8,11},{9,8},{10,9... | collective-permute-start | bytes 798728 | tf_op jit(solution)/shard_map/ppermute | solution.py:28
  158.0 3.4 %collective-permute-done.46 = f32[5,104,128]{2,1,0:T(8,128)S(1)} collective-permute-done((f32[5,104,128]{2,1,0:T(8,128)S(1)}, f32[5,104,128]{2,1,0:T(8,128)S(1)}, u32[]{:S(2)}, u32[]{:S(2)}) %collective-permute-start.46) | collective-permute-done | bytes 266272 | tf_op jit(solution)/shard_map/ppermute | solution.py:28
  161.4 3.7 %collective-permute-done.47 = f32[5,104,128]{2,1,0:T(8,128)S(1)} collective-permute-done((f32[5,104,128]{2,1,0:T(8,128)S(1)}, f32[5,104,128]{2,1,0:T(8,128)S(1)}, u32[]{:S(2)}, u32[]{:S(2)}) %collective-permute-start.47) | collective-permute-done | bytes 266272 | tf_op jit(solution)/shard_map/ppermute | solution.py:28
  165.8 0.9 copy.67
  (125 shorter events, 13.0 us)
Async XLA Ops:
  1.9 1.6 copy-start.12
  1.9 1.6 collective-permute-start
  3.5 9.5 %collective-permute-start.3 = (f32[5,192,128]{2,1,0:T(8,128)S(1)}, f32[5,192,128]{2,1,0:T(8,128)}, u32[]{:S(2)}, u32[]{:S(2)}) collective-permute-start(f32[5,192,128]{2,1,0:T(8,128)S(1)} %pad_maximum_fusion.3), channel_id=1, source_target_pairs={{0,3},{8,56},{1,0},{9,57},{2,1},{10,58},{3,2},{11,59},{4,7},{12,60... | collective-permute-start | bytes 1474568 | tf_op jit(solution)/shard_map/ppermute | solution.py:57
  6.7 10.1 %collective-permute-start.2 = (f32[5,192,128]{2,1,0:T(8,128)S(1)}, f32[5,192,128]{2,1,0:T(8,128)}, u32[]{:S(2)}, u32[]{:S(2)}) collective-permute-start(f32[5,192,128]{2,1,0:T(8,128)S(1)} %pad_maximum_fusion.3), channel_id=1, source_target_pairs={{0,1},{8,24},{1,2},{9,25},{2,3},{10,26},{3,0},{11,27},{4,5},{12,28... | collective-permute-start | bytes 1474568 | tf_op jit(solution)/shard_map/ppermute | solution.py:57
  6.7 12.8 %collective-permute-start.1 = (f32[5,192,128]{2,1,0:T(8,128)S(1)}, f32[5,192,128]{2,1,0:T(8,128)}, u32[]{:S(2)}, u32[]{:S(2)}) collective-permute-start(f32[5,192,128]{2,1,0:T(8,128)S(1)} %pad_maximum_fusion.3), channel_id=1, source_target_pairs={{0,4},{8,76},{1,5},{9,77},{2,6},{10,78},{3,7},{11,79},{4,0},{12,72... | collective-permute-start | bytes 1474568 | tf_op jit(solution)/shard_map/ppermute | solution.py:57
  8.6 12.8 %collective-permute-start.4 = (f32[5,192,128]{2,1,0:T(8,128)S(1)}, f32[5,192,128]{2,1,0:T(8,128)S(1)}, u32[]{:S(2)}, u32[]{:S(2)}) collective-permute-start(f32[5,192,128]{2,1,0:T(8,128)S(1)} %pad_maximum_fusion.3), channel_id=1, source_target_pairs={{0,8},{8,0},{1,9},{9,1},{2,10},{10,2},{3,11},{11,3},{4,12},{12,4},... | collective-permute-start | bytes 1474568 | tf_op jit(solution)/shard_map/ppermute | solution.py:32
  13.1 9.3 %collective-permute-start.7 = (f32[5,192,128]{2,1,0:T(8,128)}, f32[5,192,128]{2,1,0:T(8,128)S(1)}, u32[]{:S(2)}, u32[]{:S(2)}) collective-permute-start(f32[5,192,128]{2,1,0:T(8,128)} %collective-permute-done.3), channel_id=1, source_target_pairs={{0,8},{8,0},{1,9},{9,1},{2,10},{10,2},{3,11},{11,3},{4,12},{12,4},... | collective-permute-start | bytes 1474568 | tf_op jit(solution)/shard_map/ppermute | solution.py:32
  16.9 9.6 %collective-permute-start.6 = (f32[5,192,128]{2,1,0:T(8,128)}, f32[5,192,128]{2,1,0:T(8,128)S(1)}, u32[]{:S(2)}, u32[]{:S(2)}) collective-permute-start(f32[5,192,128]{2,1,0:T(8,128)} %collective-permute-done.2), channel_id=1, source_target_pairs={{0,8},{8,0},{1,9},{9,1},{2,10},{10,2},{3,11},{11,3},{4,12},{12,4},... | collective-permute-start | bytes 1474568 | tf_op jit(solution)/shard_map/ppermute | solution.py:32
  17.8 21.4 %collective-permute-start.8 = (f32[5,192,128]{2,1,0:T(8,128)S(1)}, f32[5,192,128]{2,1,0:T(8,128)}, u32[]{:S(2)}, u32[]{:S(2)}) collective-permute-start(f32[5,192,128]{2,1,0:T(8,128)S(1)} %pad_maximum_fusion.3), channel_id=1, source_target_pairs={{0,2},{8,40},{1,3},{9,41},{2,0},{10,42},{3,1},{11,43},{4,6},{12,44... | collective-permute-start | bytes 1474568 | tf_op jit(solution)/shard_map/ppermute | solution.py:57
  19.5 18.9 %collective-permute-start.11 = (f32[5,192,128]{2,1,0:T(8,128)}, f32[5,192,128]{2,1,0:T(8,128)}, u32[]{:S(2)}, u32[]{:S(2)}) collective-permute-start(f32[5,192,128]{2,1,0:T(8,128)} %collective-permute-done.3), channel_id=1, source_target_pairs={{0,4},{8,76},{1,5},{9,77},{2,6},{10,78},{3,7},{11,79},{4,0},{12,72... | collective-permute-start | bytes 1474568 | tf_op jit(solution)/shard_map/ppermute | solution.py:57
  21.4 0.8 copy-start
  22.2 16.4 %collective-permute-start.10 = (f32[5,192,128]{2,1,0:T(8,128)}, f32[5,192,128]{2,1,0:T(8,128)}, u32[]{:S(2)}, u32[]{:S(2)}) collective-permute-start(f32[5,192,128]{2,1,0:T(8,128)} %collective-permute-done.2), channel_id=1, source_target_pairs={{0,4},{8,76},{1,5},{9,77},{2,6},{10,78},{3,7},{11,79},{4,0},{12,72... | collective-permute-start | bytes 1474568 | tf_op jit(solution)/shard_map/ppermute | solution.py:57
  23.1 5.5 %collective-permute-start.5 = (f32[5,192,128]{2,1,0:T(8,128)}, f32[5,192,128]{2,1,0:T(8,128)S(1)}, u32[]{:S(2)}, u32[]{:S(2)}) collective-permute-start(f32[5,192,128]{2,1,0:T(8,128)} %collective-permute-done.1), channel_id=1, source_target_pairs={{0,8},{8,0},{1,9},{9,1},{2,10},{10,2},{3,11},{11,3},{4,12},{12,4},... | collective-permute-start | bytes 1474568 | tf_op jit(solution)/shard_map/ppermute | solution.py:32
  26.5 0.8 copy-start.4
  27.3 11.7 %collective-permute-start.9 = (f32[5,192,128]{2,1,0:T(8,128)}, f32[5,192,128]{2,1,0:T(8,128)}, u32[]{:S(2)}, u32[]{:S(2)}) collective-permute-start(f32[5,192,128]{2,1,0:T(8,128)} %collective-permute-done.1), channel_id=1, source_target_pairs={{0,2},{8,40},{1,3},{9,41},{2,0},{10,42},{3,1},{11,43},{4,6},{12,44... | collective-permute-start | bytes 1474568 | tf_op jit(solution)/shard_map/ppermute | solution.py:57
  28.7 0.8 copy-start.10
  29.5 1.0 copy-start.1
  30.5 1.0 copy-start.3
  31.5 1.0 copy-start.5
  32.6 1.0 copy-start.11
  37.6 0.8 copy-start.8
  38.4 2.2 %collective-permute-start.15 = (f32[5,192,128]{2,1,0:T(8,128)}, f32[5,192,128]{2,1,0:T(8,128)}, u32[]{:S(2)}, u32[]{:S(2)}) collective-permute-start(f32[5,192,128]{2,1,0:T(8,128)} %collective-permute-done.11), channel_id=1, source_target_pairs={{0,8},{8,0},{1,9},{9,1},{2,10},{10,2},{3,11},{11,3},{4,12},{12,4},... | collective-permute-start | bytes 1474568 | tf_op jit(solution)/shard_map/ppermute | solution.py:32
  38.7 2.7 %collective-permute-start.14 = (f32[5,192,128]{2,1,0:T(8,128)}, f32[5,192,128]{2,1,0:T(8,128)}, u32[]{:S(2)}, u32[]{:S(2)}) collective-permute-start(f32[5,192,128]{2,1,0:T(8,128)} %collective-permute-done.10), channel_id=1, source_target_pairs={{0,8},{8,0},{1,9},{9,1},{2,10},{10,2},{3,11},{11,3},{4,12},{12,4},... | collective-permute-start | bytes 1474568 | tf_op jit(solution)/shard_map/ppermute | solution.py:32
  39.0 3.8 %collective-permute-start.13 = (f32[5,192,128]{2,1,0:T(8,128)}, f32[5,192,128]{2,1,0:T(8,128)}, u32[]{:S(2)}, u32[]{:S(2)}) collective-permute-start(f32[5,192,128]{2,1,0:T(8,128)} %collective-permute-done.9), channel_id=1, source_target_pairs={{0,8},{8,0},{1,9},{9,1},{2,10},{10,2},{3,11},{11,3},{4,12},{12,4},... | collective-permute-start | bytes 1474568 | tf_op jit(solution)/shard_map/ppermute | solution.py:32
  39.2 3.6 %collective-permute-start.12 = (f32[5,192,128]{2,1,0:T(8,128)}, f32[5,192,128]{2,1,0:T(8,128)S(1)}, u32[]{:S(2)}, u32[]{:S(2)}) collective-permute-start(f32[5,192,128]{2,1,0:T(8,128)} %collective-permute-done.8), channel_id=1, source_target_pairs={{0,8},{8,0},{1,9},{9,1},{2,10},{10,2},{3,11},{11,3},{4,12},{12,4},... | collective-permute-start | bytes 1474568 | tf_op jit(solution)/shard_map/ppermute | solution.py:32
  46.7 11.9 %copy-start.7 = (bf16[384,640]{1,0:T(8,128)(2,1)S(1)}, bf16[384,640]{1,0:T(8,128)(2,1)}, u32[]{:S(2)}) copy-start(bf16[384,640]{1,0:T(8,128)(2,1)} %copy-done.6) | copy-start | bytes 1474564
  46.8 11.9 %copy-start.9 = (bf16[384,640]{1,0:T(8,128)(2,1)S(1)}, bf16[384,640]{1,0:T(8,128)(2,1)}, u32[]{:S(2)}) copy-start(bf16[384,640]{1,0:T(8,128)(2,1)} %copy-done.8) | copy-start | bytes 1474564
  54.6 13.4 %collective-permute-start.17 = (f32[5,192,128]{2,1,0:T(8,128)S(1)}, f32[5,192,128]{2,1,0:T(8,128)S(1)}, u32[]{:S(2)}, u32[]{:S(2)}) collective-permute-start(f32[5,192,128]{2,1,0:T(8,128)S(1)} %bitcast.122), channel_id=1, source_target_pairs={{0,4},{1,5},{2,6},{3,7},{4,0},{5,1},{6,2},{7,3},{8,12},{9,13},{10,... | collective-permute-start | bytes 1474568 | tf_op jit(solution)/shard_map/ppermute | solution.py:28
  55.2 15.1 %collective-permute-start.16 = (f32[5,192,128]{2,1,0:T(8,128)S(1)}, f32[5,192,128]{2,1,0:T(8,128)S(1)}, u32[]{:S(2)}, u32[]{:S(2)}) collective-permute-start(f32[5,192,128]{2,1,0:T(8,128)S(1)} %bitcast.121), channel_id=1, source_target_pairs={{0,2},{1,3},{2,0},{3,1},{4,6},{5,7},{6,4},{7,5},{8,10},{9,11},{10,... | collective-permute-start | bytes 1474568 | tf_op jit(solution)/shard_map/ppermute | solution.py:28
  68.1 7.3 %collective-permute-start.18 = (f32[5,96,128]{2,1,0:T(8,128)S(1)}, f32[5,96,128]{2,1,0:T(8,128)S(1)}, u32[]{:S(2)}, u32[]{:S(2)}) collective-permute-start(f32[5,96,128]{2,1,0:T(8,128)S(1)} %get-tuple-element.92), channel_id=1, source_target_pairs={{0,3},{1,0},{2,1},{3,2},{4,7},{5,4},{6,5},{7,6},{8,11},{9,8},{10,9... | collective-permute-start | bytes 737288 | tf_op jit(solution)/shard_map/ppermute | solution.py:28
  69.6 8.1 %collective-permute-start.19 = (f32[5,96,128]{2,1,0:T(8,128)S(1)}, f32[5,96,128]{2,1,0:T(8,128)S(1)}, u32[]{:S(2)}, u32[]{:S(2)}) collective-permute-start(f32[5,96,128]{2,1,0:T(8,128)S(1)} %get-tuple-element.93), channel_id=1, source_target_pairs={{0,1},{1,2},{2,3},{3,0},{4,5},{5,6},{6,7},{7,4},{8,9},{9,10},{10,1... | collective-permute-start | bytes 737288 | tf_op jit(solution)/shard_map/ppermute | solution.py:28
  70.3 7.4 %copy-start.13 = (f32[96,5,128]{2,0,1:T(8,128)S(1)}, f32[96,5,128]{2,0,1:T(8,128)}, u32[]{:S(2)}) copy-start(f32[96,5,128]{2,0,1:T(8,128)} %copy-done.12) | copy-start | bytes 737284
  70.3 7.3 %collective-permute-start.20 = (f32[5,96,128]{2,1,0:T(8,128)S(1)}, f32[5,96,128]{2,1,0:T(8,128)S(1)}, u32[]{:S(2)}, u32[]{:S(2)}) collective-permute-start(f32[5,96,128]{2,1,0:T(8,128)S(1)} %slice.83), channel_id=1, source_target_pairs={{0,4},{1,5},{2,6},{3,7},{4,0},{5,1},{6,2},{7,3},{8,12},{9,13},{10,... | collective-permute-start | bytes 737288 | tf_op jit(solution)/shard_map/ppermute | solution.py:28
  77.7 1.6 collective-permute-start.21
  79.4 8.9 %collective-permute-start.22 = (f32[5,192,128]{2,1,0:T(8,128)S(1)}, f32[5,192,128]{2,1,0:T(8,128)S(1)}, u32[]{:S(2)}, u32[]{:S(2)}) collective-permute-start(f32[5,192,128]{2,1,0:T(8,128)S(1)} %pad_maximum_fusion.4), channel_id=1, source_target_pairs={{0,4},{8,76},{1,5},{9,77},{2,6},{10,78},{3,7},{11,79},{4,0},{12,72... | collective-permute-start | bytes 1474568 | tf_op jit(solution)/shard_map/ppermute | solution.py:57
  80.6 10.0 %collective-permute-start.23 = (f32[5,192,128]{2,1,0:T(8,128)S(1)}, f32[5,192,128]{2,1,0:T(8,128)S(1)}, u32[]{:S(2)}, u32[]{:S(2)}) collective-permute-start(f32[5,192,128]{2,1,0:T(8,128)S(1)} %pad_maximum_fusion.4), channel_id=1, source_target_pairs={{0,1},{8,24},{1,2},{9,25},{2,3},{10,26},{3,0},{11,27},{4,5},{12,28... | collective-permute-start | bytes 1474568 | tf_op jit(solution)/shard_map/ppermute | solution.py:57
  81.1 10.0 %collective-permute-start.24 = (f32[5,192,128]{2,1,0:T(8,128)S(1)}, f32[5,192,128]{2,1,0:T(8,128)S(1)}, u32[]{:S(2)}, u32[]{:S(2)}) collective-permute-start(f32[5,192,128]{2,1,0:T(8,128)S(1)} %pad_maximum_fusion.4), channel_id=1, source_target_pairs={{0,3},{8,56},{1,0},{9,57},{2,1},{10,58},{3,2},{11,59},{4,7},{12,60... | collective-permute-start | bytes 1474568 | tf_op jit(solution)/shard_map/ppermute | solution.py:57
  83.8 8.2 %collective-permute-start.25 = (f32[5,192,128]{2,1,0:T(8,128)S(1)}, f32[5,192,128]{2,1,0:T(8,128)S(1)}, u32[]{:S(2)}, u32[]{:S(2)}) collective-permute-start(f32[5,192,128]{2,1,0:T(8,128)S(1)} %pad_maximum_fusion.4), channel_id=1, source_target_pairs={{0,8},{8,0},{1,9},{9,1},{2,10},{10,2},{3,11},{11,3},{4,12},{12,4},... | collective-permute-start | bytes 1474568 | tf_op jit(solution)/shard_map/ppermute | solution.py:32
  88.3 4.9 %collective-permute-start.26 = (f32[5,192,128]{2,1,0:T(8,128)S(1)}, f32[5,192,128]{2,1,0:T(8,128)S(1)}, u32[]{:S(2)}, u32[]{:S(2)}) collective-permute-start(f32[5,192,128]{2,1,0:T(8,128)S(1)} %collective-permute-done.22), channel_id=1, source_target_pairs={{0,8},{8,0},{1,9},{9,1},{2,10},{10,2},{3,11},{11,3},{4,12},{12,4},... | collective-permute-start | bytes 1474568 | tf_op jit(solution)/shard_map/ppermute | solution.py:32
  90.6 5.5 %collective-permute-start.27 = (f32[5,192,128]{2,1,0:T(8,128)S(1)}, f32[5,192,128]{2,1,0:T(8,128)S(1)}, u32[]{:S(2)}, u32[]{:S(2)}) collective-permute-start(f32[5,192,128]{2,1,0:T(8,128)S(1)} %collective-permute-done.23), channel_id=1, source_target_pairs={{0,8},{8,0},{1,9},{9,1},{2,10},{10,2},{3,11},{11,3},{4,12},{12,4},... | collective-permute-start | bytes 1474568 | tf_op jit(solution)/shard_map/ppermute | solution.py:32
  91.2 5.6 %collective-permute-start.28 = (f32[5,192,128]{2,1,0:T(8,128)S(1)}, f32[5,192,128]{2,1,0:T(8,128)S(1)}, u32[]{:S(2)}, u32[]{:S(2)}) collective-permute-start(f32[5,192,128]{2,1,0:T(8,128)S(1)} %collective-permute-done.24), channel_id=1, source_target_pairs={{0,8},{8,0},{1,9},{9,1},{2,10},{10,2},{3,11},{11,3},{4,12},{12,4},... | collective-permute-start | bytes 1474568 | tf_op jit(solution)/shard_map/ppermute | solution.py:32
  91.2 8.8 %collective-permute-start.32 = (f32[5,192,128]{2,1,0:T(8,128)S(1)}, f32[5,192,128]{2,1,0:T(8,128)S(1)}, u32[]{:S(2)}, u32[]{:S(2)}) collective-permute-start(f32[5,192,128]{2,1,0:T(8,128)S(1)} %collective-permute-done.24), channel_id=1, source_target_pairs={{0,4},{8,76},{1,5},{9,77},{2,6},{10,78},{3,7},{11,79},{4,0},{12,72... | collective-permute-start | bytes 1474568 | tf_op jit(solution)/shard_map/ppermute | solution.py:57
  92.0 13.2 %collective-permute-start.31 = (f32[5,192,128]{2,1,0:T(8,128)S(1)}, f32[5,192,128]{2,1,0:T(8,128)S(1)}, u32[]{:S(2)}, u32[]{:S(2)}) collective-permute-start(f32[5,192,128]{2,1,0:T(8,128)S(1)} %collective-permute-done.23), channel_id=1, source_target_pairs={{0,4},{8,76},{1,5},{9,77},{2,6},{10,78},{3,7},{11,79},{4,0},{12,72... | collective-permute-start | bytes 1474568 | tf_op jit(solution)/shard_map/ppermute | solution.py:57
  93.2 12.9 %collective-permute-start.30 = (f32[5,192,128]{2,1,0:T(8,128)S(1)}, f32[5,192,128]{2,1,0:T(8,128)S(1)}, u32[]{:S(2)}, u32[]{:S(2)}) collective-permute-start(f32[5,192,128]{2,1,0:T(8,128)S(1)} %collective-permute-done.22), channel_id=1, source_target_pairs={{0,2},{8,40},{1,3},{9,41},{2,0},{10,42},{3,1},{11,43},{4,6},{12,44... | collective-permute-start | bytes 1474568 | tf_op jit(solution)/shard_map/ppermute | solution.py:57
  96.1 12.7 %collective-permute-start.29 = (f32[5,192,128]{2,1,0:T(8,128)S(1)}, f32[5,192,128]{2,1,0:T(8,128)S(1)}, u32[]{:S(2)}, u32[]{:S(2)}) collective-permute-start(f32[5,192,128]{2,1,0:T(8,128)S(1)} %pad_maximum_fusion.4), channel_id=1, source_target_pairs={{0,2},{8,40},{1,3},{9,41},{2,0},{10,42},{3,1},{11,43},{4,6},{12,44... | collective-permute-start | bytes 1474568 | tf_op jit(solution)/shard_map/ppermute | solution.py:57
  100.0 8.9 %collective-permute-start.36 = (f32[5,192,128]{2,1,0:T(8,128)S(1)}, f32[5,192,128]{2,1,0:T(8,128)S(1)}, u32[]{:S(2)}, u32[]{:S(2)}) collective-permute-start(f32[5,192,128]{2,1,0:T(8,128)S(1)} %collective-permute-done.32), channel_id=1, source_target_pairs={{0,8},{8,0},{1,9},{9,1},{2,10},{10,2},{3,11},{11,3},{4,12},{12,4},... | collective-permute-start | bytes 1474568 | tf_op jit(solution)/shard_map/ppermute | solution.py:32
  105.3 3.7 %collective-permute-start.35 = (f32[5,192,128]{2,1,0:T(8,128)S(1)}, f32[5,192,128]{2,1,0:T(8,128)S(1)}, u32[]{:S(2)}, u32[]{:S(2)}) collective-permute-start(f32[5,192,128]{2,1,0:T(8,128)S(1)} %collective-permute-done.31), channel_id=1, source_target_pairs={{0,8},{8,0},{1,9},{9,1},{2,10},{10,2},{3,11},{11,3},{4,12},{12,4},... | collective-permute-start | bytes 1474568 | tf_op jit(solution)/shard_map/ppermute | solution.py:32
  106.1 2.8 %collective-permute-start.34 = (f32[5,192,128]{2,1,0:T(8,128)S(1)}, f32[5,192,128]{2,1,0:T(8,128)S(1)}, u32[]{:S(2)}, u32[]{:S(2)}) collective-permute-start(f32[5,192,128]{2,1,0:T(8,128)S(1)} %collective-permute-done.30), channel_id=1, source_target_pairs={{0,8},{8,0},{1,9},{9,1},{2,10},{10,2},{3,11},{11,3},{4,12},{12,4},... | collective-permute-start | bytes 1474568 | tf_op jit(solution)/shard_map/ppermute | solution.py:32
  108.8 1.9 %collective-permute-start.33 = (f32[5,192,128]{2,1,0:T(8,128)S(1)}, f32[5,192,128]{2,1,0:T(8,128)S(1)}, u32[]{:S(2)}, u32[]{:S(2)}) collective-permute-start(f32[5,192,128]{2,1,0:T(8,128)S(1)} %collective-permute-done.29), channel_id=1, source_target_pairs={{0,8},{8,0},{1,9},{9,1},{2,10},{10,2},{3,11},{11,3},{4,12},{12,4},... | collective-permute-start | bytes 1474568 | tf_op jit(solution)/shard_map/ppermute | solution.py:32
  126.6 26.1 %collective-permute-start.37 = (f32[5,192,128]{2,1,0:T(8,128)S(1)}, f32[5,192,128]{2,1,0:T(8,128)S(1)}, u32[]{:S(2)}, u32[]{:S(2)}) collective-permute-start(f32[5,192,128]{2,1,0:T(8,128)S(1)} %bitcast.120), channel_id=1, source_target_pairs={{0,2},{1,3},{2,0},{3,1},{4,6},{5,7},{6,4},{7,5},{8,10},{9,11},{10,... | collective-permute-start | bytes 1474568 | tf_op jit(solution)/shard_map/ppermute | solution.py:28
  129.6 24.0 %collective-permute-start.38 = (f32[5,192,128]{2,1,0:T(8,128)S(1)}, f32[5,192,128]{2,1,0:T(8,128)S(1)}, u32[]{:S(2)}, u32[]{:S(2)}) collective-permute-start(f32[5,192,128]{2,1,0:T(8,128)S(1)} %bitcast.119), channel_id=1, source_target_pairs={{0,4},{1,5},{2,6},{3,7},{4,0},{5,1},{6,2},{7,3},{8,12},{9,13},{10,... | collective-permute-start | bytes 1474568 | tf_op jit(solution)/shard_map/ppermute | solution.py:28
  130.2 1.2 collective-permute-start.39
  131.4 7.1 %collective-permute-start.40 = (f32[8,128]{1,0:T(8,128)S(1)}, f32[8,128]{1,0:T(8,128)S(1)}, u32[]{:S(2)}, u32[]{:S(2)}) collective-permute-start(f32[8,128]{1,0:T(8,128)S(1)} %add.471), channel_id=1, source_target_pairs={{0,68},{1,69},{2,70},{3,71},{4,64},{5,65},{6,66},{7,67},{8,76},{9,... | collective-permute-start | bytes 12296 | tf_op jit(solution)/shard_map/ppermute | solution.py:44
  133.4 8.6 %collective-permute-start.41 = (f32[8,128]{1,0:T(8,128)S(1)}, f32[8,128]{1,0:T(8,128)S(1)}, u32[]{:S(2)}, u32[]{:S(2)}) collective-permute-start(f32[8,128]{1,0:T(8,128)S(1)} %add.471), channel_id=1, source_target_pairs={{0,6},{1,7},{2,4},{3,5},{4,2},{5,3},{6,0},{7,1},{8,14},{9,15},{10,... | collective-permute-start | bytes 12296 | tf_op jit(solution)/shard_map/ppermute | solution.py:44
  135.2 9.1 %collective-permute-start.42 = (f32[8,128]{1,0:T(8,128)S(1)}, f32[8,128]{1,0:T(8,128)S(1)}, u32[]{:S(2)}, u32[]{:S(2)}) collective-permute-start(f32[8,128]{1,0:T(8,128)S(1)} %add.471), channel_id=1, source_target_pairs={{0,66},{1,67},{2,64},{3,65},{4,70},{5,71},{6,68},{7,69},{8,74},{9,... | collective-permute-start | bytes 12296 | tf_op jit(solution)/shard_map/ppermute | solution.py:44
  144.3 4.8 %collective-permute-start.43 = (f32[8,128]{1,0:T(8,128)S(1)}, f32[8,128]{1,0:T(8,128)S(1)}, u32[]{:S(2)}, u32[]{:S(2)}) collective-permute-start(f32[8,128]{1,0:T(8,128)S(1)} %add_add_fusion.1), channel_id=1, source_target_pairs={{0,16},{1,17},{2,18},{3,19},{4,20},{5,21},{6,22},{7,23},{8,24},{9,... | collective-permute-start | bytes 12296 | tf_op jit(solution)/shard_map/ppermute | solution.py:44
  145.6 3.6 %collective-permute-start.44 = (f32[8,128]{1,0:T(8,128)S(1)}, f32[8,128]{1,0:T(8,128)S(1)}, u32[]{:S(2)}, u32[]{:S(2)}) collective-permute-start(f32[8,128]{1,0:T(8,128)S(1)} %add_add_fusion.1), channel_id=1, source_target_pairs={{0,48},{1,49},{2,50},{3,51},{4,52},{5,53},{6,54},{7,55},{8,56},{9,... | collective-permute-start | bytes 12296 | tf_op jit(solution)/shard_map/ppermute | solution.py:44
  147.6 5.1 %collective-permute-start.45 = (f32[8,128]{1,0:T(8,128)S(1)}, f32[8,128]{1,0:T(8,128)S(1)}, u32[]{:S(2)}, u32[]{:S(2)}) collective-permute-start(f32[8,128]{1,0:T(8,128)S(1)} %add_add_fusion.1), channel_id=1, source_target_pairs={{0,32},{1,33},{2,34},{3,35},{4,36},{5,37},{6,38},{7,39},{8,40},{9,... | collective-permute-start | bytes 12296 | tf_op jit(solution)/shard_map/ppermute | solution.py:44
  152.8 0.8 copy-start.14
  153.6 0.9 slice-start
  154.6 11.0 %copy-start.15 = (f32[5,192,128]{2,1,0:T(8,128)S(1)}, f32[5,192,128]{2,1,0:T(8,128)}, u32[]{:S(2)}) copy-start(f32[5,192,128]{2,1,0:T(8,128)} %copy-done.14) | copy-start | bytes 1474564
  154.6 6.7 %collective-permute-start.46 = (f32[5,104,128]{2,1,0:T(8,128)S(1)}, f32[5,104,128]{2,1,0:T(8,128)S(1)}, u32[]{:S(2)}, u32[]{:S(2)}) collective-permute-start(f32[5,104,128]{2,1,0:T(8,128)S(1)} %get-tuple-element.94), channel_id=1, source_target_pairs={{0,3},{1,0},{2,1},{3,2},{4,7},{5,4},{6,5},{7,6},{8,11},{9,8},{10,9... | collective-permute-start | bytes 798728 | tf_op jit(solution)/shard_map/ppermute | solution.py:28
  157.4 7.6 %collective-permute-start.47 = (f32[5,104,128]{2,1,0:T(8,128)S(1)}, f32[5,104,128]{2,1,0:T(8,128)S(1)}, u32[]{:S(2)}, u32[]{:S(2)}) collective-permute-start(f32[5,104,128]{2,1,0:T(8,128)S(1)} %get-tuple-element.95), channel_id=1, source_target_pairs={{0,1},{1,2},{2,3},{3,0},{4,5},{5,6},{6,7},{7,4},{8,9},{9,10},{10,1... | collective-permute-start | bytes 798728 | tf_op jit(solution)/shard_map/ppermute | solution.py:28
  157.4 7.6 %collective-permute-start.48 = (f32[5,104,128]{2,1,0:T(8,128)S(1)}, f32[5,104,128]{2,1,0:T(8,128)S(1)}, u32[]{:S(2)}, u32[]{:S(2)}) collective-permute-start(f32[5,104,128]{2,1,0:T(8,128)S(1)} %get-tuple-element.96), channel_id=1, source_target_pairs={{0,4},{1,5},{2,6},{3,7},{4,0},{5,1},{6,2},{7,3},{8,12},{9,13},{10,... | collective-permute-start | bytes 798728 | tf_op jit(solution)/shard_map/ppermute | solution.py:28
  (4 other events, 2.9 us)

commit v2 on v1

--- a/solution.py
+++ b/solution.py
@@ -338,8 +338,8 @@
             lane = lax.broadcasted_iota(jnp.int32, (8, 128), 1)
             e = jnp.where(lane == 0, energies[0], energies[1])
             e = e + core_swap(e)
+            e = e + hop(e, 0, 1, 0, 0) + hop(e, 0, 3, 0, 0) + hop(e, 0, 2, 0, 0)
             e = e + hop(e, 1, 0, 1, 0) + hop(e, 0, 0, 1, 2) + hop(e, 1, 0, 0, 2)
-            e = e + hop(e, 0, 1, 0, 0) + hop(e, 0, 3, 0, 0) + hop(e, 0, 2, 0, 0)
             tail = jnp.broadcast_to(e[None], (TILES, 8, 128))
             to_left, to_right, to_partner = (
                 jnp.concatenate((v, tail), 1) for v in (to_left, to_right, to_partner)

time: 167 us -> 165 us (0.988)
  waiting for transfers between devices: 51.6 us -> 49.4 us
where the time goes in v2:
time: 165 us
  starting transfers between devices  55.6 us (34%)
  waiting for transfers between devices  49.4 us (30%)
  Pallas kernels  41.6 us (25%)
  local copies, waits for them, and re-layouts  16.4 us (10%)
    pallas_call x3, Pallas kernels, tile(): pl.pallas_call(functools.partial(tile_kernel, count, -1.0 / total), out_s...  28.5 us
    ppermute x14, waiting for transfers between devices, side_step(): return lax.ppermute(v, AXES, pairs)  19.4 us
    ppermute x14, starting transfers between devices, side_step(): return lax.ppermute(v, AXES, pairs)  18.8 us
    ppermute x10, starting transfers between devices, y_step(): return lax.ppermute(v, ('zl', 'y'), pairs)  15.3 us
    ppermute x10, waiting for transfers between devices, y_step(): return lax.ppermute(v, ('zl', 'y'), pairs)  13.6 us
    pallas_call x4, Pallas kernels, prepare(): pl.pallas_call(prepare_kernel, out_shape=(col, col, row, row, jax.ShapeDt...  13.1 us
    unnamed x38, local copies, waits for them, and re-layouts  12.9 us
    ppermute x6, starting transfers between devices, hop(): return lax.ppermute(v, AXES, pairs)  11.5 us
  transfers between devices with their start and end apart: 49, of which 23 were waited for; matrix products, arithmetic and copies ran while one was open for 1% of the time, Pallas kernels for 8%

profile of v2, /device:TPU:0, one launch (start us, length us, event | category | flops | bytes accessed | tf_op | source)
XLA Modules:
  0.0 165.0 jit_solution(1002348312213954136)
XLA Ops:
  0.6 1.1 copy.64
  2.0 1.5 collective-permute-done
  3.5 3.2 %collective-permute-start.3 = (f32[5,192,128]{2,1,0:T(8,128)S(1)}, f32[5,192,128]{2,1,0:T(8,128)}, u32[]{:S(2)}, u32[]{:S(2)}) collective-permute-start(f32[5,192,128]{2,1,0:T(8,128)S(1)} %pad_maximum_fusion.3), channel_id=1, source_target_pairs={{0,3},{8,56},{1,0},{9,57},{2,1},{10,58},{3,2},{11,59},{4,7},{12,60... | collective-permute-start | bytes 1474568 | tf_op jit(solution)/shard_map/ppermute | solution.py:57
  6.7 1.9 %collective-permute-start.1 = (f32[5,192,128]{2,1,0:T(8,128)S(1)}, f32[5,192,128]{2,1,0:T(8,128)}, u32[]{:S(2)}, u32[]{:S(2)}) collective-permute-start(f32[5,192,128]{2,1,0:T(8,128)S(1)} %pad_maximum_fusion.3), channel_id=1, source_target_pairs={{0,4},{8,76},{1,5},{9,77},{2,6},{10,78},{3,7},{11,79},{4,0},{12,72... | collective-permute-start | bytes 1474568 | tf_op jit(solution)/shard_map/ppermute | solution.py:57
  8.6 1.4 collective-permute-start.4
  10.1 3.0 %collective-permute-done.3 = f32[5,192,128]{2,1,0:T(8,128)} collective-permute-done((f32[5,192,128]{2,1,0:T(8,128)S(1)}, f32[5,192,128]{2,1,0:T(8,128)}, u32[]{:S(2)}, u32[]{:S(2)}) %collective-permute-start.3) | collective-permute-done | bytes 491552 | tf_op jit(solution)/shard_map/ppermute | solution.py:57
  13.1 3.8 %collective-permute-done.2 = f32[5,192,128]{2,1,0:T(8,128)} collective-permute-done((f32[5,192,128]{2,1,0:T(8,128)S(1)}, f32[5,192,128]{2,1,0:T(8,128)}, u32[]{:S(2)}, u32[]{:S(2)}) %collective-permute-start.2) | collective-permute-done | bytes 491552 | tf_op jit(solution)/shard_map/ppermute | solution.py:57
  17.8 1.7 %collective-permute-start.8 = (f32[5,192,128]{2,1,0:T(8,128)S(1)}, f32[5,192,128]{2,1,0:T(8,128)}, u32[]{:S(2)}, u32[]{:S(2)}) collective-permute-start(f32[5,192,128]{2,1,0:T(8,128)S(1)} %pad_maximum_fusion.3), channel_id=1, source_target_pairs={{0,2},{8,40},{1,3},{9,41},{2,0},{10,42},{3,1},{11,43},{4,6},{12,44... | collective-permute-start | bytes 1474568 | tf_op jit(solution)/shard_map/ppermute | solution.py:57
  19.5 1.9 %collective-permute-start.11 = (f32[5,192,128]{2,1,0:T(8,128)}, f32[5,192,128]{2,1,0:T(8,128)}, u32[]{:S(2)}, u32[]{:S(2)}) collective-permute-start(f32[5,192,128]{2,1,0:T(8,128)} %collective-permute-done.3), channel_id=1, source_target_pairs={{0,4},{8,76},{1,5},{9,77},{2,6},{10,78},{3,7},{11,79},{4,0},{12,72... | collective-permute-start | bytes 1474568 | tf_op jit(solution)/shard_map/ppermute | solution.py:57
  21.5 0.8 copy-done
  22.4 0.8 copy-done.2
  23.1 3.3 %collective-permute-start.5 = (f32[5,192,128]{2,1,0:T(8,128)}, f32[5,192,128]{2,1,0:T(8,128)S(1)}, u32[]{:S(2)}, u32[]{:S(2)}) collective-permute-start(f32[5,192,128]{2,1,0:T(8,128)} %collective-permute-done.1), channel_id=1, source_target_pairs={{0,8},{8,0},{1,9},{9,1},{2,10},{10,2},{3,11},{11,3},{4,12},{12,4},... | collective-permute-start | bytes 1474568 | tf_op jit(solution)/shard_map/ppermute | solution.py:32
  26.5 0.8 copy-done.4
  28.7 0.8 copy-done.10
  29.5 1.0 copy-done.1
  30.5 1.0 copy-done.3
  31.5 1.0 copy-done.5
  32.6 1.0 copy-done.11
  33.6 3.3 %prepare.4 = (bf16[768,640]{1,0:T(8,128)(2,1)S(1)}, bf16[768,640]{1,0:T(8,128)(2,1)S(1)}, bf16[384,640]{1,0:T(8,128)(2,1)S(1)}, bf16[384,640]{1,0:T(8,128)(2,1)S(1)}, f32[384,640]{1,0:T(8,128)S(1)}) custom-call(s32[1,1]{1,0:T(1,128)} %bitcast.refs_0_, f32[960,128]{1,0:T(8,128)S(1)} %bitcast.93, f32[960,128]{1,0:T(8,128)} %bitcast.4.refs_2_, ...), custom_call_target="tpu_custom_call" | custom-call | tf_op jit(solution)/shard_map/prepare/pallas_call | solution.py:139
  37.6 0.8 copy-done.8
  41.4 1.4 collective-permute-done.13
  42.8 3.9 %prepare.5 = (bf16[768,640]{1,0:T(8,128)(2,1)S(1)}, bf16[768,640]{1,0:T(8,128)(2,1)S(1)}, bf16[384,640]{1,0:T(8,128)(2,1)S(1)}, bf16[384,640]{1,0:T(8,128)(2,1)S(1)}, f32[384,640]{1,0:T(8,128)S(1)}) custom-call(s32[1,1]{1,0:T(1,128)} %bitcast.refs_0_, f32[960,128]{1,0:T(8,128)} %bitcast.11.refs_1_, f32[960,128]{1,0:T(8,128)} %bitcast.12.refs_2_, ...), custom_call_target="tpu_custom_call" | custom-call | tf_op jit(solution)/shard_map/prepare/pallas_call | solution.py:139
  46.8 7.9 %amplitude_tile.4 = (f32[960,128]{1,0:T(8,128)S(1)}, f32[960,128]{1,0:T(8,128)S(1)}, f32[8,128]{1,0:T(8,128)S(1)}) custom-call(bf16[768,640]{1,0:T(8,128)(2,1)S(1)} %get-tuple-element.42.refs_0_.refs_4_, bf16[768,640]{1,0:T(8,128)(2,1)S(1)} %get-tuple-element.52.refs_1_.refs_5_, bf16[768,640]{1,0:T(8,128)(2,1)S(1)} %get-tuple-element.44.refs_2_.refs_6_, ...), custom_call_target="tpu_custom_call" | custom-call | tf_op jit(solution)/shard_map/amplitude_tile/pallas_call | solution.py:277
  55.2 3.3 %collective-permute-start.16 = (f32[5,192,128]{2,1,0:T(8,128)S(1)}, f32[5,192,128]{2,1,0:T(8,128)S(1)}, u32[]{:S(2)}, u32[]{:S(2)}) collective-permute-start(f32[5,192,128]{2,1,0:T(8,128)S(1)} %bitcast.121), channel_id=1, source_target_pairs={{0,2},{1,3},{2,0},{3,1},{4,6},{5,7},{6,4},{7,5},{8,10},{9,11},{10,... | collective-permute-start | bytes 1474568 | tf_op jit(solution)/shard_map/ppermute | solution.py:28
  58.6 7.8 %amplitude_tile.3 = (f32[960,128]{1,0:T(8,128)S(1)}, f32[960,128]{1,0:T(8,128)S(1)}, f32[8,128]{1,0:T(8,128)S(1)}) custom-call(bf16[768,640]{1,0:T(8,128)(2,1)S(1)} %get-tuple-element.42.refs_0_.refs_4_, bf16[768,640]{1,0:T(8,128)(2,1)S(1)} %get-tuple-element.52.refs_1_.refs_5_, bf16[768,640]{1,0:T(8,128)(2,1)S(1)} %get-tuple-element.44.refs_2_.refs_6_, ...), custom_call_target="tpu_custom_call" | custom-call | tf_op jit(solution)/shard_map/amplitude_tile/pallas_call | solution.py:277
  66.5 1.6 collective-permute-done.17
  68.1 1.4 collective-permute-start.18
  70.3 1.4 collective-permute-start.20
  71.8 3.7 %collective-permute-done.18 = f32[5,96,128]{2,1,0:T(8,128)S(1)} collective-permute-done((f32[5,96,128]{2,1,0:T(8,128)S(1)}, f32[5,96,128]{2,1,0:T(8,128)S(1)}, u32[]{:S(2)}, u32[]{:S(2)}) %collective-permute-start.18) | collective-permute-done | bytes 245792 | tf_op jit(solution)/shard_map/ppermute | solution.py:28
  75.5 2.2 %collective-permute-done.19 = f32[5,96,128]{2,1,0:T(8,128)S(1)} collective-permute-done((f32[5,96,128]{2,1,0:T(8,128)S(1)}, f32[5,96,128]{2,1,0:T(8,128)S(1)}, u32[]{:S(2)}, u32[]{:S(2)}) %collective-permute-start.19) | collective-permute-done | bytes 245792 | tf_op jit(solution)/shard_map/ppermute | solution.py:28
  77.8 1.5 collective-permute-done.21
  79.4 1.2 collective-permute-start.22
  81.1 2.7 %collective-permute-start.24 = (f32[5,192,128]{2,1,0:T(8,128)S(1)}, f32[5,192,128]{2,1,0:T(8,128)S(1)}, u32[]{:S(2)}, u32[]{:S(2)}) collective-permute-start(f32[5,192,128]{2,1,0:T(8,128)S(1)} %pad_maximum_fusion.4), channel_id=1, source_target_pairs={{0,3},{8,56},{1,0},{9,57},{2,1},{10,58},{3,2},{11,59},{4,7},{12,60... | collective-permute-start | bytes 1474568 | tf_op jit(solution)/shard_map/ppermute | solution.py:57
  83.8 1.1 collective-permute-start.25
  84.9 3.3 %collective-permute-done.22 = f32[5,192,128]{2,1,0:T(8,128)S(1)} collective-permute-done((f32[5,192,128]{2,1,0:T(8,128)S(1)}, f32[5,192,128]{2,1,0:T(8,128)S(1)}, u32[]{:S(2)}, u32[]{:S(2)}) %collective-permute-start.22) | collective-permute-done | bytes 491552 | tf_op jit(solution)/shard_map/ppermute | solution.py:57
  88.8 1.9 %collective-permute-done.23 = f32[5,192,128]{2,1,0:T(8,128)S(1)} collective-permute-done((f32[5,192,128]{2,1,0:T(8,128)S(1)}, f32[5,192,128]{2,1,0:T(8,128)S(1)}, u32[]{:S(2)}, u32[]{:S(2)}) %collective-permute-start.23) | collective-permute-done | bytes 491552 | tf_op jit(solution)/shard_map/ppermute | solution.py:57
  91.2 0.9 collective-permute-start.32
  92.0 1.2 collective-permute-start.31
  93.2 2.9 %collective-permute-start.30 = (f32[5,192,128]{2,1,0:T(8,128)S(1)}, f32[5,192,128]{2,1,0:T(8,128)S(1)}, u32[]{:S(2)}, u32[]{:S(2)}) collective-permute-start(f32[5,192,128]{2,1,0:T(8,128)S(1)} %collective-permute-done.22), channel_id=1, source_target_pairs={{0,2},{8,40},{1,3},{9,41},{2,0},{10,42},{3,1},{11,43},{4,6},{12,44... | collective-permute-start | bytes 1474568 | tf_op jit(solution)/shard_map/ppermute | solution.py:57
  96.7 2.9 %prepare.6 = (bf16[768,640]{1,0:T(8,128)(2,1)S(1)}, bf16[768,640]{1,0:T(8,128)(2,1)S(1)}, bf16[384,640]{1,0:T(8,128)(2,1)S(1)}, bf16[384,640]{1,0:T(8,128)(2,1)S(1)}, f32[384,640]{1,0:T(8,128)}) custom-call(s32[1,1]{1,0:T(1,128)} %bitcast.refs_0_, f32[960,128]{1,0:T(8,128)S(1)} %bitcast.94, f32[960,128]{1,0:T(8,128)S(1)} %bitcast.100, ...), custom_call_target="tpu_custom_call" | custom-call | tf_op jit(solution)/shard_map/prepare/pallas_call | solution.py:139
  100.0 0.9 collective-permute-start.36
  100.8 4.4 %collective-permute-done.31 = f32[5,192,128]{2,1,0:T(8,128)S(1)} collective-permute-done((f32[5,192,128]{2,1,0:T(8,128)S(1)}, f32[5,192,128]{2,1,0:T(8,128)S(1)}, u32[]{:S(2)}, u32[]{:S(2)}) %collective-permute-start.31) | collective-permute-done | bytes 491552 | tf_op jit(solution)/shard_map/ppermute | solution.py:57
  105.3 0.9 collective-permute-start.35
  106.1 2.7 %collective-permute-done.29 = f32[5,192,128]{2,1,0:T(8,128)S(1)} collective-permute-done((f32[5,192,128]{2,1,0:T(8,128)S(1)}, f32[5,192,128]{2,1,0:T(8,128)S(1)}, u32[]{:S(2)}, u32[]{:S(2)}) %collective-permute-start.29) | collective-permute-done | bytes 491552 | tf_op jit(solution)/shard_map/ppermute | solution.py:57
  108.9 1.7 %collective-permute-done.33 = f32[5,192,128]{2,1,0:T(8,128)S(1)} collective-permute-done((f32[5,192,128]{2,1,0:T(8,128)S(1)}, f32[5,192,128]{2,1,0:T(8,128)S(1)}, u32[]{:S(2)}, u32[]{:S(2)}) %collective-permute-start.33) | collective-permute-done | bytes 491552 | tf_op jit(solution)/shard_map/ppermute | solution.py:32
  110.7 3.1 %prepare.7 = (bf16[768,640]{1,0:T(8,128)(2,1)S(1)}, bf16[768,640]{1,0:T(8,128)(2,1)S(1)}, bf16[384,640]{1,0:T(8,128)(2,1)S(1)}, bf16[384,640]{1,0:T(8,128)(2,1)S(1)}, f32[384,640]{1,0:T(8,128)}) custom-call(s32[1,1]{1,0:T(1,128)} %bitcast.refs_0_, f32[960,128]{1,0:T(8,128)S(1)} %bitcast.105, f32[960,128]{1,0:T(8,128)S(1)} %bitcast.104, ...), custom_call_target="tpu_custom_call" | custom-call | tf_op jit(solution)/shard_map/prepare/pallas_call | solution.py:139
  113.8 12.8 %amplitude_tile.5 = (f32[960,128]{1,0:T(8,128)S(1)}, f32[960,128]{1,0:T(8,128)S(1)}, f32[960,128]{1,0:T(8,128)S(1)}, f32[960,128]{1,0:T(8,128)S(1)}, f32[8,128]{1,0:T(8,128)S(1)}) custom-call(bf16[768,640]{1,0:T(8,128)(2,1)S(1)} %get-tuple-element.61.refs_0_, bf16[768,640]{1,0:T(8,128)(2,1)S(1)} %get-tuple-element.71.refs_1_, ...), custom_call_target="tpu_custom_call" | custom-call | tf_op jit(solution)/shard_map/amplitude_tile/pallas_call | solution.py:277
  126.6 3.0 %collective-permute-start.37 = (f32[5,192,128]{2,1,0:T(8,128)S(1)}, f32[5,192,128]{2,1,0:T(8,128)S(1)}, u32[]{:S(2)}, u32[]{:S(2)}) collective-permute-start(f32[5,192,128]{2,1,0:T(8,128)S(1)} %bitcast.120), channel_id=1, source_target_pairs={{0,2},{1,3},{2,0},{3,1},{4,6},{5,7},{6,4},{7,5},{8,10},{9,11},{10,... | collective-permute-start | bytes 1474568 | tf_op jit(solution)/shard_map/ppermute | solution.py:28
  130.2 1.2 collective-permute-done.39
  131.4 3.2 %collective-permute-start.41 = (f32[8,128]{1,0:T(8,128)S(1)}, f32[8,128]{1,0:T(8,128)S(1)}, u32[]{:S(2)}, u32[]{:S(2)}) collective-permute-start(f32[8,128]{1,0:T(8,128)S(1)} %add.471), channel_id=1, source_target_pairs={{0,48},{1,49},{2,50},{3,51},{4,52},{5,53},{6,54},{7,55},{8,56},{9,... | collective-permute-start | bytes 12296 | tf_op jit(solution)/shard_map/ppermute | solution.py:44
  134.6 1.2 collective-permute-start.42
  136.2 3.5 %collective-permute-done.42 = f32[8,128]{1,0:T(8,128)S(1)} collective-permute-done((f32[8,128]{1,0:T(8,128)S(1)}, f32[8,128]{1,0:T(8,128)S(1)}, u32[]{:S(2)}, u32[]{:S(2)}) %collective-permute-start.42) | collective-permute-done | bytes 4128 | tf_op jit(solution)/shard_map/ppermute | solution.py:44
  139.7 2.0 %collective-permute-start.43 = (f32[8,128]{1,0:T(8,128)S(1)}, f32[8,128]{1,0:T(8,128)S(1)}, u32[]{:S(2)}, u32[]{:S(2)}) collective-permute-start(f32[8,128]{1,0:T(8,128)S(1)} %add_add_fusion.1), channel_id=1, source_target_pairs={{0,68},{1,69},{2,70},{3,71},{4,64},{5,65},{6,66},{7,67},{8,76},{9,... | collective-permute-start | bytes 12296 | tf_op jit(solution)/shard_map/ppermute | solution.py:44
  141.8 1.8 %collective-permute-start.44 = (f32[8,128]{1,0:T(8,128)S(1)}, f32[8,128]{1,0:T(8,128)S(1)}, u32[]{:S(2)}, u32[]{:S(2)}) collective-permute-start(f32[8,128]{1,0:T(8,128)S(1)} %add_add_fusion.1), channel_id=1, source_target_pairs={{0,6},{1,7},{2,4},{3,5},{4,2},{5,3},{6,0},{7,1},{8,14},{9,15},{10,... | collective-permute-start | bytes 12296 | tf_op jit(solution)/shard_map/ppermute | solution.py:44
  143.6 3.3 %collective-permute-start.45 = (f32[8,128]{1,0:T(8,128)S(1)}, f32[8,128]{1,0:T(8,128)S(1)}, u32[]{:S(2)}, u32[]{:S(2)}) collective-permute-start(f32[8,128]{1,0:T(8,128)S(1)} %add_add_fusion.1), channel_id=1, source_target_pairs={{0,66},{1,67},{2,64},{3,65},{4,70},{5,71},{6,68},{7,69},{8,74},{9,... | collective-permute-start | bytes 12296 | tf_op jit(solution)/shard_map/ppermute | solution.py:44
  146.8 1.0 collective-permute-done.44
  147.8 3.3 %collective-permute-done.45 = f32[8,128]{1,0:T(8,128)S(1)} collective-permute-done((f32[8,128]{1,0:T(8,128)S(1)}, f32[8,128]{1,0:T(8,128)S(1)}, u32[]{:S(2)}, u32[]{:S(2)}) %collective-permute-start.45) | collective-permute-done | bytes 4128 | tf_op jit(solution)/shard_map/ppermute | solution.py:44
  151.1 0.8 copy-done.14
  152.1 0.9 slice-done
  153.0 2.8 %collective-permute-start.46 = (f32[5,104,128]{2,1,0:T(8,128)S(1)}, f32[5,104,128]{2,1,0:T(8,128)S(1)}, u32[]{:S(2)}, u32[]{:S(2)}) collective-permute-start(f32[5,104,128]{2,1,0:T(8,128)S(1)} %get-tuple-element.94), channel_id=1, source_target_pairs={{0,3},{1,0},{2,1},{3,2},{4,7},{5,4},{6,5},{7,6},{8,11},{9,8},{10,9... | collective-permute-start | bytes 798728 | tf_op jit(solution)/shard_map/ppermute | solution.py:28
  155.8 1.5 collective-permute-start.48
  157.3 2.4 %collective-permute-done.46 = f32[5,104,128]{2,1,0:T(8,128)S(1)} collective-permute-done((f32[5,104,128]{2,1,0:T(8,128)S(1)}, f32[5,104,128]{2,1,0:T(8,128)S(1)}, u32[]{:S(2)}, u32[]{:S(2)}) %collective-permute-start.46) | collective-permute-done | bytes 266272 | tf_op jit(solution)/shard_map/ppermute | solution.py:28
  159.7 3.7 %collective-permute-done.47 = f32[5,104,128]{2,1,0:T(8,128)S(1)} collective-permute-done((f32[5,104,128]{2,1,0:T(8,128)S(1)}, f32[5,104,128]{2,1,0:T(8,128)S(1)}, u32[]{:S(2)}, u32[]{:S(2)}) %collective-permute-start.47) | collective-permute-done | bytes 266272 | tf_op jit(solution)/shard_map/ppermute | solution.py:28
  164.2 0.9 copy.67
  (125 shorter events, 12.8 us)
Async XLA Ops:
  1.9 1.6 copy-start.12
  1.9 1.6 collective-permute-start
  3.5 9.5 %collective-permute-start.3 = (f32[5,192,128]{2,1,0:T(8,128)S(1)}, f32[5,192,128]{2,1,0:T(8,128)}, u32[]{:S(2)}, u32[]{:S(2)}) collective-permute-start(f32[5,192,128]{2,1,0:T(8,128)S(1)} %pad_maximum_fusion.3), channel_id=1, source_target_pairs={{0,3},{8,56},{1,0},{9,57},{2,1},{10,58},{3,2},{11,59},{4,7},{12,60... | collective-permute-start | bytes 1474568 | tf_op jit(solution)/shard_map/ppermute | solution.py:57
  6.7 10.1 %collective-permute-start.2 = (f32[5,192,128]{2,1,0:T(8,128)S(1)}, f32[5,192,128]{2,1,0:T(8,128)}, u32[]{:S(2)}, u32[]{:S(2)}) collective-permute-start(f32[5,192,128]{2,1,0:T(8,128)S(1)} %pad_maximum_fusion.3), channel_id=1, source_target_pairs={{0,1},{8,24},{1,2},{9,25},{2,3},{10,26},{3,0},{11,27},{4,5},{12,28... | collective-permute-start | bytes 1474568 | tf_op jit(solution)/shard_map/ppermute | solution.py:57
  6.7 12.8 %collective-permute-start.1 = (f32[5,192,128]{2,1,0:T(8,128)S(1)}, f32[5,192,128]{2,1,0:T(8,128)}, u32[]{:S(2)}, u32[]{:S(2)}) collective-permute-start(f32[5,192,128]{2,1,0:T(8,128)S(1)} %pad_maximum_fusion.3), channel_id=1, source_target_pairs={{0,4},{8,76},{1,5},{9,77},{2,6},{10,78},{3,7},{11,79},{4,0},{12,72... | collective-permute-start | bytes 1474568 | tf_op jit(solution)/shard_map/ppermute | solution.py:57
  8.6 12.8 %collective-permute-start.4 = (f32[5,192,128]{2,1,0:T(8,128)S(1)}, f32[5,192,128]{2,1,0:T(8,128)S(1)}, u32[]{:S(2)}, u32[]{:S(2)}) collective-permute-start(f32[5,192,128]{2,1,0:T(8,128)S(1)} %pad_maximum_fusion.3), channel_id=1, source_target_pairs={{0,8},{8,0},{1,9},{9,1},{2,10},{10,2},{3,11},{11,3},{4,12},{12,4},... | collective-permute-start | bytes 1474568 | tf_op jit(solution)/shard_map/ppermute | solution.py:32
  13.1 9.3 %collective-permute-start.7 = (f32[5,192,128]{2,1,0:T(8,128)}, f32[5,192,128]{2,1,0:T(8,128)S(1)}, u32[]{:S(2)}, u32[]{:S(2)}) collective-permute-start(f32[5,192,128]{2,1,0:T(8,128)} %collective-permute-done.3), channel_id=1, source_target_pairs={{0,8},{8,0},{1,9},{9,1},{2,10},{10,2},{3,11},{11,3},{4,12},{12,4},... | collective-permute-start | bytes 1474568 | tf_op jit(solution)/shard_map/ppermute | solution.py:32
  16.9 9.6 %collective-permute-start.6 = (f32[5,192,128]{2,1,0:T(8,128)}, f32[5,192,128]{2,1,0:T(8,128)S(1)}, u32[]{:S(2)}, u32[]{:S(2)}) collective-permute-start(f32[5,192,128]{2,1,0:T(8,128)} %collective-permute-done.2), channel_id=1, source_target_pairs={{0,8},{8,0},{1,9},{9,1},{2,10},{10,2},{3,11},{11,3},{4,12},{12,4},... | collective-permute-start | bytes 1474568 | tf_op jit(solution)/shard_map/ppermute | solution.py:32
  17.8 21.4 %collective-permute-start.8 = (f32[5,192,128]{2,1,0:T(8,128)S(1)}, f32[5,192,128]{2,1,0:T(8,128)}, u32[]{:S(2)}, u32[]{:S(2)}) collective-permute-start(f32[5,192,128]{2,1,0:T(8,128)S(1)} %pad_maximum_fusion.3), channel_id=1, source_target_pairs={{0,2},{8,40},{1,3},{9,41},{2,0},{10,42},{3,1},{11,43},{4,6},{12,44... | collective-permute-start | bytes 1474568 | tf_op jit(solution)/shard_map/ppermute | solution.py:57
  19.5 18.9 %collective-permute-start.11 = (f32[5,192,128]{2,1,0:T(8,128)}, f32[5,192,128]{2,1,0:T(8,128)}, u32[]{:S(2)}, u32[]{:S(2)}) collective-permute-start(f32[5,192,128]{2,1,0:T(8,128)} %collective-permute-done.3), channel_id=1, source_target_pairs={{0,4},{8,76},{1,5},{9,77},{2,6},{10,78},{3,7},{11,79},{4,0},{12,72... | collective-permute-start | bytes 1474568 | tf_op jit(solution)/shard_map/ppermute | solution.py:57
  21.4 0.8 copy-start
  22.2 16.4 %collective-permute-start.10 = (f32[5,192,128]{2,1,0:T(8,128)}, f32[5,192,128]{2,1,0:T(8,128)}, u32[]{:S(2)}, u32[]{:S(2)}) collective-permute-start(f32[5,192,128]{2,1,0:T(8,128)} %collective-permute-done.2), channel_id=1, source_target_pairs={{0,4},{8,76},{1,5},{9,77},{2,6},{10,78},{3,7},{11,79},{4,0},{12,72... | collective-permute-start | bytes 1474568 | tf_op jit(solution)/shard_map/ppermute | solution.py:57
  23.1 5.5 %collective-permute-start.5 = (f32[5,192,128]{2,1,0:T(8,128)}, f32[5,192,128]{2,1,0:T(8,128)S(1)}, u32[]{:S(2)}, u32[]{:S(2)}) collective-permute-start(f32[5,192,128]{2,1,0:T(8,128)} %collective-permute-done.1), channel_id=1, source_target_pairs={{0,8},{8,0},{1,9},{9,1},{2,10},{10,2},{3,11},{11,3},{4,12},{12,4},... | collective-permute-start | bytes 1474568 | tf_op jit(solution)/shard_map/ppermute | solution.py:32
  26.5 0.8 copy-start.4
  27.3 11.7 %collective-permute-start.9 = (f32[5,192,128]{2,1,0:T(8,128)}, f32[5,192,128]{2,1,0:T(8,128)}, u32[]{:S(2)}, u32[]{:S(2)}) collective-permute-start(f32[5,192,128]{2,1,0:T(8,128)} %collective-permute-done.1), channel_id=1, source_target_pairs={{0,2},{8,40},{1,3},{9,41},{2,0},{10,42},{3,1},{11,43},{4,6},{12,44... | collective-permute-start | bytes 1474568 | tf_op jit(solution)/shard_map/ppermute | solution.py:57
  28.7 0.8 copy-start.10
  29.5 1.0 copy-start.1
  30.5 1.0 copy-start.3
  31.5 1.0 copy-start.5
  32.6 1.0 copy-start.11
  37.6 0.8 copy-start.8
  38.4 2.2 %collective-permute-start.15 = (f32[5,192,128]{2,1,0:T(8,128)}, f32[5,192,128]{2,1,0:T(8,128)}, u32[]{:S(2)}, u32[]{:S(2)}) collective-permute-start(f32[5,192,128]{2,1,0:T(8,128)} %collective-permute-done.11), channel_id=1, source_target_pairs={{0,8},{8,0},{1,9},{9,1},{2,10},{10,2},{3,11},{11,3},{4,12},{12,4},... | collective-permute-start | bytes 1474568 | tf_op jit(solution)/shard_map/ppermute | solution.py:32
  38.7 2.7 %collective-permute-start.14 = (f32[5,192,128]{2,1,0:T(8,128)}, f32[5,192,128]{2,1,0:T(8,128)}, u32[]{:S(2)}, u32[]{:S(2)}) collective-permute-start(f32[5,192,128]{2,1,0:T(8,128)} %collective-permute-done.10), channel_id=1, source_target_pairs={{0,8},{8,0},{1,9},{9,1},{2,10},{10,2},{3,11},{11,3},{4,12},{12,4},... | collective-permute-start | bytes 1474568 | tf_op jit(solution)/shard_map/ppermute | solution.py:32
  39.0 3.8 %collective-permute-start.13 = (f32[5,192,128]{2,1,0:T(8,128)}, f32[5,192,128]{2,1,0:T(8,128)}, u32[]{:S(2)}, u32[]{:S(2)}) collective-permute-start(f32[5,192,128]{2,1,0:T(8,128)} %collective-permute-done.9), channel_id=1, source_target_pairs={{0,8},{8,0},{1,9},{9,1},{2,10},{10,2},{3,11},{11,3},{4,12},{12,4},... | collective-permute-start | bytes 1474568 | tf_op jit(solution)/shard_map/ppermute | solution.py:32
  39.2 3.6 %collective-permute-start.12 = (f32[5,192,128]{2,1,0:T(8,128)}, f32[5,192,128]{2,1,0:T(8,128)S(1)}, u32[]{:S(2)}, u32[]{:S(2)}) collective-permute-start(f32[5,192,128]{2,1,0:T(8,128)} %collective-permute-done.8), channel_id=1, source_target_pairs={{0,8},{8,0},{1,9},{9,1},{2,10},{10,2},{3,11},{11,3},{4,12},{12,4},... | collective-permute-start | bytes 1474568 | tf_op jit(solution)/shard_map/ppermute | solution.py:32
  46.7 11.9 %copy-start.7 = (bf16[384,640]{1,0:T(8,128)(2,1)S(1)}, bf16[384,640]{1,0:T(8,128)(2,1)}, u32[]{:S(2)}) copy-start(bf16[384,640]{1,0:T(8,128)(2,1)} %copy-done.6) | copy-start | bytes 1474564
  46.8 11.9 %copy-start.9 = (bf16[384,640]{1,0:T(8,128)(2,1)S(1)}, bf16[384,640]{1,0:T(8,128)(2,1)}, u32[]{:S(2)}) copy-start(bf16[384,640]{1,0:T(8,128)(2,1)} %copy-done.8) | copy-start | bytes 1474564
  54.6 13.4 %collective-permute-start.17 = (f32[5,192,128]{2,1,0:T(8,128)S(1)}, f32[5,192,128]{2,1,0:T(8,128)S(1)}, u32[]{:S(2)}, u32[]{:S(2)}) collective-permute-start(f32[5,192,128]{2,1,0:T(8,128)S(1)} %bitcast.122), channel_id=1, source_target_pairs={{0,4},{1,5},{2,6},{3,7},{4,0},{5,1},{6,2},{7,3},{8,12},{9,13},{10,... | collective-permute-start | bytes 1474568 | tf_op jit(solution)/shard_map/ppermute | solution.py:28
  55.2 15.1 %collective-permute-start.16 = (f32[5,192,128]{2,1,0:T(8,128)S(1)}, f32[5,192,128]{2,1,0:T(8,128)S(1)}, u32[]{:S(2)}, u32[]{:S(2)}) collective-permute-start(f32[5,192,128]{2,1,0:T(8,128)S(1)} %bitcast.121), channel_id=1, source_target_pairs={{0,2},{1,3},{2,0},{3,1},{4,6},{5,7},{6,4},{7,5},{8,10},{9,11},{10,... | collective-permute-start | bytes 1474568 | tf_op jit(solution)/shard_map/ppermute | solution.py:28
  68.1 7.3 %collective-permute-start.18 = (f32[5,96,128]{2,1,0:T(8,128)S(1)}, f32[5,96,128]{2,1,0:T(8,128)S(1)}, u32[]{:S(2)}, u32[]{:S(2)}) collective-permute-start(f32[5,96,128]{2,1,0:T(8,128)S(1)} %get-tuple-element.92), channel_id=1, source_target_pairs={{0,3},{1,0},{2,1},{3,2},{4,7},{5,4},{6,5},{7,6},{8,11},{9,8},{10,9... | collective-permute-start | bytes 737288 | tf_op jit(solution)/shard_map/ppermute | solution.py:28
  69.6 8.1 %collective-permute-start.19 = (f32[5,96,128]{2,1,0:T(8,128)S(1)}, f32[5,96,128]{2,1,0:T(8,128)S(1)}, u32[]{:S(2)}, u32[]{:S(2)}) collective-permute-start(f32[5,96,128]{2,1,0:T(8,128)S(1)} %get-tuple-element.93), channel_id=1, source_target_pairs={{0,1},{1,2},{2,3},{3,0},{4,5},{5,6},{6,7},{7,4},{8,9},{9,10},{10,1... | collective-permute-start | bytes 737288 | tf_op jit(solution)/shard_map/ppermute | solution.py:28
  70.3 7.4 %copy-start.13 = (f32[96,5,128]{2,0,1:T(8,128)S(1)}, f32[96,5,128]{2,0,1:T(8,128)}, u32[]{:S(2)}) copy-start(f32[96,5,128]{2,0,1:T(8,128)} %copy-done.12) | copy-start | bytes 737284
  70.3 7.3 %collective-permute-start.20 = (f32[5,96,128]{2,1,0:T(8,128)S(1)}, f32[5,96,128]{2,1,0:T(8,128)S(1)}, u32[]{:S(2)}, u32[]{:S(2)}) collective-permute-start(f32[5,96,128]{2,1,0:T(8,128)S(1)} %slice.83), channel_id=1, source_target_pairs={{0,4},{1,5},{2,6},{3,7},{4,0},{5,1},{6,2},{7,3},{8,12},{9,13},{10,... | collective-permute-start | bytes 737288 | tf_op jit(solution)/shard_map/ppermute | solution.py:28
  77.7 1.6 collective-permute-start.21
  79.4 8.9 %collective-permute-start.22 = (f32[5,192,128]{2,1,0:T(8,128)S(1)}, f32[5,192,128]{2,1,0:T(8,128)S(1)}, u32[]{:S(2)}, u32[]{:S(2)}) collective-permute-start(f32[5,192,128]{2,1,0:T(8,128)S(1)} %pad_maximum_fusion.4), channel_id=1, source_target_pairs={{0,4},{8,76},{1,5},{9,77},{2,6},{10,78},{3,7},{11,79},{4,0},{12,72... | collective-permute-start | bytes 1474568 | tf_op jit(solution)/shard_map/ppermute | solution.py:57
  80.6 10.0 %collective-permute-start.23 = (f32[5,192,128]{2,1,0:T(8,128)S(1)}, f32[5,192,128]{2,1,0:T(8,128)S(1)}, u32[]{:S(2)}, u32[]{:S(2)}) collective-permute-start(f32[5,192,128]{2,1,0:T(8,128)S(1)} %pad_maximum_fusion.4), channel_id=1, source_target_pairs={{0,1},{8,24},{1,2},{9,25},{2,3},{10,26},{3,0},{11,27},{4,5},{12,28... | collective-permute-start | bytes 1474568 | tf_op jit(solution)/shard_map/ppermute | solution.py:57
  81.1 10.0 %collective-permute-start.24 = (f32[5,192,128]{2,1,0:T(8,128)S(1)}, f32[5,192,128]{2,1,0:T(8,128)S(1)}, u32[]{:S(2)}, u32[]{:S(2)}) collective-permute-start(f32[5,192,128]{2,1,0:T(8,128)S(1)} %pad_maximum_fusion.4), channel_id=1, source_target_pairs={{0,3},{8,56},{1,0},{9,57},{2,1},{10,58},{3,2},{11,59},{4,7},{12,60... | collective-permute-start | bytes 1474568 | tf_op jit(solution)/shard_map/ppermute | solution.py:57
  83.8 8.2 %collective-permute-start.25 = (f32[5,192,128]{2,1,0:T(8,128)S(1)}, f32[5,192,128]{2,1,0:T(8,128)S(1)}, u32[]{:S(2)}, u32[]{:S(2)}) collective-permute-start(f32[5,192,128]{2,1,0:T(8,128)S(1)} %pad_maximum_fusion.4), channel_id=1, source_target_pairs={{0,8},{8,0},{1,9},{9,1},{2,10},{10,2},{3,11},{11,3},{4,12},{12,4},... | collective-permute-start | bytes 1474568 | tf_op jit(solution)/shard_map/ppermute | solution.py:32
  88.3 4.9 %collective-permute-start.26 = (f32[5,192,128]{2,1,0:T(8,128)S(1)}, f32[5,192,128]{2,1,0:T(8,128)S(1)}, u32[]{:S(2)}, u32[]{:S(2)}) collective-permute-start(f32[5,192,128]{2,1,0:T(8,128)S(1)} %collective-permute-done.22), channel_id=1, source_target_pairs={{0,8},{8,0},{1,9},{9,1},{2,10},{10,2},{3,11},{11,3},{4,12},{12,4},... | collective-permute-start | bytes 1474568 | tf_op jit(solution)/shard_map/ppermute | solution.py:32
  90.6 5.5 %collective-permute-start.27 = (f32[5,192,128]{2,1,0:T(8,128)S(1)}, f32[5,192,128]{2,1,0:T(8,128)S(1)}, u32[]{:S(2)}, u32[]{:S(2)}) collective-permute-start(f32[5,192,128]{2,1,0:T(8,128)S(1)} %collective-permute-done.23), channel_id=1, source_target_pairs={{0,8},{8,0},{1,9},{9,1},{2,10},{10,2},{3,11},{11,3},{4,12},{12,4},... | collective-permute-start | bytes 1474568 | tf_op jit(solution)/shard_map/ppermute | solution.py:32
  91.2 5.6 %collective-permute-start.28 = (f32[5,192,128]{2,1,0:T(8,128)S(1)}, f32[5,192,128]{2,1,0:T(8,128)S(1)}, u32[]{:S(2)}, u32[]{:S(2)}) collective-permute-start(f32[5,192,128]{2,1,0:T(8,128)S(1)} %collective-permute-done.24), channel_id=1, source_target_pairs={{0,8},{8,0},{1,9},{9,1},{2,10},{10,2},{3,11},{11,3},{4,12},{12,4},... | collective-permute-start | bytes 1474568 | tf_op jit(solution)/shard_map/ppermute | solution.py:32
  91.2 8.8 %collective-permute-start.32 = (f32[5,192,128]{2,1,0:T(8,128)S(1)}, f32[5,192,128]{2,1,0:T(8,128)S(1)}, u32[]{:S(2)}, u32[]{:S(2)}) collective-permute-start(f32[5,192,128]{2,1,0:T(8,128)S(1)} %collective-permute-done.24), channel_id=1, source_target_pairs={{0,4},{8,76},{1,5},{9,77},{2,6},{10,78},{3,7},{11,79},{4,0},{12,72... | collective-permute-start | bytes 1474568 | tf_op jit(solution)/shard_map/ppermute | solution.py:57
  92.0 13.2 %collective-permute-start.31 = (f32[5,192,128]{2,1,0:T(8,128)S(1)}, f32[5,192,128]{2,1,0:T(8,128)S(1)}, u32[]{:S(2)}, u32[]{:S(2)}) collective-permute-start(f32[5,192,128]{2,1,0:T(8,128)S(1)} %collective-permute-done.23), channel_id=1, source_target_pairs={{0,4},{8,76},{1,5},{9,77},{2,6},{10,78},{3,7},{11,79},{4,0},{12,72... | collective-permute-start | bytes 1474568 | tf_op jit(solution)/shard_map/ppermute | solution.py:57
  93.2 12.9 %collective-permute-start.30 = (f32[5,192,128]{2,1,0:T(8,128)S(1)}, f32[5,192,128]{2,1,0:T(8,128)S(1)}, u32[]{:S(2)}, u32[]{:S(2)}) collective-permute-start(f32[5,192,128]{2,1,0:T(8,128)S(1)} %collective-permute-done.22), channel_id=1, source_target_pairs={{0,2},{8,40},{1,3},{9,41},{2,0},{10,42},{3,1},{11,43},{4,6},{12,44... | collective-permute-start | bytes 1474568 | tf_op jit(solution)/shard_map/ppermute | solution.py:57
  96.1 12.7 %collective-permute-start.29 = (f32[5,192,128]{2,1,0:T(8,128)S(1)}, f32[5,192,128]{2,1,0:T(8,128)S(1)}, u32[]{:S(2)}, u32[]{:S(2)}) collective-permute-start(f32[5,192,128]{2,1,0:T(8,128)S(1)} %pad_maximum_fusion.4), channel_id=1, source_target_pairs={{0,2},{8,40},{1,3},{9,41},{2,0},{10,42},{3,1},{11,43},{4,6},{12,44... | collective-permute-start | bytes 1474568 | tf_op jit(solution)/shard_map/ppermute | solution.py:57
  100.0 8.9 %collective-permute-start.36 = (f32[5,192,128]{2,1,0:T(8,128)S(1)}, f32[5,192,128]{2,1,0:T(8,128)S(1)}, u32[]{:S(2)}, u32[]{:S(2)}) collective-permute-start(f32[5,192,128]{2,1,0:T(8,128)S(1)} %collective-permute-done.32), channel_id=1, source_target_pairs={{0,8},{8,0},{1,9},{9,1},{2,10},{10,2},{3,11},{11,3},{4,12},{12,4},... | collective-permute-start | bytes 1474568 | tf_op jit(solution)/shard_map/ppermute | solution.py:32
  105.3 3.7 %collective-permute-start.35 = (f32[5,192,128]{2,1,0:T(8,128)S(1)}, f32[5,192,128]{2,1,0:T(8,128)S(1)}, u32[]{:S(2)}, u32[]{:S(2)}) collective-permute-start(f32[5,192,128]{2,1,0:T(8,128)S(1)} %collective-permute-done.31), channel_id=1, source_target_pairs={{0,8},{8,0},{1,9},{9,1},{2,10},{10,2},{3,11},{11,3},{4,12},{12,4},... | collective-permute-start | bytes 1474568 | tf_op jit(solution)/shard_map/ppermute | solution.py:32
  106.1 2.8 %collective-permute-start.34 = (f32[5,192,128]{2,1,0:T(8,128)S(1)}, f32[5,192,128]{2,1,0:T(8,128)S(1)}, u32[]{:S(2)}, u32[]{:S(2)}) collective-permute-start(f32[5,192,128]{2,1,0:T(8,128)S(1)} %collective-permute-done.30), channel_id=1, source_target_pairs={{0,8},{8,0},{1,9},{9,1},{2,10},{10,2},{3,11},{11,3},{4,12},{12,4},... | collective-permute-start | bytes 1474568 | tf_op jit(solution)/shard_map/ppermute | solution.py:32
  108.8 1.9 %collective-permute-start.33 = (f32[5,192,128]{2,1,0:T(8,128)S(1)}, f32[5,192,128]{2,1,0:T(8,128)S(1)}, u32[]{:S(2)}, u32[]{:S(2)}) collective-permute-start(f32[5,192,128]{2,1,0:T(8,128)S(1)} %collective-permute-done.29), channel_id=1, source_target_pairs={{0,8},{8,0},{1,9},{9,1},{2,10},{10,2},{3,11},{11,3},{4,12},{12,4},... | collective-permute-start | bytes 1474568 | tf_op jit(solution)/shard_map/ppermute | solution.py:32
  126.6 24.5 %collective-permute-start.37 = (f32[5,192,128]{2,1,0:T(8,128)S(1)}, f32[5,192,128]{2,1,0:T(8,128)S(1)}, u32[]{:S(2)}, u32[]{:S(2)}) collective-permute-start(f32[5,192,128]{2,1,0:T(8,128)S(1)} %bitcast.120), channel_id=1, source_target_pairs={{0,2},{1,3},{2,0},{3,1},{4,6},{5,7},{6,4},{7,5},{8,10},{9,11},{10,... | collective-permute-start | bytes 1474568 | tf_op jit(solution)/shard_map/ppermute | solution.py:28
  129.6 22.3 %collective-permute-start.38 = (f32[5,192,128]{2,1,0:T(8,128)S(1)}, f32[5,192,128]{2,1,0:T(8,128)S(1)}, u32[]{:S(2)}, u32[]{:S(2)}) collective-permute-start(f32[5,192,128]{2,1,0:T(8,128)S(1)} %bitcast.119), channel_id=1, source_target_pairs={{0,4},{1,5},{2,6},{3,7},{4,0},{5,1},{6,2},{7,3},{8,12},{9,13},{10,... | collective-permute-start | bytes 1474568 | tf_op jit(solution)/shard_map/ppermute | solution.py:28
  130.2 1.2 collective-permute-start.39
  131.4 4.8 %collective-permute-start.40 = (f32[8,128]{1,0:T(8,128)S(1)}, f32[8,128]{1,0:T(8,128)S(1)}, u32[]{:S(2)}, u32[]{:S(2)}) collective-permute-start(f32[8,128]{1,0:T(8,128)S(1)} %add.471), channel_id=1, source_target_pairs={{0,16},{1,17},{2,18},{3,19},{4,20},{5,21},{6,22},{7,23},{8,24},{9,... | collective-permute-start | bytes 12296 | tf_op jit(solution)/shard_map/ppermute | solution.py:44
  131.4 4.8 %collective-permute-start.41 = (f32[8,128]{1,0:T(8,128)S(1)}, f32[8,128]{1,0:T(8,128)S(1)}, u32[]{:S(2)}, u32[]{:S(2)}) collective-permute-start(f32[8,128]{1,0:T(8,128)S(1)} %add.471), channel_id=1, source_target_pairs={{0,48},{1,49},{2,50},{3,51},{4,52},{5,53},{6,54},{7,55},{8,56},{9,... | collective-permute-start | bytes 12296 | tf_op jit(solution)/shard_map/ppermute | solution.py:44
  134.6 5.1 %collective-permute-start.42 = (f32[8,128]{1,0:T(8,128)S(1)}, f32[8,128]{1,0:T(8,128)S(1)}, u32[]{:S(2)}, u32[]{:S(2)}) collective-permute-start(f32[8,128]{1,0:T(8,128)S(1)} %add.471), channel_id=1, source_target_pairs={{0,32},{1,33},{2,34},{3,35},{4,36},{5,37},{6,38},{7,39},{8,40},{9,... | collective-permute-start | bytes 12296 | tf_op jit(solution)/shard_map/ppermute | solution.py:44
  139.7 7.1 %collective-permute-start.43 = (f32[8,128]{1,0:T(8,128)S(1)}, f32[8,128]{1,0:T(8,128)S(1)}, u32[]{:S(2)}, u32[]{:S(2)}) collective-permute-start(f32[8,128]{1,0:T(8,128)S(1)} %add_add_fusion.1), channel_id=1, source_target_pairs={{0,68},{1,69},{2,70},{3,71},{4,64},{5,65},{6,66},{7,67},{8,76},{9,... | collective-permute-start | bytes 12296 | tf_op jit(solution)/shard_map/ppermute | solution.py:44
  141.8 6.0 %collective-permute-start.44 = (f32[8,128]{1,0:T(8,128)S(1)}, f32[8,128]{1,0:T(8,128)S(1)}, u32[]{:S(2)}, u32[]{:S(2)}) collective-permute-start(f32[8,128]{1,0:T(8,128)S(1)} %add_add_fusion.1), channel_id=1, source_target_pairs={{0,6},{1,7},{2,4},{3,5},{4,2},{5,3},{6,0},{7,1},{8,14},{9,15},{10,... | collective-permute-start | bytes 12296 | tf_op jit(solution)/shard_map/ppermute | solution.py:44
  143.6 7.5 %collective-permute-start.45 = (f32[8,128]{1,0:T(8,128)S(1)}, f32[8,128]{1,0:T(8,128)S(1)}, u32[]{:S(2)}, u32[]{:S(2)}) collective-permute-start(f32[8,128]{1,0:T(8,128)S(1)} %add_add_fusion.1), channel_id=1, source_target_pairs={{0,66},{1,67},{2,64},{3,65},{4,70},{5,71},{6,68},{7,69},{8,74},{9,... | collective-permute-start | bytes 12296 | tf_op jit(solution)/shard_map/ppermute | solution.py:44
  151.1 0.8 copy-start.14
  152.0 0.9 slice-start
  152.9 11.0 %copy-start.15 = (f32[5,192,128]{2,1,0:T(8,128)S(1)}, f32[5,192,128]{2,1,0:T(8,128)}, u32[]{:S(2)}) copy-start(f32[5,192,128]{2,1,0:T(8,128)} %copy-done.14) | copy-start | bytes 1474564
  153.0 6.7 %collective-permute-start.46 = (f32[5,104,128]{2,1,0:T(8,128)S(1)}, f32[5,104,128]{2,1,0:T(8,128)S(1)}, u32[]{:S(2)}, u32[]{:S(2)}) collective-permute-start(f32[5,104,128]{2,1,0:T(8,128)S(1)} %get-tuple-element.94), channel_id=1, source_target_pairs={{0,3},{1,0},{2,1},{3,2},{4,7},{5,4},{6,5},{7,6},{8,11},{9,8},{10,9... | collective-permute-start | bytes 798728 | tf_op jit(solution)/shard_map/ppermute | solution.py:28
  155.8 7.6 %collective-permute-start.47 = (f32[5,104,128]{2,1,0:T(8,128)S(1)}, f32[5,104,128]{2,1,0:T(8,128)S(1)}, u32[]{:S(2)}, u32[]{:S(2)}) collective-permute-start(f32[5,104,128]{2,1,0:T(8,128)S(1)} %get-tuple-element.95), channel_id=1, source_target_pairs={{0,1},{1,2},{2,3},{3,0},{4,5},{5,6},{6,7},{7,4},{8,9},{9,10},{10,1... | collective-permute-start | bytes 798728 | tf_op jit(solution)/shard_map/ppermute | solution.py:28
  155.8 7.6 %collective-permute-start.48 = (f32[5,104,128]{2,1,0:T(8,128)S(1)}, f32[5,104,128]{2,1,0:T(8,128)S(1)}, u32[]{:S(2)}, u32[]{:S(2)}) collective-permute-start(f32[5,104,128]{2,1,0:T(8,128)S(1)} %get-tuple-element.96), channel_id=1, source_target_pairs={{0,4},{1,5},{2,6},{3,7},{4,0},{5,1},{6,2},{7,3},{8,12},{9,13},{10,... | collective-permute-start | bytes 798728 | tf_op jit(solution)/shard_map/ppermute | solution.py:28
  (4 other events, 2.9 us)

commit v3 on v2

--- a/solution.py
+++ b/solution.py
@@ -337,7 +337,6 @@
         if step == ITERS - 1:
             lane = lax.broadcasted_iota(jnp.int32, (8, 128), 1)
             e = jnp.where(lane == 0, energies[0], energies[1])
-            e = e + core_swap(e)
             e = e + hop(e, 0, 1, 0, 0) + hop(e, 0, 3, 0, 0) + hop(e, 0, 2, 0, 0)
             e = e + hop(e, 1, 0, 1, 0) + hop(e, 0, 0, 1, 2) + hop(e, 1, 0, 0, 2)
             tail = jnp.broadcast_to(e[None], (TILES, 8, 128))
@@ -351,6 +350,7 @@
         factor = chol + work
 
     e = e + a[0, half:] + b[0, half:] + p[0, half:]
+    e = e + core_swap(e)
     work = jnp.transpose(work, (1, 0, 2)).reshape(half, -1)
     return (work, e[0, :2] / jnp.float32(total))
 

time: 165 us -> 166 us (level); the launches traced: 165 us -> 164 us
  transfers between devices with their start and end apart: 49 -> 49, of which waited for: 23 -> 23; matrix products, arithmetic and copies ran while one was open for 1% -> 2% of each run, Pallas kernels for 8% -> 9%
where the time goes in v3:
time: 166 us; the launch traced here: 164 us
  starting transfers between devices  55.7 us (34%)
  waiting for transfers between devices  48.3 us (29%)
  Pallas kernels  41.6 us (25%)
  local copies, waits for them, and re-layouts  16.4 us (10%)
    pallas_call x3, Pallas kernels, tile(): pl.pallas_call(functools.partial(tile_kernel, count, -1.0 / total), out_s...  28.5 us
    ppermute x14, waiting for transfers between devices, side_step(): return lax.ppermute(v, AXES, pairs)  19.4 us
    ppermute x14, starting transfers between devices, side_step(): return lax.ppermute(v, AXES, pairs)  18.8 us
    ppermute x10, starting transfers between devices, y_step(): return lax.ppermute(v, ('zl', 'y'), pairs)  15.3 us
    ppermute x10, waiting for transfers between devices, y_step(): return lax.ppermute(v, ('zl', 'y'), pairs)  13.6 us
    pallas_call x4, Pallas kernels, prepare(): pl.pallas_call(prepare_kernel, out_shape=(col, col, row, row, jax.ShapeDt...  13.1 us
    unnamed x38, local copies, waits for them, and re-layouts  12.9 us
    ppermute x6, starting transfers between devices, hop(): return lax.ppermute(v, AXES, pairs)  11.5 us
  transfers between devices with their start and end apart: 49, of which 23 were waited for; matrix products, arithmetic and copies ran while one was open for 2% of the time, Pallas kernels for 9%

profile of v3, /device:TPU:0, one launch (start us, length us, event | category | flops | bytes accessed | tf_op | source)
XLA Modules:
  0.0 164.0 jit_solution(6718260845769545874)
XLA Ops:
  0.6 1.1 copy.64
  2.0 1.5 collective-permute-done
  3.5 3.2 %collective-permute-start.3 = (f32[5,192,128]{2,1,0:T(8,128)S(1)}, f32[5,192,128]{2,1,0:T(8,128)}, u32[]{:S(2)}, u32[]{:S(2)}) collective-permute-start(f32[5,192,128]{2,1,0:T(8,128)S(1)} %pad_maximum_fusion.3), channel_id=1, source_target_pairs={{0,3},{8,56},{1,0},{9,57},{2,1},{10,58},{3,2},{11,59},{4,7},{12,60... | collective-permute-start | bytes 1474568 | tf_op jit(solution)/shard_map/ppermute | solution.py:57
  6.7 1.9 %collective-permute-start.1 = (f32[5,192,128]{2,1,0:T(8,128)S(1)}, f32[5,192,128]{2,1,0:T(8,128)}, u32[]{:S(2)}, u32[]{:S(2)}) collective-permute-start(f32[5,192,128]{2,1,0:T(8,128)S(1)} %pad_maximum_fusion.3), channel_id=1, source_target_pairs={{0,4},{8,76},{1,5},{9,77},{2,6},{10,78},{3,7},{11,79},{4,0},{12,72... | collective-permute-start | bytes 1474568 | tf_op jit(solution)/shard_map/ppermute | solution.py:57
  8.6 1.4 collective-permute-start.4
  10.1 3.0 %collective-permute-done.3 = f32[5,192,128]{2,1,0:T(8,128)} collective-permute-done((f32[5,192,128]{2,1,0:T(8,128)S(1)}, f32[5,192,128]{2,1,0:T(8,128)}, u32[]{:S(2)}, u32[]{:S(2)}) %collective-permute-start.3) | collective-permute-done | bytes 491552 | tf_op jit(solution)/shard_map/ppermute | solution.py:57
  13.1 3.8 %collective-permute-done.2 = f32[5,192,128]{2,1,0:T(8,128)} collective-permute-done((f32[5,192,128]{2,1,0:T(8,128)S(1)}, f32[5,192,128]{2,1,0:T(8,128)}, u32[]{:S(2)}, u32[]{:S(2)}) %collective-permute-start.2) | collective-permute-done | bytes 491552 | tf_op jit(solution)/shard_map/ppermute | solution.py:57
  17.8 1.7 %collective-permute-start.8 = (f32[5,192,128]{2,1,0:T(8,128)S(1)}, f32[5,192,128]{2,1,0:T(8,128)}, u32[]{:S(2)}, u32[]{:S(2)}) collective-permute-start(f32[5,192,128]{2,1,0:T(8,128)S(1)} %pad_maximum_fusion.3), channel_id=1, source_target_pairs={{0,2},{8,40},{1,3},{9,41},{2,0},{10,42},{3,1},{11,43},{4,6},{12,44... | collective-permute-start | bytes 1474568 | tf_op jit(solution)/shard_map/ppermute | solution.py:57
  19.5 1.9 %collective-permute-start.11 = (f32[5,192,128]{2,1,0:T(8,128)}, f32[5,192,128]{2,1,0:T(8,128)}, u32[]{:S(2)}, u32[]{:S(2)}) collective-permute-start(f32[5,192,128]{2,1,0:T(8,128)} %collective-permute-done.3), channel_id=1, source_target_pairs={{0,4},{8,76},{1,5},{9,77},{2,6},{10,78},{3,7},{11,79},{4,0},{12,72... | collective-permute-start | bytes 1474568 | tf_op jit(solution)/shard_map/ppermute | solution.py:57
  21.5 0.8 copy-done
  22.4 0.8 copy-done.2
  23.1 3.3 %collective-permute-start.5 = (f32[5,192,128]{2,1,0:T(8,128)}, f32[5,192,128]{2,1,0:T(8,128)S(1)}, u32[]{:S(2)}, u32[]{:S(2)}) collective-permute-start(f32[5,192,128]{2,1,0:T(8,128)} %collective-permute-done.1), channel_id=1, source_target_pairs={{0,8},{8,0},{1,9},{9,1},{2,10},{10,2},{3,11},{11,3},{4,12},{12,4},... | collective-permute-start | bytes 1474568 | tf_op jit(solution)/shard_map/ppermute | solution.py:32
  26.5 0.8 copy-done.4
  28.7 0.8 copy-done.10
  29.5 1.0 copy-done.1
  30.5 1.0 copy-done.3
  31.5 1.0 copy-done.5
  32.6 1.0 copy-done.11
  33.6 3.3 %prepare.4 = (bf16[768,640]{1,0:T(8,128)(2,1)S(1)}, bf16[768,640]{1,0:T(8,128)(2,1)S(1)}, bf16[384,640]{1,0:T(8,128)(2,1)S(1)}, bf16[384,640]{1,0:T(8,128)(2,1)S(1)}, f32[384,640]{1,0:T(8,128)S(1)}) custom-call(s32[1,1]{1,0:T(1,128)} %bitcast.refs_0_, f32[960,128]{1,0:T(8,128)S(1)} %bitcast.93, f32[960,128]{1,0:T(8,128)} %bitcast.4.refs_2_, ...), custom_call_target="tpu_custom_call" | custom-call | tf_op jit(solution)/shard_map/prepare/pallas_call | solution.py:139
  36.9 0.8 copy-done.6
  37.6 0.8 copy-done.8
  41.4 1.4 collective-permute-done.13
  42.8 3.9 %prepare.5 = (bf16[768,640]{1,0:T(8,128)(2,1)S(1)}, bf16[768,640]{1,0:T(8,128)(2,1)S(1)}, bf16[384,640]{1,0:T(8,128)(2,1)S(1)}, bf16[384,640]{1,0:T(8,128)(2,1)S(1)}, f32[384,640]{1,0:T(8,128)S(1)}) custom-call(s32[1,1]{1,0:T(1,128)} %bitcast.refs_0_, f32[960,128]{1,0:T(8,128)} %bitcast.11.refs_1_, f32[960,128]{1,0:T(8,128)} %bitcast.12.refs_2_, ...), custom_call_target="tpu_custom_call" | custom-call | tf_op jit(solution)/shard_map/prepare/pallas_call | solution.py:139
  46.8 7.9 %amplitude_tile.4 = (f32[960,128]{1,0:T(8,128)S(1)}, f32[960,128]{1,0:T(8,128)S(1)}, f32[8,128]{1,0:T(8,128)S(1)}) custom-call(bf16[768,640]{1,0:T(8,128)(2,1)S(1)} %get-tuple-element.42.refs_0_.refs_4_, bf16[768,640]{1,0:T(8,128)(2,1)S(1)} %get-tuple-element.52.refs_1_.refs_5_, bf16[768,640]{1,0:T(8,128)(2,1)S(1)} %get-tuple-element.44.refs_2_.refs_6_, ...), custom_call_target="tpu_custom_call" | custom-call | tf_op jit(solution)/shard_map/amplitude_tile/pallas_call | solution.py:277
  55.2 3.3 %collective-permute-start.16 = (f32[5,192,128]{2,1,0:T(8,128)S(1)}, f32[5,192,128]{2,1,0:T(8,128)S(1)}, u32[]{:S(2)}, u32[]{:S(2)}) collective-permute-start(f32[5,192,128]{2,1,0:T(8,128)S(1)} %bitcast.121), channel_id=1, source_target_pairs={{0,2},{1,3},{2,0},{3,1},{4,6},{5,7},{6,4},{7,5},{8,10},{9,11},{10,... | collective-permute-start | bytes 1474568 | tf_op jit(solution)/shard_map/ppermute | solution.py:28
  58.6 7.8 %amplitude_tile.3 = (f32[960,128]{1,0:T(8,128)S(1)}, f32[960,128]{1,0:T(8,128)S(1)}, f32[8,128]{1,0:T(8,128)S(1)}) custom-call(bf16[768,640]{1,0:T(8,128)(2,1)S(1)} %get-tuple-element.42.refs_0_.refs_4_, bf16[768,640]{1,0:T(8,128)(2,1)S(1)} %get-tuple-element.52.refs_1_.refs_5_, bf16[768,640]{1,0:T(8,128)(2,1)S(1)} %get-tuple-element.44.refs_2_.refs_6_, ...), custom_call_target="tpu_custom_call" | custom-call | tf_op jit(solution)/shard_map/amplitude_tile/pallas_call | solution.py:277
  66.5 1.6 collective-permute-done.17
  68.1 1.4 collective-permute-start.18
  70.3 1.4 collective-permute-start.20
  71.8 3.7 %collective-permute-done.18 = f32[5,96,128]{2,1,0:T(8,128)S(1)} collective-permute-done((f32[5,96,128]{2,1,0:T(8,128)S(1)}, f32[5,96,128]{2,1,0:T(8,128)S(1)}, u32[]{:S(2)}, u32[]{:S(2)}) %collective-permute-start.18) | collective-permute-done | bytes 245792 | tf_op jit(solution)/shard_map/ppermute | solution.py:28
  75.5 2.2 %collective-permute-done.19 = f32[5,96,128]{2,1,0:T(8,128)S(1)} collective-permute-done((f32[5,96,128]{2,1,0:T(8,128)S(1)}, f32[5,96,128]{2,1,0:T(8,128)S(1)}, u32[]{:S(2)}, u32[]{:S(2)}) %collective-permute-start.19) | collective-permute-done | bytes 245792 | tf_op jit(solution)/shard_map/ppermute | solution.py:28
  77.8 1.5 collective-permute-done.21
  79.4 1.2 collective-permute-start.22
  81.1 2.7 %collective-permute-start.24 = (f32[5,192,128]{2,1,0:T(8,128)S(1)}, f32[5,192,128]{2,1,0:T(8,128)S(1)}, u32[]{:S(2)}, u32[]{:S(2)}) collective-permute-start(f32[5,192,128]{2,1,0:T(8,128)S(1)} %pad_maximum_fusion.4), channel_id=1, source_target_pairs={{0,3},{8,56},{1,0},{9,57},{2,1},{10,58},{3,2},{11,59},{4,7},{12,60... | collective-permute-start | bytes 1474568 | tf_op jit(solution)/shard_map/ppermute | solution.py:57
  83.8 1.1 collective-permute-start.25
  84.9 3.3 %collective-permute-done.22 = f32[5,192,128]{2,1,0:T(8,128)S(1)} collective-permute-done((f32[5,192,128]{2,1,0:T(8,128)S(1)}, f32[5,192,128]{2,1,0:T(8,128)S(1)}, u32[]{:S(2)}, u32[]{:S(2)}) %collective-permute-start.22) | collective-permute-done | bytes 491552 | tf_op jit(solution)/shard_map/ppermute | solution.py:57
  88.8 1.9 %collective-permute-done.23 = f32[5,192,128]{2,1,0:T(8,128)S(1)} collective-permute-done((f32[5,192,128]{2,1,0:T(8,128)S(1)}, f32[5,192,128]{2,1,0:T(8,128)S(1)}, u32[]{:S(2)}, u32[]{:S(2)}) %collective-permute-start.23) | collective-permute-done | bytes 491552 | tf_op jit(solution)/shard_map/ppermute | solution.py:57
  91.2 0.9 collective-permute-start.32
  92.0 1.2 collective-permute-start.31
  93.2 2.9 %collective-permute-start.30 = (f32[5,192,128]{2,1,0:T(8,128)S(1)}, f32[5,192,128]{2,1,0:T(8,128)S(1)}, u32[]{:S(2)}, u32[]{:S(2)}) collective-permute-start(f32[5,192,128]{2,1,0:T(8,128)S(1)} %collective-permute-done.22), channel_id=1, source_target_pairs={{0,2},{8,40},{1,3},{9,41},{2,0},{10,42},{3,1},{11,43},{4,6},{12,44... | collective-permute-start | bytes 1474568 | tf_op jit(solution)/shard_map/ppermute | solution.py:57
  96.7 2.9 %prepare.6 = (bf16[768,640]{1,0:T(8,128)(2,1)S(1)}, bf16[768,640]{1,0:T(8,128)(2,1)S(1)}, bf16[384,640]{1,0:T(8,128)(2,1)S(1)}, bf16[384,640]{1,0:T(8,128)(2,1)S(1)}, f32[384,640]{1,0:T(8,128)}) custom-call(s32[1,1]{1,0:T(1,128)} %bitcast.refs_0_, f32[960,128]{1,0:T(8,128)S(1)} %bitcast.94, f32[960,128]{1,0:T(8,128)S(1)} %bitcast.100, ...), custom_call_target="tpu_custom_call" | custom-call | tf_op jit(solution)/shard_map/prepare/pallas_call | solution.py:139
  100.0 0.9 collective-permute-start.36
  100.8 4.4 %collective-permute-done.31 = f32[5,192,128]{2,1,0:T(8,128)S(1)} collective-permute-done((f32[5,192,128]{2,1,0:T(8,128)S(1)}, f32[5,192,128]{2,1,0:T(8,128)S(1)}, u32[]{:S(2)}, u32[]{:S(2)}) %collective-permute-start.31) | collective-permute-done | bytes 491552 | tf_op jit(solution)/shard_map/ppermute | solution.py:57
  105.3 0.9 collective-permute-start.35
  106.1 2.7 %collective-permute-done.29 = f32[5,192,128]{2,1,0:T(8,128)S(1)} collective-permute-done((f32[5,192,128]{2,1,0:T(8,128)S(1)}, f32[5,192,128]{2,1,0:T(8,128)S(1)}, u32[]{:S(2)}, u32[]{:S(2)}) %collective-permute-start.29) | collective-permute-done | bytes 491552 | tf_op jit(solution)/shard_map/ppermute | solution.py:57
  108.9 1.7 %collective-permute-done.33 = f32[5,192,128]{2,1,0:T(8,128)S(1)} collective-permute-done((f32[5,192,128]{2,1,0:T(8,128)S(1)}, f32[5,192,128]{2,1,0:T(8,128)S(1)}, u32[]{:S(2)}, u32[]{:S(2)}) %collective-permute-start.33) | collective-permute-done | bytes 491552 | tf_op jit(solution)/shard_map/ppermute | solution.py:32
  110.7 3.1 %prepare.7 = (bf16[768,640]{1,0:T(8,128)(2,1)S(1)}, bf16[768,640]{1,0:T(8,128)(2,1)S(1)}, bf16[384,640]{1,0:T(8,128)(2,1)S(1)}, bf16[384,640]{1,0:T(8,128)(2,1)S(1)}, f32[384,640]{1,0:T(8,128)}) custom-call(s32[1,1]{1,0:T(1,128)} %bitcast.refs_0_, f32[960,128]{1,0:T(8,128)S(1)} %bitcast.105, f32[960,128]{1,0:T(8,128)S(1)} %bitcast.104, ...), custom_call_target="tpu_custom_call" | custom-call | tf_op jit(solution)/shard_map/prepare/pallas_call | solution.py:139
  113.8 12.8 %amplitude_tile.5 = (f32[960,128]{1,0:T(8,128)S(1)}, f32[960,128]{1,0:T(8,128)S(1)}, f32[960,128]{1,0:T(8,128)S(1)}, f32[960,128]{1,0:T(8,128)S(1)}, f32[8,128]{1,0:T(8,128)S(1)}) custom-call(bf16[768,640]{1,0:T(8,128)(2,1)S(1)} %get-tuple-element.61.refs_0_, bf16[768,640]{1,0:T(8,128)(2,1)S(1)} %get-tuple-element.71.refs_1_, ...), custom_call_target="tpu_custom_call" | custom-call | tf_op jit(solution)/shard_map/amplitude_tile/pallas_call | solution.py:277
  126.6 3.0 %collective-permute-start.37 = (f32[5,192,128]{2,1,0:T(8,128)S(1)}, f32[5,192,128]{2,1,0:T(8,128)S(1)}, u32[]{:S(2)}, u32[]{:S(2)}) collective-permute-start(f32[5,192,128]{2,1,0:T(8,128)S(1)} %bitcast.120), channel_id=1, source_target_pairs={{0,2},{1,3},{2,0},{3,1},{4,6},{5,7},{6,4},{7,5},{8,10},{9,11},{10,... | collective-permute-start | bytes 1474568 | tf_op jit(solution)/shard_map/ppermute | solution.py:28
  130.2 3.2 %collective-permute-start.40 = (f32[8,128]{1,0:T(8,128)S(1)}, f32[8,128]{1,0:T(8,128)S(1)}, u32[]{:S(2)}, u32[]{:S(2)}) collective-permute-start(f32[8,128]{1,0:T(8,128)S(1)} %add_select_fusion), channel_id=1, source_target_pairs={{0,48},{1,49},{2,50},{3,51},{4,52},{5,53},{6,54},{7,55},{8,56},{9,... | collective-permute-start | bytes 12296 | tf_op jit(solution)/shard_map/ppermute | solution.py:44
  133.4 1.2 collective-permute-start.41
  135.0 3.5 %collective-permute-done.41 = f32[8,128]{1,0:T(8,128)S(1)} collective-permute-done((f32[8,128]{1,0:T(8,128)S(1)}, f32[8,128]{1,0:T(8,128)S(1)}, u32[]{:S(2)}, u32[]{:S(2)}) %collective-permute-start.41) | collective-permute-done | bytes 4128 | tf_op jit(solution)/shard_map/ppermute | solution.py:44
  138.5 2.0 %collective-permute-start.42 = (f32[8,128]{1,0:T(8,128)S(1)}, f32[8,128]{1,0:T(8,128)S(1)}, u32[]{:S(2)}, u32[]{:S(2)}) collective-permute-start(f32[8,128]{1,0:T(8,128)S(1)} %add_add_fusion.1), channel_id=1, source_target_pairs={{0,68},{1,69},{2,70},{3,71},{4,64},{5,65},{6,66},{7,67},{8,76},{9,... | collective-permute-start | bytes 12296 | tf_op jit(solution)/shard_map/ppermute | solution.py:44
  140.6 1.8 %collective-permute-start.43 = (f32[8,128]{1,0:T(8,128)S(1)}, f32[8,128]{1,0:T(8,128)S(1)}, u32[]{:S(2)}, u32[]{:S(2)}) collective-permute-start(f32[8,128]{1,0:T(8,128)S(1)} %add_add_fusion.1), channel_id=1, source_target_pairs={{0,6},{1,7},{2,4},{3,5},{4,2},{5,3},{6,0},{7,1},{8,14},{9,15},{10,... | collective-permute-start | bytes 12296 | tf_op jit(solution)/shard_map/ppermute | solution.py:44
  142.4 3.3 %collective-permute-start.44 = (f32[8,128]{1,0:T(8,128)S(1)}, f32[8,128]{1,0:T(8,128)S(1)}, u32[]{:S(2)}, u32[]{:S(2)}) collective-permute-start(f32[8,128]{1,0:T(8,128)S(1)} %add_add_fusion.1), channel_id=1, source_target_pairs={{0,66},{1,67},{2,64},{3,65},{4,70},{5,71},{6,68},{7,69},{8,74},{9,... | collective-permute-start | bytes 12296 | tf_op jit(solution)/shard_map/ppermute | solution.py:44
  145.6 1.0 collective-permute-done.43
  146.6 3.3 %collective-permute-done.44 = f32[8,128]{1,0:T(8,128)S(1)} collective-permute-done((f32[8,128]{1,0:T(8,128)S(1)}, f32[8,128]{1,0:T(8,128)S(1)}, u32[]{:S(2)}, u32[]{:S(2)}) %collective-permute-start.44) | collective-permute-done | bytes 4128 | tf_op jit(solution)/shard_map/ppermute | solution.py:44
  150.0 0.8 copy-done.14
  150.9 0.9 slice-done
  151.8 2.8 %collective-permute-start.45 = (f32[5,104,128]{2,1,0:T(8,128)S(1)}, f32[5,104,128]{2,1,0:T(8,128)S(1)}, u32[]{:S(2)}, u32[]{:S(2)}) collective-permute-start(f32[5,104,128]{2,1,0:T(8,128)S(1)} %get-tuple-element.94), channel_id=1, source_target_pairs={{0,3},{1,0},{2,1},{3,2},{4,7},{5,4},{6,5},{7,6},{8,11},{9,8},{10,9... | collective-permute-start | bytes 798728 | tf_op jit(solution)/shard_map/ppermute | solution.py:28
  154.6 1.5 collective-permute-start.47
  156.1 2.4 %collective-permute-done.45 = f32[5,104,128]{2,1,0:T(8,128)S(1)} collective-permute-done((f32[5,104,128]{2,1,0:T(8,128)S(1)}, f32[5,104,128]{2,1,0:T(8,128)S(1)}, u32[]{:S(2)}, u32[]{:S(2)}) %collective-permute-start.45) | collective-permute-done | bytes 266272 | tf_op jit(solution)/shard_map/ppermute | solution.py:28
  158.6 3.7 %collective-permute-done.46 = f32[5,104,128]{2,1,0:T(8,128)S(1)} collective-permute-done((f32[5,104,128]{2,1,0:T(8,128)S(1)}, f32[5,104,128]{2,1,0:T(8,128)S(1)}, u32[]{:S(2)}, u32[]{:S(2)}) %collective-permute-start.46) | collective-permute-done | bytes 266272 | tf_op jit(solution)/shard_map/ppermute | solution.py:28
  162.6 0.9 copy.67
  (125 shorter events, 12.2 us)
Async XLA Ops:
  1.9 1.6 %copy-start.12 = (f32[96,5,128]{2,0,1:T(8,128)}, f32[96,5,128]{2,0,1:T(8,128)S(1)}, u32[]{:S(2)}) copy-start(f32[96,5,128]{2,0,1:T(8,128)S(1)} %copy.65) | copy-start | bytes 737284
  1.9 1.6 collective-permute-start
  3.5 9.5 %collective-permute-start.3 = (f32[5,192,128]{2,1,0:T(8,128)S(1)}, f32[5,192,128]{2,1,0:T(8,128)}, u32[]{:S(2)}, u32[]{:S(2)}) collective-permute-start(f32[5,192,128]{2,1,0:T(8,128)S(1)} %pad_maximum_fusion.3), channel_id=1, source_target_pairs={{0,3},{8,56},{1,0},{9,57},{2,1},{10,58},{3,2},{11,59},{4,7},{12,60... | collective-permute-start | bytes 1474568 | tf_op jit(solution)/shard_map/ppermute | solution.py:57
  6.7 10.1 %collective-permute-start.2 = (f32[5,192,128]{2,1,0:T(8,128)S(1)}, f32[5,192,128]{2,1,0:T(8,128)}, u32[]{:S(2)}, u32[]{:S(2)}) collective-permute-start(f32[5,192,128]{2,1,0:T(8,128)S(1)} %pad_maximum_fusion.3), channel_id=1, source_target_pairs={{0,1},{8,24},{1,2},{9,25},{2,3},{10,26},{3,0},{11,27},{4,5},{12,28... | collective-permute-start | bytes 1474568 | tf_op jit(solution)/shard_map/ppermute | solution.py:57
  6.7 12.8 %collective-permute-start.1 = (f32[5,192,128]{2,1,0:T(8,128)S(1)}, f32[5,192,128]{2,1,0:T(8,128)}, u32[]{:S(2)}, u32[]{:S(2)}) collective-permute-start(f32[5,192,128]{2,1,0:T(8,128)S(1)} %pad_maximum_fusion.3), channel_id=1, source_target_pairs={{0,4},{8,76},{1,5},{9,77},{2,6},{10,78},{3,7},{11,79},{4,0},{12,72... | collective-permute-start | bytes 1474568 | tf_op jit(solution)/shard_map/ppermute | solution.py:57
  8.6 12.8 %collective-permute-start.4 = (f32[5,192,128]{2,1,0:T(8,128)S(1)}, f32[5,192,128]{2,1,0:T(8,128)S(1)}, u32[]{:S(2)}, u32[]{:S(2)}) collective-permute-start(f32[5,192,128]{2,1,0:T(8,128)S(1)} %pad_maximum_fusion.3), channel_id=1, source_target_pairs={{0,8},{8,0},{1,9},{9,1},{2,10},{10,2},{3,11},{11,3},{4,12},{12,4},... | collective-permute-start | bytes 1474568 | tf_op jit(solution)/shard_map/ppermute | solution.py:32
  13.1 9.3 %collective-permute-start.7 = (f32[5,192,128]{2,1,0:T(8,128)}, f32[5,192,128]{2,1,0:T(8,128)S(1)}, u32[]{:S(2)}, u32[]{:S(2)}) collective-permute-start(f32[5,192,128]{2,1,0:T(8,128)} %collective-permute-done.3), channel_id=1, source_target_pairs={{0,8},{8,0},{1,9},{9,1},{2,10},{10,2},{3,11},{11,3},{4,12},{12,4},... | collective-permute-start | bytes 1474568 | tf_op jit(solution)/shard_map/ppermute | solution.py:32
  16.9 9.6 %collective-permute-start.6 = (f32[5,192,128]{2,1,0:T(8,128)}, f32[5,192,128]{2,1,0:T(8,128)S(1)}, u32[]{:S(2)}, u32[]{:S(2)}) collective-permute-start(f32[5,192,128]{2,1,0:T(8,128)} %collective-permute-done.2), channel_id=1, source_target_pairs={{0,8},{8,0},{1,9},{9,1},{2,10},{10,2},{3,11},{11,3},{4,12},{12,4},... | collective-permute-start | bytes 1474568 | tf_op jit(solution)/shard_map/ppermute | solution.py:32
  17.8 21.4 %collective-permute-start.8 = (f32[5,192,128]{2,1,0:T(8,128)S(1)}, f32[5,192,128]{2,1,0:T(8,128)}, u32[]{:S(2)}, u32[]{:S(2)}) collective-permute-start(f32[5,192,128]{2,1,0:T(8,128)S(1)} %pad_maximum_fusion.3), channel_id=1, source_target_pairs={{0,2},{8,40},{1,3},{9,41},{2,0},{10,42},{3,1},{11,43},{4,6},{12,44... | collective-permute-start | bytes 1474568 | tf_op jit(solution)/shard_map/ppermute | solution.py:57
  19.5 18.9 %collective-permute-start.11 = (f32[5,192,128]{2,1,0:T(8,128)}, f32[5,192,128]{2,1,0:T(8,128)}, u32[]{:S(2)}, u32[]{:S(2)}) collective-permute-start(f32[5,192,128]{2,1,0:T(8,128)} %collective-permute-done.3), channel_id=1, source_target_pairs={{0,4},{8,76},{1,5},{9,77},{2,6},{10,78},{3,7},{11,79},{4,0},{12,72... | collective-permute-start | bytes 1474568 | tf_op jit(solution)/shard_map/ppermute | solution.py:57
  21.4 0.8 copy-start
  22.2 16.4 %collective-permute-start.10 = (f32[5,192,128]{2,1,0:T(8,128)}, f32[5,192,128]{2,1,0:T(8,128)}, u32[]{:S(2)}, u32[]{:S(2)}) collective-permute-start(f32[5,192,128]{2,1,0:T(8,128)} %collective-permute-done.2), channel_id=1, source_target_pairs={{0,4},{8,76},{1,5},{9,77},{2,6},{10,78},{3,7},{11,79},{4,0},{12,72... | collective-permute-start | bytes 1474568 | tf_op jit(solution)/shard_map/ppermute | solution.py:57
  23.1 5.5 %collective-permute-start.5 = (f32[5,192,128]{2,1,0:T(8,128)}, f32[5,192,128]{2,1,0:T(8,128)S(1)}, u32[]{:S(2)}, u32[]{:S(2)}) collective-permute-start(f32[5,192,128]{2,1,0:T(8,128)} %collective-permute-done.1), channel_id=1, source_target_pairs={{0,8},{8,0},{1,9},{9,1},{2,10},{10,2},{3,11},{11,3},{4,12},{12,4},... | collective-permute-start | bytes 1474568 | tf_op jit(solution)/shard_map/ppermute | solution.py:32
  26.5 0.8 copy-start.4
  27.3 11.7 %collective-permute-start.9 = (f32[5,192,128]{2,1,0:T(8,128)}, f32[5,192,128]{2,1,0:T(8,128)}, u32[]{:S(2)}, u32[]{:S(2)}) collective-permute-start(f32[5,192,128]{2,1,0:T(8,128)} %collective-permute-done.1), channel_id=1, source_target_pairs={{0,2},{8,40},{1,3},{9,41},{2,0},{10,42},{3,1},{11,43},{4,6},{12,44... | collective-permute-start | bytes 1474568 | tf_op jit(solution)/shard_map/ppermute | solution.py:57
  28.7 0.8 copy-start.10
  29.5 1.0 copy-start.1
  30.5 1.0 copy-start.3
  31.5 1.0 copy-start.5
  32.6 1.0 copy-start.11
  37.6 0.8 copy-start.8
  38.4 2.2 %collective-permute-start.15 = (f32[5,192,128]{2,1,0:T(8,128)}, f32[5,192,128]{2,1,0:T(8,128)}, u32[]{:S(2)}, u32[]{:S(2)}) collective-permute-start(f32[5,192,128]{2,1,0:T(8,128)} %collective-permute-done.11), channel_id=1, source_target_pairs={{0,8},{8,0},{1,9},{9,1},{2,10},{10,2},{3,11},{11,3},{4,12},{12,4},... | collective-permute-start | bytes 1474568 | tf_op jit(solution)/shard_map/ppermute | solution.py:32
  38.7 2.7 %collective-permute-start.14 = (f32[5,192,128]{2,1,0:T(8,128)}, f32[5,192,128]{2,1,0:T(8,128)}, u32[]{:S(2)}, u32[]{:S(2)}) collective-permute-start(f32[5,192,128]{2,1,0:T(8,128)} %collective-permute-done.10), channel_id=1, source_target_pairs={{0,8},{8,0},{1,9},{9,1},{2,10},{10,2},{3,11},{11,3},{4,12},{12,4},... | collective-permute-start | bytes 1474568 | tf_op jit(solution)/shard_map/ppermute | solution.py:32
  39.0 3.8 %collective-permute-start.13 = (f32[5,192,128]{2,1,0:T(8,128)}, f32[5,192,128]{2,1,0:T(8,128)}, u32[]{:S(2)}, u32[]{:S(2)}) collective-permute-start(f32[5,192,128]{2,1,0:T(8,128)} %collective-permute-done.9), channel_id=1, source_target_pairs={{0,8},{8,0},{1,9},{9,1},{2,10},{10,2},{3,11},{11,3},{4,12},{12,4},... | collective-permute-start | bytes 1474568 | tf_op jit(solution)/shard_map/ppermute | solution.py:32
  39.2 3.6 %collective-permute-start.12 = (f32[5,192,128]{2,1,0:T(8,128)}, f32[5,192,128]{2,1,0:T(8,128)S(1)}, u32[]{:S(2)}, u32[]{:S(2)}) collective-permute-start(f32[5,192,128]{2,1,0:T(8,128)} %collective-permute-done.8), channel_id=1, source_target_pairs={{0,8},{8,0},{1,9},{9,1},{2,10},{10,2},{3,11},{11,3},{4,12},{12,4},... | collective-permute-start | bytes 1474568 | tf_op jit(solution)/shard_map/ppermute | solution.py:32
  46.7 11.9 %copy-start.7 = (bf16[384,640]{1,0:T(8,128)(2,1)S(1)}, bf16[384,640]{1,0:T(8,128)(2,1)}, u32[]{:S(2)}) copy-start(bf16[384,640]{1,0:T(8,128)(2,1)} %copy-done.6) | copy-start | bytes 1474564
  46.8 11.9 %copy-start.9 = (bf16[384,640]{1,0:T(8,128)(2,1)S(1)}, bf16[384,640]{1,0:T(8,128)(2,1)}, u32[]{:S(2)}) copy-start(bf16[384,640]{1,0:T(8,128)(2,1)} %copy-done.8) | copy-start | bytes 1474564
  54.6 13.4 %collective-permute-start.17 = (f32[5,192,128]{2,1,0:T(8,128)S(1)}, f32[5,192,128]{2,1,0:T(8,128)S(1)}, u32[]{:S(2)}, u32[]{:S(2)}) collective-permute-start(f32[5,192,128]{2,1,0:T(8,128)S(1)} %bitcast.122), channel_id=1, source_target_pairs={{0,4},{1,5},{2,6},{3,7},{4,0},{5,1},{6,2},{7,3},{8,12},{9,13},{10,... | collective-permute-start | bytes 1474568 | tf_op jit(solution)/shard_map/ppermute | solution.py:28
  55.2 15.1 %collective-permute-start.16 = (f32[5,192,128]{2,1,0:T(8,128)S(1)}, f32[5,192,128]{2,1,0:T(8,128)S(1)}, u32[]{:S(2)}, u32[]{:S(2)}) collective-permute-start(f32[5,192,128]{2,1,0:T(8,128)S(1)} %bitcast.121), channel_id=1, source_target_pairs={{0,2},{1,3},{2,0},{3,1},{4,6},{5,7},{6,4},{7,5},{8,10},{9,11},{10,... | collective-permute-start | bytes 1474568 | tf_op jit(solution)/shard_map/ppermute | solution.py:28
  68.1 7.3 %collective-permute-start.18 = (f32[5,96,128]{2,1,0:T(8,128)S(1)}, f32[5,96,128]{2,1,0:T(8,128)S(1)}, u32[]{:S(2)}, u32[]{:S(2)}) collective-permute-start(f32[5,96,128]{2,1,0:T(8,128)S(1)} %get-tuple-element.92), channel_id=1, source_target_pairs={{0,3},{1,0},{2,1},{3,2},{4,7},{5,4},{6,5},{7,6},{8,11},{9,8},{10,9... | collective-permute-start | bytes 737288 | tf_op jit(solution)/shard_map/ppermute | solution.py:28
  69.6 8.1 %collective-permute-start.19 = (f32[5,96,128]{2,1,0:T(8,128)S(1)}, f32[5,96,128]{2,1,0:T(8,128)S(1)}, u32[]{:S(2)}, u32[]{:S(2)}) collective-permute-start(f32[5,96,128]{2,1,0:T(8,128)S(1)} %get-tuple-element.93), channel_id=1, source_target_pairs={{0,1},{1,2},{2,3},{3,0},{4,5},{5,6},{6,7},{7,4},{8,9},{9,10},{10,1... | collective-permute-start | bytes 737288 | tf_op jit(solution)/shard_map/ppermute | solution.py:28
  70.3 7.4 %copy-start.13 = (f32[96,5,128]{2,0,1:T(8,128)S(1)}, f32[96,5,128]{2,0,1:T(8,128)}, u32[]{:S(2)}) copy-start(f32[96,5,128]{2,0,1:T(8,128)} %copy-done.12) | copy-start | bytes 737284
  70.3 7.3 %collective-permute-start.20 = (f32[5,96,128]{2,1,0:T(8,128)S(1)}, f32[5,96,128]{2,1,0:T(8,128)S(1)}, u32[]{:S(2)}, u32[]{:S(2)}) collective-permute-start(f32[5,96,128]{2,1,0:T(8,128)S(1)} %slice.83), channel_id=1, source_target_pairs={{0,4},{1,5},{2,6},{3,7},{4,0},{5,1},{6,2},{7,3},{8,12},{9,13},{10,... | collective-permute-start | bytes 737288 | tf_op jit(solution)/shard_map/ppermute | solution.py:28
  77.7 1.6 collective-permute-start.21
  79.4 8.9 %collective-permute-start.22 = (f32[5,192,128]{2,1,0:T(8,128)S(1)}, f32[5,192,128]{2,1,0:T(8,128)S(1)}, u32[]{:S(2)}, u32[]{:S(2)}) collective-permute-start(f32[5,192,128]{2,1,0:T(8,128)S(1)} %pad_maximum_fusion.4), channel_id=1, source_target_pairs={{0,4},{8,76},{1,5},{9,77},{2,6},{10,78},{3,7},{11,79},{4,0},{12,72... | collective-permute-start | bytes 1474568 | tf_op jit(solution)/shard_map/ppermute | solution.py:57
  80.6 10.0 %collective-permute-start.23 = (f32[5,192,128]{2,1,0:T(8,128)S(1)}, f32[5,192,128]{2,1,0:T(8,128)S(1)}, u32[]{:S(2)}, u32[]{:S(2)}) collective-permute-start(f32[5,192,128]{2,1,0:T(8,128)S(1)} %pad_maximum_fusion.4), channel_id=1, source_target_pairs={{0,1},{8,24},{1,2},{9,25},{2,3},{10,26},{3,0},{11,27},{4,5},{12,28... | collective-permute-start | bytes 1474568 | tf_op jit(solution)/shard_map/ppermute | solution.py:57
  81.1 10.0 %collective-permute-start.24 = (f32[5,192,128]{2,1,0:T(8,128)S(1)}, f32[5,192,128]{2,1,0:T(8,128)S(1)}, u32[]{:S(2)}, u32[]{:S(2)}) collective-permute-start(f32[5,192,128]{2,1,0:T(8,128)S(1)} %pad_maximum_fusion.4), channel_id=1, source_target_pairs={{0,3},{8,56},{1,0},{9,57},{2,1},{10,58},{3,2},{11,59},{4,7},{12,60... | collective-permute-start | bytes 1474568 | tf_op jit(solution)/shard_map/ppermute | solution.py:57
  83.8 8.2 %collective-permute-start.25 = (f32[5,192,128]{2,1,0:T(8,128)S(1)}, f32[5,192,128]{2,1,0:T(8,128)S(1)}, u32[]{:S(2)}, u32[]{:S(2)}) collective-permute-start(f32[5,192,128]{2,1,0:T(8,128)S(1)} %pad_maximum_fusion.4), channel_id=1, source_target_pairs={{0,8},{8,0},{1,9},{9,1},{2,10},{10,2},{3,11},{11,3},{4,12},{12,4},... | collective-permute-start | bytes 1474568 | tf_op jit(solution)/shard_map/ppermute | solution.py:32
  88.3 4.9 %collective-permute-start.26 = (f32[5,192,128]{2,1,0:T(8,128)S(1)}, f32[5,192,128]{2,1,0:T(8,128)S(1)}, u32[]{:S(2)}, u32[]{:S(2)}) collective-permute-start(f32[5,192,128]{2,1,0:T(8,128)S(1)} %collective-permute-done.22), channel_id=1, source_target_pairs={{0,8},{8,0},{1,9},{9,1},{2,10},{10,2},{3,11},{11,3},{4,12},{12,4},... | collective-permute-start | bytes 1474568 | tf_op jit(solution)/shard_map/ppermute | solution.py:32
  90.6 5.5 %collective-permute-start.27 = (f32[5,192,128]{2,1,0:T(8,128)S(1)}, f32[5,192,128]{2,1,0:T(8,128)S(1)}, u32[]{:S(2)}, u32[]{:S(2)}) collective-permute-start(f32[5,192,128]{2,1,0:T(8,128)S(1)} %collective-permute-done.23), channel_id=1, source_target_pairs={{0,8},{8,0},{1,9},{9,1},{2,10},{10,2},{3,11},{11,3},{4,12},{12,4},... | collective-permute-start | bytes 1474568 | tf_op jit(solution)/shard_map/ppermute | solution.py:32
  91.2 5.6 %collective-permute-start.28 = (f32[5,192,128]{2,1,0:T(8,128)S(1)}, f32[5,192,128]{2,1,0:T(8,128)S(1)}, u32[]{:S(2)}, u32[]{:S(2)}) collective-permute-start(f32[5,192,128]{2,1,0:T(8,128)S(1)} %collective-permute-done.24), channel_id=1, source_target_pairs={{0,8},{8,0},{1,9},{9,1},{2,10},{10,2},{3,11},{11,3},{4,12},{12,4},... | collective-permute-start | bytes 1474568 | tf_op jit(solution)/shard_map/ppermute | solution.py:32
  91.2 8.8 %collective-permute-start.32 = (f32[5,192,128]{2,1,0:T(8,128)S(1)}, f32[5,192,128]{2,1,0:T(8,128)S(1)}, u32[]{:S(2)}, u32[]{:S(2)}) collective-permute-start(f32[5,192,128]{2,1,0:T(8,128)S(1)} %collective-permute-done.24), channel_id=1, source_target_pairs={{0,4},{8,76},{1,5},{9,77},{2,6},{10,78},{3,7},{11,79},{4,0},{12,72... | collective-permute-start | bytes 1474568 | tf_op jit(solution)/shard_map/ppermute | solution.py:57
  92.0 13.2 %collective-permute-start.31 = (f32[5,192,128]{2,1,0:T(8,128)S(1)}, f32[5,192,128]{2,1,0:T(8,128)S(1)}, u32[]{:S(2)}, u32[]{:S(2)}) collective-permute-start(f32[5,192,128]{2,1,0:T(8,128)S(1)} %collective-permute-done.23), channel_id=1, source_target_pairs={{0,4},{8,76},{1,5},{9,77},{2,6},{10,78},{3,7},{11,79},{4,0},{12,72... | collective-permute-start | bytes 1474568 | tf_op jit(solution)/shard_map/ppermute | solution.py:57
  93.2 12.9 %collective-permute-start.30 = (f32[5,192,128]{2,1,0:T(8,128)S(1)}, f32[5,192,128]{2,1,0:T(8,128)S(1)}, u32[]{:S(2)}, u32[]{:S(2)}) collective-permute-start(f32[5,192,128]{2,1,0:T(8,128)S(1)} %collective-permute-done.22), channel_id=1, source_target_pairs={{0,2},{8,40},{1,3},{9,41},{2,0},{10,42},{3,1},{11,43},{4,6},{12,44... | collective-permute-start | bytes 1474568 | tf_op jit(solution)/shard_map/ppermute | solution.py:57
  96.1 12.7 %collective-permute-start.29 = (f32[5,192,128]{2,1,0:T(8,128)S(1)}, f32[5,192,128]{2,1,0:T(8,128)S(1)}, u32[]{:S(2)}, u32[]{:S(2)}) collective-permute-start(f32[5,192,128]{2,1,0:T(8,128)S(1)} %pad_maximum_fusion.4), channel_id=1, source_target_pairs={{0,2},{8,40},{1,3},{9,41},{2,0},{10,42},{3,1},{11,43},{4,6},{12,44... | collective-permute-start | bytes 1474568 | tf_op jit(solution)/shard_map/ppermute | solution.py:57
  100.0 8.9 %collective-permute-start.36 = (f32[5,192,128]{2,1,0:T(8,128)S(1)}, f32[5,192,128]{2,1,0:T(8,128)S(1)}, u32[]{:S(2)}, u32[]{:S(2)}) collective-permute-start(f32[5,192,128]{2,1,0:T(8,128)S(1)} %collective-permute-done.32), channel_id=1, source_target_pairs={{0,8},{8,0},{1,9},{9,1},{2,10},{10,2},{3,11},{11,3},{4,12},{12,4},... | collective-permute-start | bytes 1474568 | tf_op jit(solution)/shard_map/ppermute | solution.py:32
  105.3 3.7 %collective-permute-start.35 = (f32[5,192,128]{2,1,0:T(8,128)S(1)}, f32[5,192,128]{2,1,0:T(8,128)S(1)}, u32[]{:S(2)}, u32[]{:S(2)}) collective-permute-start(f32[5,192,128]{2,1,0:T(8,128)S(1)} %collective-permute-done.31), channel_id=1, source_target_pairs={{0,8},{8,0},{1,9},{9,1},{2,10},{10,2},{3,11},{11,3},{4,12},{12,4},... | collective-permute-start | bytes 1474568 | tf_op jit(solution)/shard_map/ppermute | solution.py:32
  106.1 2.8 %collective-permute-start.34 = (f32[5,192,128]{2,1,0:T(8,128)S(1)}, f32[5,192,128]{2,1,0:T(8,128)S(1)}, u32[]{:S(2)}, u32[]{:S(2)}) collective-permute-start(f32[5,192,128]{2,1,0:T(8,128)S(1)} %collective-permute-done.30), channel_id=1, source_target_pairs={{0,8},{8,0},{1,9},{9,1},{2,10},{10,2},{3,11},{11,3},{4,12},{12,4},... | collective-permute-start | bytes 1474568 | tf_op jit(solution)/shard_map/ppermute | solution.py:32
  108.8 1.9 %collective-permute-start.33 = (f32[5,192,128]{2,1,0:T(8,128)S(1)}, f32[5,192,128]{2,1,0:T(8,128)S(1)}, u32[]{:S(2)}, u32[]{:S(2)}) collective-permute-start(f32[5,192,128]{2,1,0:T(8,128)S(1)} %collective-permute-done.29), channel_id=1, source_target_pairs={{0,8},{8,0},{1,9},{9,1},{2,10},{10,2},{3,11},{11,3},{4,12},{12,4},... | collective-permute-start | bytes 1474568 | tf_op jit(solution)/shard_map/ppermute | solution.py:32
  126.6 23.3 %collective-permute-start.37 = (f32[5,192,128]{2,1,0:T(8,128)S(1)}, f32[5,192,128]{2,1,0:T(8,128)S(1)}, u32[]{:S(2)}, u32[]{:S(2)}) collective-permute-start(f32[5,192,128]{2,1,0:T(8,128)S(1)} %bitcast.120), channel_id=1, source_target_pairs={{0,2},{1,3},{2,0},{3,1},{4,6},{5,7},{6,4},{7,5},{8,10},{9,11},{10,... | collective-permute-start | bytes 1474568 | tf_op jit(solution)/shard_map/ppermute | solution.py:28
  129.6 21.2 %collective-permute-start.38 = (f32[5,192,128]{2,1,0:T(8,128)S(1)}, f32[5,192,128]{2,1,0:T(8,128)S(1)}, u32[]{:S(2)}, u32[]{:S(2)}) collective-permute-start(f32[5,192,128]{2,1,0:T(8,128)S(1)} %bitcast.119), channel_id=1, source_target_pairs={{0,4},{1,5},{2,6},{3,7},{4,0},{5,1},{6,2},{7,3},{8,12},{9,13},{10,... | collective-permute-start | bytes 1474568 | tf_op jit(solution)/shard_map/ppermute | solution.py:28
  130.2 4.8 %collective-permute-start.39 = (f32[8,128]{1,0:T(8,128)S(1)}, f32[8,128]{1,0:T(8,128)S(1)}, u32[]{:S(2)}, u32[]{:S(2)}) collective-permute-start(f32[8,128]{1,0:T(8,128)S(1)} %add_select_fusion), channel_id=1, source_target_pairs={{0,16},{1,17},{2,18},{3,19},{4,20},{5,21},{6,22},{7,23},{8,24},{9,... | collective-permute-start | bytes 12296 | tf_op jit(solution)/shard_map/ppermute | solution.py:44
  130.2 4.8 %collective-permute-start.40 = (f32[8,128]{1,0:T(8,128)S(1)}, f32[8,128]{1,0:T(8,128)S(1)}, u32[]{:S(2)}, u32[]{:S(2)}) collective-permute-start(f32[8,128]{1,0:T(8,128)S(1)} %add_select_fusion), channel_id=1, source_target_pairs={{0,48},{1,49},{2,50},{3,51},{4,52},{5,53},{6,54},{7,55},{8,56},{9,... | collective-permute-start | bytes 12296 | tf_op jit(solution)/shard_map/ppermute | solution.py:44
  133.4 5.1 %collective-permute-start.41 = (f32[8,128]{1,0:T(8,128)S(1)}, f32[8,128]{1,0:T(8,128)S(1)}, u32[]{:S(2)}, u32[]{:S(2)}) collective-permute-start(f32[8,128]{1,0:T(8,128)S(1)} %add_select_fusion), channel_id=1, source_target_pairs={{0,32},{1,33},{2,34},{3,35},{4,36},{5,37},{6,38},{7,39},{8,40},{9,... | collective-permute-start | bytes 12296 | tf_op jit(solution)/shard_map/ppermute | solution.py:44
  138.5 7.1 %collective-permute-start.42 = (f32[8,128]{1,0:T(8,128)S(1)}, f32[8,128]{1,0:T(8,128)S(1)}, u32[]{:S(2)}, u32[]{:S(2)}) collective-permute-start(f32[8,128]{1,0:T(8,128)S(1)} %add_add_fusion.1), channel_id=1, source_target_pairs={{0,68},{1,69},{2,70},{3,71},{4,64},{5,65},{6,66},{7,67},{8,76},{9,... | collective-permute-start | bytes 12296 | tf_op jit(solution)/shard_map/ppermute | solution.py:44
  140.6 6.0 %collective-permute-start.43 = (f32[8,128]{1,0:T(8,128)S(1)}, f32[8,128]{1,0:T(8,128)S(1)}, u32[]{:S(2)}, u32[]{:S(2)}) collective-permute-start(f32[8,128]{1,0:T(8,128)S(1)} %add_add_fusion.1), channel_id=1, source_target_pairs={{0,6},{1,7},{2,4},{3,5},{4,2},{5,3},{6,0},{7,1},{8,14},{9,15},{10,... | collective-permute-start | bytes 12296 | tf_op jit(solution)/shard_map/ppermute | solution.py:44
  142.4 7.5 %collective-permute-start.44 = (f32[8,128]{1,0:T(8,128)S(1)}, f32[8,128]{1,0:T(8,128)S(1)}, u32[]{:S(2)}, u32[]{:S(2)}) collective-permute-start(f32[8,128]{1,0:T(8,128)S(1)} %add_add_fusion.1), channel_id=1, source_target_pairs={{0,66},{1,67},{2,64},{3,65},{4,70},{5,71},{6,68},{7,69},{8,74},{9,... | collective-permute-start | bytes 12296 | tf_op jit(solution)/shard_map/ppermute | solution.py:44
  150.0 0.8 copy-start.14
  150.8 0.9 slice-start
  151.8 10.6 %copy-start.15 = (f32[5,192,128]{2,1,0:T(8,128)S(1)}, f32[5,192,128]{2,1,0:T(8,128)}, u32[]{:S(2)}) copy-start(f32[5,192,128]{2,1,0:T(8,128)} %copy-done.14) | copy-start | bytes 1474564
  151.8 6.7 %collective-permute-start.45 = (f32[5,104,128]{2,1,0:T(8,128)S(1)}, f32[5,104,128]{2,1,0:T(8,128)S(1)}, u32[]{:S(2)}, u32[]{:S(2)}) collective-permute-start(f32[5,104,128]{2,1,0:T(8,128)S(1)} %get-tuple-element.94), channel_id=1, source_target_pairs={{0,3},{1,0},{2,1},{3,2},{4,7},{5,4},{6,5},{7,6},{8,11},{9,8},{10,9... | collective-permute-start | bytes 798728 | tf_op jit(solution)/shard_map/ppermute | solution.py:28
  154.6 7.6 %collective-permute-start.46 = (f32[5,104,128]{2,1,0:T(8,128)S(1)}, f32[5,104,128]{2,1,0:T(8,128)S(1)}, u32[]{:S(2)}, u32[]{:S(2)}) collective-permute-start(f32[5,104,128]{2,1,0:T(8,128)S(1)} %get-tuple-element.95), channel_id=1, source_target_pairs={{0,1},{1,2},{2,3},{3,0},{4,5},{5,6},{6,7},{7,4},{8,9},{9,10},{10,1... | collective-permute-start | bytes 798728 | tf_op jit(solution)/shard_map/ppermute | solution.py:28
  154.6 7.6 %collective-permute-start.47 = (f32[5,104,128]{2,1,0:T(8,128)S(1)}, f32[5,104,128]{2,1,0:T(8,128)S(1)}, u32[]{:S(2)}, u32[]{:S(2)}) collective-permute-start(f32[5,104,128]{2,1,0:T(8,128)S(1)} %get-tuple-element.96), channel_id=1, source_target_pairs={{0,4},{1,5},{2,6},{3,7},{4,0},{5,1},{6,2},{7,3},{8,12},{9,13},{10,... | collective-permute-start | bytes 798728 | tf_op jit(solution)/shard_map/ppermute | solution.py:28
  162.3 1.2 collective-permute-start.48
  (4 other events, 2.9 us)
